TPU v7x, 256 devices: a whole 4x4x8 slice. The times are simulated.
256 devices in a mesh: ctx: 32 (over z, x_lo, core), head: 8 (over x_hi, y).
Axes of the slice: x: 4 (x_hi: 2, x_lo: 2; x = x_hi * 2 + x_lo), y: 4, z: 8, core: 2. Of those that a mesh axis runs over, the one named last changes fastest.
Arguments:
- queries: bfloat16 [16384, 2048], P('ctx', 'head'), may hold values from -24 to 24
- keys: bfloat16 [16384, 1024], P('ctx', 'head'), may hold values from -6 to 6
- values: bfloat16 [16384, 1024], P('ctx', 'head'), may hold values from -6 to 6
- out_weight: bfloat16 [128, 16, 4608], P(None, 'head'), may hold values from -0.125 to 0.125
- cotangent: bfloat16 [16384, 4608], P(('ctx', 'head')), may hold values from -3 to 3
Outputs:
- query_grad: float32 [16384, 2048], P('ctx', 'head')
- key_grad: float32 [16384, 1024], P('ctx', 'head')
- value_grad: float32 [16384, 1024], P('ctx', 'head')
- weight_grad: float32 [128, 16, 4608], P('ctx', 'head')
All inputs are finite; a program needn't handle non-finite values.
Results may differ from a plain program's by a relative error of at most 0.02.
Values may be sent and summed in bfloat16 or wider, within the bound.
No kernel may reach another device: no remote copies, remote signals or barrier semaphores. Data moves between devices by JAX's collectives and lax.ppermute only.
A program may use at most 128 MiB of HBM per device.

v0:
```python
import jax
import jax.numpy as jnp
from jax import lax
from jax.sharding import PartitionSpec as P

WINDOW = 4096
SPAN = 8


SOFT_CAP = 50.0
QUERY_MULTIPLIER = 144.0 ** (-0.5)
ROPE_BASE = 10000.0


def passed_along(block, axis, distance):
    devices = range(lax.axis_size(axis))
    route = [(i - distance, i) for i in devices if i - distance in devices]
    return lax.ppermute(block, axis, route)


def rotary_tables(positions, width):
    half_width = width // 2
    frequency = ROPE_BASE ** (-(jnp.arange(half_width, dtype=jnp.float32) * 2.0) / width)
    angles = positions.astype(jnp.float32)[:, None] * frequency[None, :]
    return (jnp.cos(angles)[:, None, :], jnp.sin(angles)[:, None, :])


def rotate(values_in, cosine, sine_table):
    half_width = values_in.shape[-1] // 2
    first_half = values_in[..., :half_width]
    second_half = values_in[..., half_width:]
    return jnp.concatenate(
        [
            first_half * cosine - second_half * sine_table,
            second_half * cosine + first_half * sine_table,
        ],
        axis=-1,
    )


def unrotate(values_in, cosine, sine_table):
    half_width = values_in.shape[-1] // 2
    first_half = values_in[..., :half_width]
    second_half = values_in[..., half_width:]
    return jnp.concatenate(
        [
            first_half * cosine + second_half * sine_table,
            second_half * cosine - first_half * sine_table,
        ],
        axis=-1,
    )


def weight_reduce(attn_out, full_grad, query_heads, head_dim):
    attn_flat = attn_out.reshape(attn_out.shape[0], query_heads, head_dim)
    full_term = jnp.einsum("the,td->ehd", attn_flat, full_grad, preferred_element_type=jnp.float32)
    return lax.psum_scatter(full_term, "ctx", scatter_dimension=0, tiled=True)


def local(queries, keys, values, out_weight, cotangent):
    tok_rows = queries.shape[0]
    head_dim = out_weight.shape[0]
    query_heads = queries.shape[1] // head_dim
    kv_heads = keys.shape[1] // head_dim
    group_size = query_heads // kv_heads
    first_row = lax.axis_index("ctx") * tok_rows
    positions = first_row + jnp.arange(tok_rows, dtype=jnp.int32)
    cosine, sine_table = rotary_tables(positions, head_dim)
    query_rotated = (
        rotate(
            queries.reshape(tok_rows, query_heads, head_dim).astype(jnp.float32), cosine, sine_table
        )
        .astype(jnp.bfloat16)
        .reshape(tok_rows, kv_heads, group_size, head_dim)
    )
    key_rot = rotate(
        keys.reshape(tok_rows, kv_heads, head_dim).astype(jnp.float32), cosine, sine_table
    ).astype(jnp.bfloat16)
    value_own = values.reshape(tok_rows, kv_heads, head_dim)
    full_grad = lax.all_gather(cotangent, "head", axis=0, tiled=True)
    output_gradient = (
        jnp.einsum("td,ehd->the", full_grad, out_weight, preferred_element_type=jnp.float32)
        .astype(jnp.bfloat16)
        .reshape(tok_rows, kv_heads, group_size, head_dim)
    )
    own_pair = jnp.stack([key_rot, value_own])
    fetched = []
    for distance in range(1, SPAN + 1):
        fetched.append(passed_along(own_pair, "ctx", distance))
    key_tiles = jnp.stack(fetched[::-1] + [own_pair])
    key_first = first_row - SPAN * tok_rows
    tile_ids = jnp.arange(SPAN + 1, dtype=jnp.int32)

    def tile_setup(tile_index, key_panel):
        key_pos = key_first + tile_index * tok_rows + jnp.arange(tok_rows, dtype=jnp.int32)
        offset = positions[:, None] - key_pos[None, :]
        visible = (offset >= 0) & (offset < WINDOW) & (key_pos[None, :] >= 0)
        uncapped_score = (
            jnp.einsum(
                "qfwy,vfy->fwqv", query_rotated, key_panel[0], preferred_element_type=jnp.float32
            )
            * QUERY_MULTIPLIER
        )
        return (visible, jnp.tanh(uncapped_score / SOFT_CAP))

    def forward_tile(state, inputs):
        row_total, weighted_values = state
        tile_index, key_panel = inputs
        visible, tanh_val = tile_setup(tile_index, key_panel)
        exponent_score = jnp.where(visible, jnp.exp(SOFT_CAP * tanh_val), 0.0)
        row_total = row_total + jnp.sum(exponent_score, axis=-1)
        weighted_values = weighted_values + jnp.einsum(
            "fpxe,efv->xfpv",
            exponent_score.astype(jnp.bfloat16),
            key_panel[1],
            preferred_element_type=jnp.float32,
        )
        return ((row_total, weighted_values), None)

    start_state = (
        jnp.zeros((kv_heads, group_size, tok_rows), jnp.float32),
        jnp.zeros((tok_rows, kv_heads, group_size, head_dim), jnp.float32),
    )
    (row_total, weighted_values), unused = lax.scan(
        forward_tile, start_state, (tile_ids, key_tiles)
    )
    attn_out = (weighted_values / jnp.transpose(row_total, (2, 0, 1))[..., None]).astype(
        jnp.bfloat16
    )
    log_total = jnp.log(row_total)
    row_delta = jnp.transpose(
        jnp.sum(output_gradient.astype(jnp.float32) * attn_out.astype(jnp.float32), axis=-1),
        (1, 2, 0),
    )

    def backward_tile(query_acc, inputs):
        tile_index, key_panel = inputs
        visible, tanh_val = tile_setup(tile_index, key_panel)
        softmax_probability = jnp.where(
            visible, jnp.exp(SOFT_CAP * tanh_val - log_total[..., None]), 0.0
        )
        probability_gradient = jnp.einsum(
            "qfwy,vfy->fwqv", output_gradient, key_panel[1], preferred_element_type=jnp.float32
        )
        score_gradient = (
            softmax_probability
            * (probability_gradient - row_delta[..., None])
            * (1.0 - tanh_val * tanh_val)
            * QUERY_MULTIPLIER
        ).astype(jnp.bfloat16)
        query_acc = query_acc + jnp.einsum(
            "fpxe,efv->xfpv", score_gradient, key_panel[0], preferred_element_type=jnp.float32
        )
        key_portion = jnp.einsum(
            "vcfh,fvcx->hvx", score_gradient, query_rotated, preferred_element_type=jnp.float32
        )
        value_portion = jnp.einsum(
            "vcfh,fvcx->hvx",
            softmax_probability.astype(jnp.bfloat16),
            output_gradient,
            preferred_element_type=jnp.float32,
        )
        return (query_acc, jnp.stack([key_portion, value_portion]))

    query_acc, contrib = lax.scan(
        backward_tile,
        jnp.zeros((tok_rows, kv_heads, group_size, head_dim), jnp.float32),
        (tile_ids, key_tiles),
    )
    pair_grad = contrib[SPAN]
    for distance in range(1, SPAN + 1):
        pair_grad = pair_grad + passed_along(contrib[SPAN - distance], "ctx", -distance)
    query_grad = unrotate(
        query_acc.reshape(tok_rows, query_heads, head_dim), cosine, sine_table
    ).reshape(tok_rows, query_heads * head_dim)
    key_grad = unrotate(pair_grad[0], cosine, sine_table).reshape(tok_rows, kv_heads * head_dim)
    value_grad = pair_grad[1].reshape(tok_rows, kv_heads * head_dim)
    weight_grad = weight_reduce(attn_out, full_grad, query_heads, head_dim)
    return (query_grad, key_grad, value_grad, weight_grad)


def solution(mesh):
    placed = (
        P("ctx", "head"),
        P("ctx", "head"),
        P("ctx", "head"),
        P(None, "head", None),
        P(("ctx", "head"), None),
    )
    return jax.shard_map(
        local,
        mesh=mesh,
        in_specs=placed,
        out_specs=(P("ctx", "head"), P("ctx", "head"), P("ctx", "head"), P("ctx", "head", None)),
        check_vma=False,
    )
```

profile of v0, /device:TPU:107, one launch (start us, length us, event | category | flops | bytes accessed | tf_op | source)
XLA Modules:
  0.0 417.9 jit_solution(16782943966289065811)
XLA Ops:
  10.4 5.3 %collective-permute-start.7 = (bf16[2,512,1,128]{3,1,0,2:T(8,128)(2,1)S(1)}, bf16[2,512,1,128]{3,1,0,2:T(8,128)(2,1)S(1)}, u32[]{:S(2)}, u32[]{:S(2)}) collective-permute-start(bf16[2,512,1,128]{3,1,0,2:T(8,128)(2,1)S(1)} %fusion.81), channel_id=1, source_target_pairs={{0,8},{8,16},{16,24},{24,32},{32,40},{40,48},{48,56},{56,64},{64,7... | collective-permute-start | bytes 786440 | tf_op jit(solution)/shard_map/ppermute | solution.py:18
  15.7 3.1 collective-permute-start.6
  20.8 4.1 collective-permute-start.1
  24.9 1.9 collective-permute-start
  27.9 29.3 %collective-permute-done = bf16[2,512,1,128]{3,1,0,2:T(8,128)(2,1)} collective-permute-done((bf16[2,512,1,128]{3,1,0,2:T(8,128)(2,1)S(1)}, bf16[2,512,1,128]{3,1,0,2:T(8,128)(2,1)}, u32[]{:S(2)}, u32[]{:S(2)}) %collective-permute-start) | collective-permute-done | bytes 262176 | tf_op jit(solution)/shard_map/ppermute | solution.py:18
  62.1 5.4 %collective-permute-done.2 = bf16[2,512,1,128]{3,1,0,2:T(8,128)(2,1)S(1)} collective-permute-done((bf16[2,512,1,128]{3,1,0,2:T(8,128)(2,1)S(1)}, bf16[2,512,1,128]{3,1,0,2:T(8,128)(2,1)S(1)}, u32[]{:S(2)}, u32[]{:S(2)}) %collective-permute-start.2) | collective-permute-done | bytes 262176 | tf_op jit(solution)/shard_map/ppermute | solution.py:18
  69.5 3.2 collective-permute-done.3
  72.7 6.8 %collective-permute-done.4 = bf16[2,512,1,128]{3,1,0,2:T(8,128)(2,1)S(1)} collective-permute-done((bf16[2,512,1,128]{3,1,0,2:T(8,128)(2,1)S(1)}, bf16[2,512,1,128]{3,1,0,2:T(8,128)(2,1)S(1)}, u32[]{:S(2)}, u32[]{:S(2)}) %collective-permute-start.4) | collective-permute-done | bytes 262176 | tf_op jit(solution)/shard_map/ppermute | solution.py:18
  81.2 42.5 %while.30 = (s32[]{:T(128)}, f32[1,2,512]{2,1,0:T(2,128)S(1)}, f32[512,1,2,128]{0,3,2,1:T(8,128)S(1)}, s32[9]{0:T(128)S(1)}, s32[]{:T(128)}, /*index=5*/bf16[9,2...) while((s32[]{:T(128)}, f32[1,2,512]{2,1,0:T(2,128)S(1)}, ...), condition=%wide.region_2.3_spmd.clone, body=%wide.region_0.2_spmd.clone.sunk | while | flops 272632832 | bytes 4220112 | solution.py:124
  123.8 5.9 %convolution_bitcast_fusion.4 = f32[128,2,4608]{2,0,1:T(8,128)} fusion(bf16[512,4608]{1,0:T(8,128)(2,1)} %all-gather.2.cloned.1.call-done, f32[512,1,2,128]{0,3,2,1:T(8,128)S(1)} %get-tuple-element.245, f32[512,2]{0,1:T(2,128)S(1)} %bitcast.305), kind=kOutput, calls=%fused_computation.63 | convolution fusion | flops 1208221696 | bytes 9965568 | tf_op jit(solution)/shard_map/the,td->ehd/dot_general | solution.py:56
  129.7 4.5 %multiply_reduce_fusion = (f32[512,2]{0,1:T(2,128)S(1)}, bf16[512,1,2,128]{0,3,2,1:T(8,128)(2,1)S(1)}) fusion(f32[512,1,2,128]{0,3,2,1:T(8,128)S(1)} %get-tuple-element.245, f32[512,2]{0,1:T(2,128)S(1)} %bitcast.306, bf16[512,4608]{1,0:T(8,128)(2,1)} %all-gather.2.cloned.1.call-done, bf16[128,2,4608]{2,1,0:T(2,128)(2,1)} %param.12), kind=kOutput, calls=%fused_computation.87 | convolution fusion | flops 1208876032 | bytes 7872512 | tf_op jit(solution)/shard_map/td,ehd->the/dot_general | solution.py:82
  134.4 75.6 %while.31 = (s32[]{:T(128)}, f32[512,1,2,128]{0,3,2,1:T(8,128)S(1)}, f32[9,2,512,1,128]{4,2,1,3,0:T(8,128)}, bf16[9,2,512,1,128]{4,2,3,1,0:T(8,128)(2,1)}, s32[9...) while((s32[]{:T(128)}, ...), condition=%wide.region_5.6_spmd.clone, body=%wide.region_4.5_spmd.clone.sunk | while | flops 681183232 | bytes 14308591 | solution.py:165
  138.1 2.1 fusion.114
  146.5 2.1 fusion.114
  154.9 2.1 fusion.114
  163.3 2.1 fusion.114
  171.6 2.1 fusion.114
  180.1 2.1 fusion.114
  188.5 2.1 fusion.114
  196.9 2.1 fusion.114
  205.3 2.1 fusion.114
  210.0 3.5 slice_bitcast_fusion.7
  213.5 2.6 collective-permute-start.8
  220.0 1.9 collective-permute-start.11
  221.9 2.8 collective-permute-start.10
  224.7 11.9 %collective-permute-done.8 = f32[2,512,1,128]{3,1,2,0:T(8,128)S(1)} collective-permute-done((f32[2,512,1,128]{3,1,2,0:T(8,128)S(1)}, f32[2,512,1,128]{3,1,2,0:T(8,128)S(1)}, u32[]{:S(2)}, u32[]{:S(2)}) %collective-permute-start.8) | collective-permute-done | bytes 524320 | tf_op jit(solution)/shard_map/ppermute | solution.py:18
  236.6 15.9 %collective-permute-start.9 = (f32[2,512,1,128]{3,1,2,0:T(8,128)}, f32[2,512,1,128]{3,1,2,0:T(8,128)}, u32[]{:S(2)}, u32[]{:S(2)}) collective-permute-start(f32[2,512,1,128]{3,1,2,0:T(8,128)} %get-tuple-element.412), channel_id=1, source_target_pairs={{16,0},{24,8},{32,16},{40,24},{48,32},{56,40},{64,48},{72,56},{80,... | collective-permute-start | bytes 1572872 | tf_op jit(solution)/shard_map/ppermute | solution.py:18
  252.6 1.9 collective-permute-start.15
  254.5 23.1 %collective-permute-done.12 = f32[2,512,1,128]{3,1,2,0:T(8,128)S(1)} collective-permute-done((f32[2,512,1,128]{3,1,2,0:T(8,128)S(1)}, f32[2,512,1,128]{3,1,2,0:T(8,128)S(1)}, u32[]{:S(2)}, u32[]{:S(2)}) %collective-permute-start.12) | collective-permute-done | bytes 524320 | tf_op jit(solution)/shard_map/ppermute | solution.py:18
  281.9 26.7 %collective-permute-done.9 = f32[2,512,1,128]{3,1,2,0:T(8,128)} collective-permute-done((f32[2,512,1,128]{3,1,2,0:T(8,128)}, f32[2,512,1,128]{3,1,2,0:T(8,128)}, u32[]{:S(2)}, u32[]{:S(2)}) %collective-permute-start.9) | collective-permute-done | bytes 524320 | tf_op jit(solution)/shard_map/ppermute | solution.py:18
  308.6 2.1 fusion.61
  313.5 95.9 %all-reduce.3.cloned.1.call-done = f32[128,2,4608]{2,0,1:T(8,128)} async-done(((f32[128,2,4608]{2,0,1:T(8,128)}), f32[128,2,4608]{2,0,1:T(8,128)}) %all-reduce.3.cloned.1.call-update) | async-done | bytes 4718608
  (209 shorter events, 113.3 us)
Async XLA Ops:
  7.2 20.3 %copy-start.2 = (bf16[512,256]{1,0:T(8,128)(2,1)S(1)}, bf16[512,256]{1,0:T(8,128)(2,1)}, u32[]{:S(2)}) copy-start(bf16[512,256]{1,0:T(8,128)(2,1)} %param.9) | copy-start | bytes 786436
  7.2 116.6 %all-gather.2.cloned.1.call-start = ((), (), s32[]{:S(2)}) async-start(), calls=%async_computation | async-start | bytes 5308416 | tf_op jit(solution)/shard_map/all_gather | solution.py:80
  10.4 69.2 %collective-permute-start.7 = (bf16[2,512,1,128]{3,1,0,2:T(8,128)(2,1)S(1)}, bf16[2,512,1,128]{3,1,0,2:T(8,128)(2,1)S(1)}, u32[]{:S(2)}, u32[]{:S(2)}) collective-permute-start(bf16[2,512,1,128]{3,1,0,2:T(8,128)(2,1)S(1)} %fusion.81), channel_id=1, source_target_pairs={{0,8},{8,16},{16,24},{24,32},{32,40},{40,48},{48,56},{56,64},{64,7... | collective-permute-start | bytes 786440 | tf_op jit(solution)/shard_map/ppermute | solution.py:18
  15.7 63.8 %collective-permute-start.6 = (bf16[2,512,1,128]{3,1,0,2:T(8,128)(2,1)S(1)}, bf16[2,512,1,128]{3,1,0,2:T(8,128)(2,1)S(1)}, u32[]{:S(2)}, u32[]{:S(2)}) collective-permute-start(bf16[2,512,1,128]{3,1,0,2:T(8,128)(2,1)S(1)} %fusion.81), channel_id=1, source_target_pairs={{0,16},{8,24},{16,32},{24,40},{32,48},{40,56},{48,64},{56,72},{64,... | collective-permute-start | bytes 786440 | tf_op jit(solution)/shard_map/ppermute | solution.py:18
  18.9 60.7 %collective-permute-start.5 = (bf16[2,512,1,128]{3,1,0,2:T(8,128)(2,1)S(1)}, bf16[2,512,1,128]{3,1,0,2:T(8,128)(2,1)S(1)}, u32[]{:S(2)}, u32[]{:S(2)}) collective-permute-start(bf16[2,512,1,128]{3,1,0,2:T(8,128)(2,1)S(1)} %fusion.81), channel_id=1, source_target_pairs={{0,24},{8,32},{16,40},{24,48},{32,56},{40,64},{48,72},{56,80},{64,... | collective-permute-start | bytes 786440 | tf_op jit(solution)/shard_map/ppermute | solution.py:18
  20.8 39.4 %collective-permute-start.1 = (bf16[2,512,1,128]{3,1,0,2:T(8,128)(2,1)S(1)}, bf16[2,512,1,128]{3,1,0,2:T(8,128)(2,1)S(1)}, u32[]{:S(2)}, u32[]{:S(2)}) collective-permute-start(bf16[2,512,1,128]{3,1,0,2:T(8,128)(2,1)S(1)} %fusion.81), channel_id=1, source_target_pairs={{0,56},{8,64},{16,72},{24,80},{32,88},{40,96},{48,104},{56,112},{6... | collective-permute-start | bytes 786440 | tf_op jit(solution)/shard_map/ppermute | solution.py:18
  24.9 32.4 %collective-permute-start = (bf16[2,512,1,128]{3,1,0,2:T(8,128)(2,1)S(1)}, bf16[2,512,1,128]{3,1,0,2:T(8,128)(2,1)}, u32[]{:S(2)}, u32[]{:S(2)}) collective-permute-start(bf16[2,512,1,128]{3,1,0,2:T(8,128)(2,1)S(1)} %fusion.81), channel_id=1, source_target_pairs={{0,64},{8,72},{16,80},{24,88},{32,96},{40,104},{48,112},{56,120},{... | collective-permute-start | bytes 786440 | tf_op jit(solution)/shard_map/ppermute | solution.py:18
  26.8 382.5 %all-reduce.3.cloned.1.call-start = ((), (), s32[]{:S(2)}) async-start(), calls=%async_computation.1 | async-start | bytes 9437184
  27.7 52.0 %copy-start.1 = (bf16[512,128]{1,0:T(8,128)(2,1)S(1)}, bf16[512,128]{1,0:T(8,128)(2,1)}, u32[]{:S(2)}) copy-start(bf16[512,128]{1,0:T(8,128)(2,1)} %param.11) | copy-start | bytes 393220
  57.2 10.3 %collective-permute-start.2 = (bf16[2,512,1,128]{3,1,0,2:T(8,128)(2,1)S(1)}, bf16[2,512,1,128]{3,1,0,2:T(8,128)(2,1)S(1)}, u32[]{:S(2)}, u32[]{:S(2)}) collective-permute-start(bf16[2,512,1,128]{3,1,0,2:T(8,128)(2,1)S(1)} %fusion.81), channel_id=1, source_target_pairs={{0,48},{8,56},{16,64},{24,72},{32,80},{40,88},{48,96},{56,104},{64... | collective-permute-start | bytes 786440 | tf_op jit(solution)/shard_map/ppermute | solution.py:18
  60.1 12.5 %collective-permute-start.3 = (bf16[2,512,1,128]{3,1,0,2:T(8,128)(2,1)S(1)}, bf16[2,512,1,128]{3,1,0,2:T(8,128)(2,1)S(1)}, u32[]{:S(2)}, u32[]{:S(2)}) collective-permute-start(bf16[2,512,1,128]{3,1,0,2:T(8,128)(2,1)S(1)} %fusion.81), channel_id=1, source_target_pairs={{0,40},{8,48},{16,56},{24,64},{32,72},{40,80},{48,88},{56,96},{64,... | collective-permute-start | bytes 786440 | tf_op jit(solution)/shard_map/ppermute | solution.py:18
  67.5 12.0 %collective-permute-start.4 = (bf16[2,512,1,128]{3,1,0,2:T(8,128)(2,1)S(1)}, bf16[2,512,1,128]{3,1,0,2:T(8,128)(2,1)S(1)}, u32[]{:S(2)}, u32[]{:S(2)}) collective-permute-start(bf16[2,512,1,128]{3,1,0,2:T(8,128)(2,1)S(1)} %fusion.81), channel_id=1, source_target_pairs={{0,32},{8,40},{16,48},{24,56},{32,64},{40,72},{48,80},{56,88},{64,... | collective-permute-start | bytes 786440 | tf_op jit(solution)/shard_map/ppermute | solution.py:18
  79.8 1.4 copy-start
  210.0 69.6 %copy-start.3 = (u32[256]{0:T(256)S(1)}, u32[256]{0:T(256)}, u32[]{:S(2)}) copy-start(u32[256]{0:T(256)} %constant.132) | copy-start | bytes 3076
  213.5 23.1 %collective-permute-start.8 = (f32[2,512,1,128]{3,1,2,0:T(8,128)S(1)}, f32[2,512,1,128]{3,1,2,0:T(8,128)S(1)}, u32[]{:S(2)}, u32[]{:S(2)}) collective-permute-start(f32[2,512,1,128]{3,1,2,0:T(8,128)S(1)} %get-tuple-element.407), channel_id=1, source_target_pairs={{8,0},{16,8},{24,16},{32,24},{40,32},{48,40},{56,48},{64,56},{72,6... | collective-permute-start | bytes 1572872 | tf_op jit(solution)/shard_map/ppermute | solution.py:18
  216.1 36.4 %collective-permute-start.13 = (f32[2,512,1,128]{3,1,2,0:T(8,128)S(1)}, f32[2,512,1,128]{3,1,2,0:T(8,128)S(1)}, u32[]{:S(2)}, u32[]{:S(2)}) collective-permute-start(f32[2,512,1,128]{3,1,2,0:T(8,128)S(1)} %get-tuple-element.408), channel_id=1, source_target_pairs={{48,0},{56,8},{64,16},{72,24},{80,32},{88,40},{96,48},{104,56},{11... | collective-permute-start | bytes 1572872 | tf_op jit(solution)/shard_map/ppermute | solution.py:18
  218.1 59.6 %collective-permute-start.12 = (f32[2,512,1,128]{3,1,2,0:T(8,128)S(1)}, f32[2,512,1,128]{3,1,2,0:T(8,128)S(1)}, u32[]{:S(2)}, u32[]{:S(2)}) collective-permute-start(f32[2,512,1,128]{3,1,2,0:T(8,128)S(1)} %get-tuple-element.409), channel_id=1, source_target_pairs={{40,0},{48,8},{56,16},{64,24},{72,32},{80,40},{88,48},{96,56},{104... | collective-permute-start | bytes 1572872 | tf_op jit(solution)/shard_map/ppermute | solution.py:18
  220.0 61.9 %collective-permute-start.11 = (f32[2,512,1,128]{3,1,2,0:T(8,128)}, f32[2,512,1,128]{3,1,2,0:T(8,128)}, u32[]{:S(2)}, u32[]{:S(2)}) collective-permute-start(f32[2,512,1,128]{3,1,2,0:T(8,128)} %get-tuple-element.410), channel_id=1, source_target_pairs={{32,0},{40,8},{48,16},{56,24},{64,32},{72,40},{80,48},{88,56},{96,... | collective-permute-start | bytes 1572872 | tf_op jit(solution)/shard_map/ppermute | solution.py:18
  221.9 60.0 %collective-permute-start.10 = (f32[2,512,1,128]{3,1,2,0:T(8,128)}, f32[2,512,1,128]{3,1,2,0:T(8,128)}, u32[]{:S(2)}, u32[]{:S(2)}) collective-permute-start(f32[2,512,1,128]{3,1,2,0:T(8,128)} %get-tuple-element.411), channel_id=1, source_target_pairs={{24,0},{32,8},{40,16},{48,24},{56,32},{64,40},{72,48},{80,56},{88,... | collective-permute-start | bytes 1572872 | tf_op jit(solution)/shard_map/ppermute | solution.py:18
  236.6 72.0 %collective-permute-start.9 = (f32[2,512,1,128]{3,1,2,0:T(8,128)}, f32[2,512,1,128]{3,1,2,0:T(8,128)}, u32[]{:S(2)}, u32[]{:S(2)}) collective-permute-start(f32[2,512,1,128]{3,1,2,0:T(8,128)} %get-tuple-element.412), channel_id=1, source_target_pairs={{16,0},{24,8},{32,16},{40,24},{48,32},{56,40},{64,48},{72,56},{80,... | collective-permute-start | bytes 1572872 | tf_op jit(solution)/shard_map/ppermute | solution.py:18
  252.6 56.1 %collective-permute-start.15 = (f32[2,512,1,128]{3,1,2,0:T(8,128)S(1)}, f32[2,512,1,128]{3,1,2,0:T(8,128)}, u32[]{:S(2)}, u32[]{:S(2)}) collective-permute-start(f32[2,512,1,128]{3,1,2,0:T(8,128)S(1)} %get-tuple-element.413), channel_id=1, source_target_pairs={{64,0},{72,8},{80,16},{88,24},{96,32},{104,40},{112,48},{120,56},{... | collective-permute-start | bytes 1572872 | tf_op jit(solution)/shard_map/ppermute | solution.py:18
  277.6 31.0 %collective-permute-start.14 = (f32[2,512,1,128]{3,1,2,0:T(8,128)S(1)}, f32[2,512,1,128]{3,1,2,0:T(8,128)}, u32[]{:S(2)}, u32[]{:S(2)}) collective-permute-start(f32[2,512,1,128]{3,1,2,0:T(8,128)S(1)} %get-tuple-element.414), channel_id=1, source_target_pairs={{56,0},{64,8},{72,16},{80,24},{88,32},{96,40},{104,48},{112,56},{1... | collective-permute-start | bytes 1572872 | tf_op jit(solution)/shard_map/ppermute | solution.py:18
Sparse Core Ops, SparseCore 0:
  26.9 81.0 all-gather.1
  129.8 279.4 all-reduce.2
where the time goes:
time: 420 us; the launch traced here: 418 us
  waiting for transfers between devices  202 us (48%)
  matrix products  90.9 us (22%)
  starting transfers between devices  53.1 us (13%)
  other arithmetic  22.4 us (5%)
  local copies, waits for them, and re-layouts  21.5 us (5%)
  between operations  15.1 us (4%)
  loops' own time  12.5 us (3%)
    ppermute x16, waiting for transfers between devices, passed_along(): return lax.ppermute(block, axis, route)  106 us
    unnamed x3, waiting for transfers between devices  95.9 us
    ppermute x16, starting transfers between devices, passed_along(): return lax.ppermute(block, axis, route)  53 us
    dot_general x18, matrix products, tile_setup(): jnp.einsum('qfwy,vfy->fwqv', query_rotated, key_panel[0], preferred_eleme...  28.1 us
    dot_general x9, matrix products, backward_tile(): jnp.einsum('qfwy,vfy->fwqv', output_gradient, key_panel[1], preferred_ele...  19.1 us
    dot_general x9, matrix products, forward_tile(): jnp.einsum('fpxe,efv->xfpv', exponent_score.astype(jnp.bfloat16), key_pan...  11.5 us
    dot_general x9, matrix products, backward_tile(): jnp.einsum('fpxe,efv->xfpv', score_gradient, key_panel[0], preferred_elem...  11.5 us
    dynamic_slice x18, local copies, waits for them, and re-layouts, local(): lax.scan(forward_tile, start_state, (tile_ids, key_tiles))  10.8 us
  transfers between devices with their start and end apart: 18, of which 8 were waited for; matrix products, arithmetic and copies ran while one was open for 29% of the time, Pallas kernels for 0%

commit v1 on v0

v1 whole, which is shorter than its diff:
```python
import jax
import jax.numpy as jnp
from jax import lax
from jax.experimental import pallas as pl
from jax.experimental.pallas import tpu as pltpu
from jax.sharding import Mesh, PartitionSpec as P

SOFT_CAP = 50.0
QUERY_MULTIPLIER = 144.0 ** (-0.5)
ROPE_BASE = 10000.0
LOG2E = 1.4426950408889634
CTX = ("z", "xl", "c")
HEAD = ("xh", "y")
TOK = 512
HALF = 256
HD = 128
PANELS = 3
SLOTS = 12
TILES = 9
NT = (((1,), (1,)), ((), ()))
F32 = jnp.float32
BF16 = jnp.bfloat16


def permute(x, axis, pairs):
    return lax.ppermute(x, axis, pairs)


def from_y(x, d):
    return permute(x, "y", [((i + d) % 4, i) for i in range(4)])


def swap(x, axis):
    return permute(x, axis, [(0, 1), (1, 0)])


def along_z(x, step):
    return permute(x, "z", [(i, i + step) for i in range(8) if 0 <= i + step < 8])


def tables(first_row):
    half = HD // 2
    positions = first_row + jnp.arange(TOK, dtype=jnp.int32)
    frequency = ROPE_BASE ** (-(jnp.arange(half, dtype=F32) * 2.0) / HD)
    angles = positions.astype(F32)[:, None] * frequency[None, :]
    return jnp.cos(angles), jnp.sin(angles)


def ndot(a, b):
    return jnp.dot(a, b, preferred_element_type=F32)


def tdot(a, b):
    return lax.dot_general(a, b, NT, preferred_element_type=F32)


def forward_kernel(slot, tile, flag, q_ref, cos_ref, sin_ref, r0, r2, r1, r3, e_ref, g_ref, qr_ref, at_ref, li_ref, kv_ref, pt_ref, acc):
    step = pl.program_id(0)

    @pl.when(step == 0)
    def _():
        for n, ref in enumerate((r0, r2, r1, r3)):
            kv_ref[n * PANELS : (n + 1) * PANELS] = ref[...]
        acc[...] = jnp.zeros_like(acc)
        cosine = cos_ref[...]
        sine = sin_ref[...]
        for h in range(2):
            x = q_ref[:, h * HD : (h + 1) * HD].astype(F32)
            qr_ref[:, h * HD : (h + 1) * HD] = (x * cosine + pltpu.roll(x, HD // 2, 1) * sine).astype(BF16)

    def body(mode):
        key = kv_ref[slot[step], 0]
        value = jnp.concatenate([kv_ref[slot[step], 1], jnp.ones((TOK, HD), BF16)], axis=1)
        rows = HALF
        for h in range(2):
            for part in range(TOK // rows):
                at = pl.ds(part * rows, rows)
                s = tdot(qr_ref[at, h * HD : (h + 1) * HD], key)
                th = jnp.tanh(s * (QUERY_MULTIPLIER / SOFT_CAP))
                ex = jnp.exp2(th * (SOFT_CAP * LOG2E))
                if mode:
                    t = lax.broadcasted_iota(jnp.int32, (rows, TOK), 0) + part * rows
                    u = lax.broadcasted_iota(jnp.int32, (rows, TOK), 1)
                    ex = jnp.where(u > t if mode == 1 else u <= t, ex, 0.0)
                eb = ex.astype(BF16)
                e_ref[0, h, at, :] = eb
                g_ref[0, h, at, :] = (ex * (1.0 - th * th)).astype(BF16)
                acc[h, at, :] += ndot(eb, value)

    @pl.when(flag[step] == 1)
    def _():
        body(1)

    @pl.when(flag[step] == 2)
    def _():
        body(2)

    @pl.when(flag[step] == 3)
    def _():
        body(0)

    @pl.when(step == SLOTS - 1)
    def _():
        for h in range(2):
            inverse = 1.0 / acc[h, :, HD:]
            at_ref[:, h * HD : (h + 1) * HD] = (acc[h, :, :HD] * inverse).astype(BF16)
            li_ref[:, h * HD : (h + 1) * HD] = inverse
        row = lax.broadcasted_iota(jnp.int32, (2 * HD, 2 * HD), 0)
        col = lax.broadcasted_iota(jnp.int32, (2 * HD, 2 * HD), 1)
        core, left, plane, four, head = row // 128, (row // 64) % 2, (row // 8) % 8, (row // 2) % 4, row % 2
        source = head * HD + plane * 16 + left * 8 + core * 4 + four
        pick = jnp.where(col == source, 1.0, 0.0).astype(BF16)
        pt_ref[...] = tdot(pick, at_ref[...]).astype(BF16)


def forward(slot, tile, flag, queries, cosf, sinf, panels):
    whole = lambda *shape: pl.BlockSpec(shape, lambda i, *_: (0,) * len(shape))
    sds = jax.ShapeDtypeStruct
    eg = pl.BlockSpec((1, 2, TOK, TOK), lambda i, s, t, f: (t[i], 0, 0, 0))
    return pl.pallas_call(
        forward_kernel,
        out_shape=(
            sds((TILES, 2, TOK, TOK), BF16),
            sds((TILES, 2, TOK, TOK), BF16),
            sds((TOK, 2 * HD), BF16),
            sds((TOK, 2 * HD), BF16),
            sds((TOK, 2 * HD), F32),
            sds((SLOTS, 2, TOK, HD), BF16),
            sds((2 * HD, TOK), BF16),
        ),
        grid_spec=pltpu.PrefetchScalarGridSpec(
            num_scalar_prefetch=3,
            grid=(SLOTS,),
            in_specs=[
                whole(TOK, 2 * HD),
                whole(TOK, HD),
                whole(TOK, HD),
                *([whole(PANELS, 2, TOK, HD)] * 4),
            ],
            out_specs=(
                eg,
                eg,
                whole(TOK, 2 * HD),
                whole(TOK, 2 * HD),
                whole(TOK, 2 * HD),
                whole(SLOTS, 2, TOK, HD),
                whole(2 * HD, TOK),
            ),
            scratch_shapes=[pltpu.VMEM((2, TOK, 2 * HD), F32)],
        ),
        compiler_params=pltpu.CompilerParams(dimension_semantics=("arbitrary",), vmem_limit_bytes=60 << 20),
        cost_estimate=pl.CostEstimate(flops=10_000_000_000, bytes_accessed=24_000_000, transcendentals=10_000_000),
        name="attend",
    )(slot, tile, flag, queries, cosf, sinf, *panels)


def backward_kernel(last, *refs):
    slot, _, flag, where = refs[:4]
    c0, c1, c2, c3, w_ref, q_ref, at_ref, li_ref, cos_ref, sin_ref, kv_ref, e_ref, g_ref = refs[4:17]
    rest = refs[17:]
    if last:
        prev_ref, _, keep_ref, send_ref, qg_ref = rest[:5]
    else:
        part_ref, qg_ref = rest[:2]
    cs, do, dl, qt, dt, dq = rest[-6:]
    step = pl.program_id(0)

    @pl.when(step == 0)
    def _():
        y = where[0]
        for d, ref in enumerate((c0, c1, c2, c3)):
            row = pl.multiple_of(lax.rem(y + d, 4) * 64, 64)
            cs[pl.ds(row, 64), :] = ref[...]
        do[...] = tdot(cs[...], w_ref[...]).astype(BF16)
        for h in range(2):
            col = slice(h * HD, (h + 1) * HD)
            grad = do[:, col].astype(F32)
            inverse = li_ref[:, col]
            total = jnp.sum(grad * at_ref[:, col].astype(F32), axis=1, keepdims=True)
            dl[h] = jnp.broadcast_to(total, (HALF, HD))
            dt[h] = (grad * inverse).T.astype(BF16)
            qt[h] = (q_ref[:, col].astype(F32) * (inverse * QUERY_MULTIPLIER)).T.astype(BF16)
        dq[...] = jnp.zeros_like(dq)

    @pl.when(flag[step] > 0)
    def _():
        key = kv_ref[0, 0]
        value = kv_ref[0, 1]
        dk = jnp.zeros((HD, TOK), F32)
        dv = jnp.zeros((HD, TOK), F32)
        for h in range(2):
            dp = tdot(do[:, h * HD : (h + 1) * HD], value)
            x = (g_ref[0, h].astype(F32) * (dp - dl[h][:, :1])).astype(BF16)
            dq[h] += ndot(x, key)
            dk += ndot(qt[h], x)
            dv += ndot(dt[h], e_ref[0, h])
        if last:
            dk = (dk + prev_ref[0, 0]).astype(BF16)
            dv = (dv + prev_ref[0, 1]).astype(BF16)
            at = slot[step]

            @pl.when(at < 6)
            def _():
                keep_ref[at, 0] = dk
                keep_ref[at, 1] = dv

            @pl.when(at >= 6)
            def _():
                send_ref[at - 6, 0] = dk
                send_ref[at - 6, 1] = dv
        else:
            part_ref[0, 0] = dk
            part_ref[0, 1] = dv

    if last:

        @pl.when(flag[step] == 0)
        def _():
            at = slot[step]
            zero = jnp.zeros((2, HD, TOK), BF16)

            @pl.when(at < 6)
            def _():
                keep_ref[at] = zero

            @pl.when(at >= 6)
            def _():
                send_ref[at - 6] = zero

    @pl.when(step == SLOTS - 1)
    def _():
        cosine = cos_ref[...]
        sine = sin_ref[...]
        for h in range(2):
            col = slice(h * HD, (h + 1) * HD)
            g = dq[h] * (li_ref[:, col] * QUERY_MULTIPLIER)
            qg_ref[:, col] = g * cosine - pltpu.roll(g, HD // 2, 1) * sine


def backward(slot, tile, flag, where, cots, w2, qr, attn, linv, cosf, sinf, kv, e, g, before):
    last = before is not None
    sds = jax.ShapeDtypeStruct
    whole = lambda *shape: pl.BlockSpec(shape, lambda i, *_: (0,) * len(shape))
    tok = lambda width: pl.BlockSpec((HALF, width), lambda i, s, t, f, w: (w[1], 0))
    eg = pl.BlockSpec((1, 2, HALF, TOK), lambda i, s, t, f, w: (t[i], 0, w[1], 0))
    part = pl.BlockSpec((1, 2, HD, TOK), lambda i, s, t, f, w: (s[i], 0, 0, 0))
    ins = [whole(64, 4608)] * 4 + [
        whole(2 * HD, 4608),
        tok(2 * HD),
        tok(2 * HD),
        tok(2 * HD),
        tok(HD),
        tok(HD),
        pl.BlockSpec((1, 2, TOK, HD), lambda i, s, t, f, w: (s[i], 0, 0, 0)),
        eg,
        eg,
    ]
    args = [*cots, w2, qr, attn, linv, cosf, sinf, kv, e, g]
    alias = {}
    if last:
        ins += [part, pl.BlockSpec(memory_space=pl.ANY)]
        args += list(before)
        outs = (whole(6, 2, HD, TOK), whole(6, 2, HD, TOK), tok(2 * HD))
        shapes = (sds((6, 2, HD, TOK), BF16), sds((6, 2, HD, TOK), BF16), sds((TOK, 2 * HD), F32))
        alias = {4 + len(args) - 1: 2}
    else:
        outs = (part, tok(2 * HD))
        shapes = (sds((SLOTS, 2, HD, TOK), F32), sds((TOK, 2 * HD), F32))

    def kernel(*refs):
        backward_kernel(last, *refs)

    return pl.pallas_call(
        kernel,
        out_shape=shapes,
        grid_spec=pltpu.PrefetchScalarGridSpec(
            num_scalar_prefetch=4,
            grid=(SLOTS,),
            in_specs=ins,
            out_specs=outs,
            scratch_shapes=[
                pltpu.VMEM((HALF, 4608), BF16),
                pltpu.VMEM((HALF, 2 * HD), BF16),
                pltpu.VMEM((2, HALF, HD), F32),
                pltpu.VMEM((2, HD, HALF), BF16),
                pltpu.VMEM((2, HD, HALF), BF16),
                pltpu.VMEM((2, HALF, HD), F32),
            ],
        ),
        compiler_params=pltpu.CompilerParams(dimension_semantics=("arbitrary",), vmem_limit_bytes=60 << 20),
        input_output_aliases=alias,
        cost_estimate=pl.CostEstimate(flops=8_000_000_000, bytes_accessed=24_000_000, transcendentals=0),
        name="pull_last" if last else "pull_first",
    )(slot, tile, flag, where, *args)


def weight_kernel(where, *refs):
    cots = refs[:8]
    at_ref, keep_ref, send_ref, cs = refs[8:]
    y, own, core = where[0], where[1], where[2]
    for n, ref in enumerate(cots):
        base = own if n < 4 else 1 - own
        row = pl.multiple_of(base * HALF + lax.rem(y + n % 4, 4) * 64, 64)
        cs[pl.ds(row, 64), :] = ref[...]
    rows = cs[...]
    mine = pl.multiple_of(core * HD, HD)
    other = pl.multiple_of((1 - core) * HD, HD)
    keep_ref[...] = ndot(at_ref[pl.ds(mine, HD), :], rows)
    send_ref[...] = ndot(at_ref[pl.ds(other, HD), :], rows).astype(BF16)


def weight(where, cots, attn_t):
    chunk = 512
    sds = jax.ShapeDtypeStruct
    block = lambda rows: pl.BlockSpec((rows, chunk), lambda i, w: (0, i))
    return pl.pallas_call(
        weight_kernel,
        out_shape=(sds((HD, 4608), F32), sds((HD, 4608), BF16)),
        grid_spec=pltpu.PrefetchScalarGridSpec(
            num_scalar_prefetch=1,
            grid=(4608 // chunk,),
            in_specs=[block(64)] * 8 + [pl.BlockSpec((2 * HD, TOK), lambda i, w: (0, 0))],
            out_specs=(block(HD), block(HD)),
            scratch_shapes=[pltpu.VMEM((TOK, chunk), BF16)],
        ),
        compiler_params=pltpu.CompilerParams(dimension_semantics=("arbitrary",), vmem_limit_bytes=60 << 20),
        cost_estimate=pl.CostEstimate(flops=1_300_000_000, bytes_accessed=9_000_000, transcendentals=0),
        name="weigh",
    )(where, *cots, attn_t)


def local(queries, keys, values, out_weight, cotangent):
    z, xl, c = (lax.axis_index(a) for a in CTX)
    xh, y = (lax.axis_index(a) for a in HEAD)
    lane = xl * 2 + c
    ctx = z * 4 + lane
    cosine, sine = tables(ctx * TOK)
    kf = keys.astype(F32)
    k1, k2 = kf[:, : HD // 2], kf[:, HD // 2 :]
    key_rot = jnp.concatenate([k1 * cosine - k2 * sine, k2 * cosine + k1 * sine], axis=-1).astype(BF16)
    own = jnp.stack([key_rot, values])[None]
    cosf = jnp.concatenate([cosine, cosine], axis=1)
    sinf = jnp.concatenate([-sine, sine], axis=1)

    near1 = from_y(cotangent, 1)
    near3 = from_y(cotangent, 3)
    far0 = swap(cotangent, "xh")
    near2 = from_y(cotangent, 2)
    near = [cotangent, near1, near2, near3]
    far = [far0]
    for d in (1, 2, 3):
        far.append(from_y(far0, d))
    behind1 = along_z(own, 1)
    behind2 = along_z(own, 2)
    mine = jnp.concatenate([behind2, behind1, own])
    across = swap(mine, "xl")
    partner1 = swap(mine, "c")
    partner2 = swap(across, "c")
    panels = (mine, across, partner1, partner2)

    w2 = jnp.transpose(out_weight, (1, 0, 2)).reshape(2 * HD, 4608)

    steps = jnp.arange(SLOTS, dtype=jnp.int32)
    panel, member = steps // 4, steps % 4
    rel = member ^ lane
    slot = (((rel & 1) << 1) | (rel >> 1)) * PANELS + panel
    index = steps - lane
    valid = (index >= 0) & (index < TILES) & (ctx - (TILES - 1) + index >= 0)
    flag = jnp.where(valid, jnp.where(index == 0, 1, jnp.where(index == TILES - 1, 2, 3)), 0)
    tile = jnp.clip(index, 0, TILES - 1)

    e, g, qr, attn, linv, kv, attn_t = forward(slot, tile, flag, queries, cosf, sinf, panels)

    shared = (w2, qr, attn, linv, cosf, sinf, kv, e, g)
    first = backward(slot, tile, flag, jnp.stack([y, xh]), near, *shared, None)
    keep, send, query_grad = backward(slot, tile, flag, jnp.stack([y, 1 - xh]), far, *shared, first)

    got = swap(send, "c")
    both = keep.astype(F32) + got.astype(F32)
    turned = [swap(both[PANELS + p].astype(BF16), "xl") for p in range(PANELS)]
    total = [both[p] + turned[p].astype(F32) for p in range(PANELS)]
    middle = total[1] + along_z(total[0].astype(BF16), -1).astype(F32)
    final = total[2] + along_z(middle.astype(BF16), -1).astype(F32)

    wkeep, wsend = weight(jnp.stack([y, xh, c]), near + far, attn_t)
    wgot = swap(wsend, "c")
    wsum = (wkeep + wgot.astype(F32)).reshape(2, 64, 4608)
    wgive = lax.dynamic_index_in_dim(wsum, 1 - xl, 0, False).astype(BF16)
    wown = lax.dynamic_index_in_dim(wsum, xl, 0, False)
    wback = swap(wgive, "xl")
    wz = (wown + wback.astype(F32)).astype(BF16).reshape(8, 8, 4608)
    wz = lax.all_to_all(wz, "z", 0, 0, tiled=True)
    weight_grad = jnp.sum(wz.astype(F32), axis=0).reshape(4, 2, 4608)

    gk = final[0]
    g1, g2 = gk[: HD // 2], gk[HD // 2 :]
    ct, st = cosine.T, sine.T
    key_grad = jnp.concatenate([g1 * ct + g2 * st, g2 * ct - g1 * st], axis=0).T
    value_grad = final[1].T
    return query_grad, key_grad, value_grad, weight_grad


def solution(mesh):
    fine = Mesh(mesh.devices.reshape(8, 2, 2, 2, 4), CTX + HEAD)
    placed = (P(CTX, HEAD), P(CTX, HEAD), P(CTX, HEAD), P(None, HEAD, None), P(CTX + HEAD, None))
    return jax.shard_map(
        local,
        mesh=fine,
        in_specs=placed,
        out_specs=(P(CTX, HEAD), P(CTX, HEAD), P(CTX, HEAD), P(CTX, HEAD, None)),
        check_vma=False,
    )
```

time: 420 us -> 219 us (0.52)
  the two profiles are of different devices: /device:TPU:107 before, /device:TPU:6 now
where the time goes in v1:
time: 219 us; the launch traced here: 218 us
  waiting for transfers between devices  79.8 us (36%)
  starting transfers between devices  57.1 us (26%)
  Pallas kernels  54 us (25%)
  other arithmetic  19.8 us (9%)
  local copies, waits for them, and re-layouts  6.03 us (3%)
    ppermute x20, waiting for transfers between devices, permute(): return lax.ppermute(x, axis, pairs)  65.7 us
    ppermute x20, starting transfers between devices, permute(): return lax.ppermute(x, axis, pairs)  38.2 us
    pallas_call x2, Pallas kernels, backward(): pl.pallas_call(kernel, out_shape=shapes, grid_spec=pltpu.PrefetchScalarGr...  31.3 us
    all_to_all x1, starting transfers between devices, local(): wz = lax.all_to_all(wz, 'z', 0, 0, tiled=True)  18.9 us
    all_to_all x1, waiting for transfers between devices, local(): wz = lax.all_to_all(wz, 'z', 0, 0, tiled=True)  14.1 us
    pallas_call x1, Pallas kernels, forward(): pl.pallas_call(forward_kernel, out_shape=(sds((TILES, 2, TOK, TOK), BF16)...  13.8 us
    pallas_call x1, Pallas kernels, weight(): pl.pallas_call(weight_kernel, out_shape=(sds((HD, 4608), F32), sds((HD, 4...  8.9 us
  transfers between devices with their start and end apart: 21, of which 12 were waited for; matrix products, arithmetic and copies ran while one was open for 7% of the time, Pallas kernels for 21%

profile of v1, /device:TPU:6, one launch (start us, length us, event | category | flops | bytes accessed | tf_op | source)
XLA Modules:
  0.0 217.6 jit_solution(12260912663250455496)
XLA Ops:
  1.8 1.9 fusion.24
  4.7 3.8 %collective-permute-start.5 = (bf16[1,2,512,128]{3,2,1,0:T(8,128)(2,1)S(1)}, bf16[1,2,512,128]{3,2,1,0:T(8,128)(2,1)S(1)}, u32[]{:S(2)}, u32[]{:S(2)}) collective-permute-start(bf16[1,2,512,128]{3,2,1,0:T(8,128)(2,1)S(1)} %maximum_bitcast_fusion), channel_id=1, source_target_pairs={{0,32},{32,64},{64,96},{96,128},{128,160},{160,192},{192,224},{1,3... | collective-permute-start | bytes 786440 | tf_op jit(solution)/shard_map/ppermute | solution.py:26
  8.5 5.2 %collective-permute-start.4 = (bf16[1,2,512,128]{3,2,1,0:T(8,128)(2,1)S(1)}, bf16[1,2,512,128]{3,2,1,0:T(8,128)(2,1)S(1)}, u32[]{:S(2)}, u32[]{:S(2)}) collective-permute-start(bf16[1,2,512,128]{3,2,1,0:T(8,128)(2,1)S(1)} %maximum_bitcast_fusion), channel_id=1, source_target_pairs={{0,64},{32,96},{64,128},{96,160},{128,192},{160,224},{1,65},{33,97... | collective-permute-start | bytes 786440 | tf_op jit(solution)/shard_map/ppermute | solution.py:26
  14.7 5.0 %collective-permute-done.4 = bf16[1,2,512,128]{3,2,1,0:T(8,128)(2,1)S(1)} collective-permute-done((bf16[1,2,512,128]{3,2,1,0:T(8,128)(2,1)S(1)}, bf16[1,2,512,128]{3,2,1,0:T(8,128)(2,1)S(1)}, u32[]{:S(2)}, u32[]{:S(2)}) %collective-permute-start.4) | collective-permute-done | bytes 262176 | tf_op jit(solution)/shard_map/ppermute | solution.py:26
  21.5 18.3 %collective-permute-done.6.r2 = bf16[3,2,512,128]{3,2,1,0:T(8,128)(2,1)} collective-permute-done((bf16[3,2,512,128]{3,2,1,0:T(8,128)(2,1)}, bf16[3,2,512,128]{3,2,1,0:T(8,128)(2,1)}, u32[]{:S(2)}, u32[]{:S(2)}) %collective-permute-start.6) | collective-permute-done | bytes 786464 | tf_op jit(solution)/shard_map/ppermute | solution.py:26
  39.8 1.6 collective-permute-start.11
  41.4 2.9 %collective-permute-start.10 = (bf16[64,4608]{1,0:T(8,128)(2,1)}, bf16[64,4608]{1,0:T(8,128)(2,1)}, u32[]{:S(2)}, u32[]{:S(2)}) collective-permute-start(bf16[64,4608]{1,0:T(8,128)(2,1)} %refs_0_.1), channel_id=1, source_target_pairs={{2,0},{3,1},{0,2},{1,3},{6,4},{7,5},{4,6},{5,7},{10,8},{11,9},{8,1... | collective-permute-start | bytes 1769480 | tf_op jit(solution)/shard_map/ppermute | solution.py:26
  44.3 1.4 collective-permute-start
  46.3 1.7 copy.10
  50.6 2.0 pad_maximum_fusion.1
  52.6 4.6 %collective-permute-done.11.refs_7_.refs_3_ = bf16[64,4608]{1,0:T(8,128)(2,1)} collective-permute-done((bf16[64,4608]{1,0:T(8,128)(2,1)}, bf16[64,4608]{1,0:T(8,128)(2,1)}, u32[]{:S(2)}, u32[]{:S(2)}) %collective-permute-start.11) | collective-permute-done | bytes 589856 | tf_op jit(solution)/shard_map/ppermute | solution.py:26
  57.2 2.2 %collective-permute-start.9 = (bf16[64,4608]{1,0:T(8,128)(2,1)}, bf16[64,4608]{1,0:T(8,128)(2,1)S(1)}, u32[]{:S(2)}, u32[]{:S(2)}) collective-permute-start(bf16[64,4608]{1,0:T(8,128)(2,1)} %refs_0_.1), channel_id=1, source_target_pairs={{1,0},{2,1},{3,2},{0,3},{5,4},{6,5},{7,6},{4,7},{9,8},{10,9},{11,1... | collective-permute-start | bytes 1769480 | tf_op jit(solution)/shard_map/ppermute | solution.py:26
  59.4 1.8 collective-permute-done.refs_4_
  61.2 12.2 %collective-permute-start.2 = (bf16[64,4608]{1,0:T(8,128)(2,1)S(1)}, bf16[64,4608]{1,0:T(8,128)(2,1)S(1)}, u32[]{:S(2)}, u32[]{:S(2)}) collective-permute-start(bf16[64,4608]{1,0:T(8,128)(2,1)S(1)} %collective-permute-done.refs_4_), channel_id=1, source_target_pairs={{2,0},{3,1},{0,2},{1,3},{6,4},{7,5},{4,6},{5,7},{10,8},{11,9},{8,1... | collective-permute-start | bytes 1769480 | tf_op jit(solution)/shard_map/ppermute | solution.py:26
  74.1 13.8 %attend.1 = (bf16[9,2,512,512]{3,2,1,0:T(8,128)(2,1)}, bf16[9,2,512,512]{3,2,1,0:T(8,128)(2,1)}, bf16[512,256]{1,0:T(8,128)(2,1)}, bf16[512,256]{1,0:T(8,128)(2,...) custom-call(s32[12]{0:T(128)} %get-tuple-element.49.slot.refs_0_, ...), custom_call_target="tpu_custom_call" | custom-call | flops 10000000000 | bytes 24000000 | tf_op jit(solution)/shard_map/attend/pallas_call | solution.py:120
  87.9 8.3 %collective-permute-done.2.refs_6_ = bf16[64,4608]{1,0:T(8,128)(2,1)S(1)} collective-permute-done((bf16[64,4608]{1,0:T(8,128)(2,1)S(1)}, bf16[64,4608]{1,0:T(8,128)(2,1)S(1)}, u32[]{:S(2)}, u32[]{:S(2)}) %collective-permute-start.2) | collective-permute-done | bytes 589856 | tf_op jit(solution)/shard_map/ppermute | solution.py:26
  96.2 1.4 collective-permute-done.1.refs_5_
  98.5 8.9 %weigh.1 = (f32[128,4608]{1,0:T(8,128)}, bf16[128,4608]{1,0:T(8,128)(2,1)}) custom-call(s32[3]{0:T(128)} %pad_add_fusion.2.where, bf16[64,4608]{1,0:T(8,128)(2,1)} %refs_0_.1, bf16[64,4608]{1,0:T(8,128)(2,1)} %copy-done.7, bf16[64,4608]{1,0:T(8,128)(2,1)} %collective-permute-done.10.refs_6_.refs_2_, ...), custom_call_target="tpu_custom_call" | custom-call | flops 1300000000 | bytes 9000000 | tf_op jit(solution)/shard_map/weigh/pallas_call | solution.py:316
  107.7 15.0 %pull_first.1 = (f32[12,2,128,512]{3,2,1,0:T(8,128)}, f32[512,256]{1,0:T(8,128)}) custom-call(s32[12]{0:T(128)} %get-tuple-element.49.slot.refs_0_, s32[12]{0:T(128)} %fusion.27.tile.refs_1_, s32[12]{0:T(128)} %get-tuple-element.48.flag.refs_2_, s32[2]{0:T(128)} %pad_add_fusion.1.refs_3_, bf16[64,4608]{1,0:T(8,128)(2,1)} %refs_0_.1, ...), custom_call_target="tpu_custom_call" | custom-call | flops 8000000000 | bytes 24000000 | tf_op jit(solution)/shard_map/pull_first/pallas_call | solution.py:273
  122.7 16.3 %pull_last.1 = (bf16[6,2,128,512]{3,2,1,0:T(8,128)(2,1)}, bf16[6,2,128,512]{3,2,1,0:T(8,128)(2,1)}, f32[512,256]{1,0:T(8,128)}) custom-call(s32[12]{0:T(128)} %get-tuple-element.49.slot.refs_0_, s32[12]{0:T(128)} %fusion.27.tile.refs_1_, s32[12]{0:T(128)} %get-tuple-element.48.flag.refs_2_, s32[2]{0:T(128)} %pad_add_fusion.refs_3_, ...), custom_call_target="tpu_custom_call", output_to_operand_aliasing={{2}: (18, {})} | custom-call | flops 8000000000 | bytes 24000000 | tf_op jit(solution)/shard_map/pull_last/pallas_call | solution.py:273
  139.0 2.3 %collective-permute-start.12 = (bf16[6,2,128,512]{3,2,1,0:T(8,128)(2,1)}, bf16[6,2,128,512]{3,2,1,0:T(8,128)(2,1)}, u32[]{:S(2)}, u32[]{:S(2)}) collective-permute-start(bf16[6,2,128,512]{3,2,1,0:T(8,128)(2,1)} %get-tuple-element.28), channel_id=1, source_target_pairs={{0,8},{8,0},{1,9},{9,1},{2,10},{10,2},{3,11},{11,3},{4,12},{12,4},... | collective-permute-start | bytes 4718600 | tf_op jit(solution)/shard_map/ppermute | solution.py:26
  141.3 2.0 convert_add_fusion.1
  143.3 1.4 collective-permute-done.12
  144.7 2.0 fusion.28
  147.7 2.1 collective-permute-start.19
  149.9 6.9 %collective-permute-done.15 = bf16[2,128,512]{2,1,0:T(8,128)(2,1)S(1)} collective-permute-done((bf16[2,128,512]{2,1,0:T(8,128)(2,1)S(1)}, bf16[2,128,512]{2,1,0:T(8,128)(2,1)S(1)}, u32[]{:S(2)}, u32[]{:S(2)}) %collective-permute-start.15) | collective-permute-done | bytes 262176 | tf_op jit(solution)/shard_map/ppermute | solution.py:26
  157.6 1.3 collective-permute-start.16
  159.0 16.2 %collective-permute-done.14 = bf16[2,128,512]{2,1,0:T(8,128)(2,1)} collective-permute-done((bf16[2,128,512]{2,1,0:T(8,128)(2,1)}, bf16[2,128,512]{2,1,0:T(8,128)(2,1)}, u32[]{:S(2)}, u32[]{:S(2)}) %collective-permute-start.14) | collective-permute-done | bytes 262176 | tf_op jit(solution)/shard_map/ppermute | solution.py:26
  175.9 2.0 fusion.7
  180.2 18.9 %all-to-all-start = ((bf16[8,8,4608]{2,1,0:T(8,128)(2,1)}), bf16[8,8,4608]{2,1,0:T(8,128)(2,1)S(1)}, u32[]{:S(2)}, u32[]{:S(2)}) async-start(bf16[8,8,4608]{2,1,0:T(8,128)(2,1)} %fusion.2), calls=%async_computation | async-start | bytes 1179648 | tf_op jit(solution)/shard_map/all_to_all | solution.py:392
  199.1 1.3 fusion.9
  202.7 14.1 %all-to-all-done = bf16[8,8,4608]{2,1,0:T(8,128)(2,1)S(1)} async-done(((bf16[8,8,4608]{2,1,0:T(8,128)(2,1)}), bf16[8,8,4608]{2,1,0:T(8,128)(2,1)S(1)}, u32[]{:S(2)}, u32[]{:S(2)}) %all-to-all-start) | async-done | bytes 589856 | tf_op jit(solution)/shard_map/all_to_all | solution.py:392
  (58 shorter events, 18.0 us)
Async XLA Ops:
  0.6 45.7 %copy-start.1 = (bf16[128,2,4608]{2,1,0:T(2,128)(2,1)S(1)}, bf16[128,2,4608]{2,1,0:T(2,128)(2,1)}, u32[]{:S(2)}) copy-start(bf16[128,2,4608]{2,1,0:T(2,128)(2,1)} %param.8) | copy-start | bytes 7077892
  4.7 10.1 %collective-permute-start.5 = (bf16[1,2,512,128]{3,2,1,0:T(8,128)(2,1)S(1)}, bf16[1,2,512,128]{3,2,1,0:T(8,128)(2,1)S(1)}, u32[]{:S(2)}, u32[]{:S(2)}) collective-permute-start(bf16[1,2,512,128]{3,2,1,0:T(8,128)(2,1)S(1)} %maximum_bitcast_fusion), channel_id=1, source_target_pairs={{0,32},{32,64},{64,96},{96,128},{128,160},{160,192},{192,224},{1,3... | collective-permute-start | bytes 786440 | tf_op jit(solution)/shard_map/ppermute | solution.py:26
  8.5 11.2 %collective-permute-start.4 = (bf16[1,2,512,128]{3,2,1,0:T(8,128)(2,1)S(1)}, bf16[1,2,512,128]{3,2,1,0:T(8,128)(2,1)S(1)}, u32[]{:S(2)}, u32[]{:S(2)}) collective-permute-start(bf16[1,2,512,128]{3,2,1,0:T(8,128)(2,1)S(1)} %maximum_bitcast_fusion), channel_id=1, source_target_pairs={{0,64},{32,96},{64,128},{96,160},{128,192},{160,224},{1,65},{33,97... | collective-permute-start | bytes 786440 | tf_op jit(solution)/shard_map/ppermute | solution.py:26
  20.7 19.2 %collective-permute-start.6 = (bf16[3,2,512,128]{3,2,1,0:T(8,128)(2,1)}, bf16[3,2,512,128]{3,2,1,0:T(8,128)(2,1)}, u32[]{:S(2)}, u32[]{:S(2)}) collective-permute-start(bf16[3,2,512,128]{3,2,1,0:T(8,128)(2,1)} %pad_maximum_fusion.r0), channel_id=1, source_target_pairs={{0,16},{16,0},{1,17},{17,1},{2,18},{18,2},{3,19},{19,3},{4,20},{20... | collective-permute-start | bytes 2359304 | tf_op jit(solution)/shard_map/ppermute | solution.py:26
  21.5 39.7 %collective-permute-start.7 = (bf16[3,2,512,128]{3,2,1,0:T(8,128)(2,1)}, bf16[3,2,512,128]{3,2,1,0:T(8,128)(2,1)}, u32[]{:S(2)}, u32[]{:S(2)}) collective-permute-start(bf16[3,2,512,128]{3,2,1,0:T(8,128)(2,1)} %pad_maximum_fusion.r0), channel_id=1, source_target_pairs={{0,8},{8,0},{1,9},{9,1},{2,10},{10,2},{3,11},{11,3},{4,12},{12,4},... | collective-permute-start | bytes 2359304 | tf_op jit(solution)/shard_map/ppermute | solution.py:26
  39.8 33.6 %collective-permute-start.8 = (bf16[3,2,512,128]{3,2,1,0:T(8,128)(2,1)}, bf16[3,2,512,128]{3,2,1,0:T(8,128)(2,1)}, u32[]{:S(2)}, u32[]{:S(2)}) collective-permute-start(bf16[3,2,512,128]{3,2,1,0:T(8,128)(2,1)} %collective-permute-done.6.r2), channel_id=1, source_target_pairs={{0,8},{8,0},{1,9},{9,1},{2,10},{10,2},{3,11},{11,3},{4,12},{12,4},... | collective-permute-start | bytes 2359304 | tf_op jit(solution)/shard_map/ppermute | solution.py:26
  39.8 17.3 %collective-permute-start.11 = (bf16[64,4608]{1,0:T(8,128)(2,1)}, bf16[64,4608]{1,0:T(8,128)(2,1)}, u32[]{:S(2)}, u32[]{:S(2)}) collective-permute-start(bf16[64,4608]{1,0:T(8,128)(2,1)} %refs_0_.1), channel_id=1, source_target_pairs={{3,0},{0,1},{1,2},{2,3},{7,4},{4,5},{5,6},{6,7},{11,8},{8,9},{9,10... | collective-permute-start | bytes 1769480 | tf_op jit(solution)/shard_map/ppermute | solution.py:26
  41.4 46.5 %collective-permute-start.10 = (bf16[64,4608]{1,0:T(8,128)(2,1)}, bf16[64,4608]{1,0:T(8,128)(2,1)}, u32[]{:S(2)}, u32[]{:S(2)}) collective-permute-start(bf16[64,4608]{1,0:T(8,128)(2,1)} %refs_0_.1), channel_id=1, source_target_pairs={{2,0},{3,1},{0,2},{1,3},{6,4},{7,5},{4,6},{5,7},{10,8},{11,9},{8,1... | collective-permute-start | bytes 1769480 | tf_op jit(solution)/shard_map/ppermute | solution.py:26
  44.3 16.9 %collective-permute-start = (bf16[64,4608]{1,0:T(8,128)(2,1)}, bf16[64,4608]{1,0:T(8,128)(2,1)S(1)}, u32[]{:S(2)}, u32[]{:S(2)}) collective-permute-start(bf16[64,4608]{1,0:T(8,128)(2,1)} %refs_0_.1), channel_id=1, source_target_pairs={{0,4},{4,0},{1,5},{5,1},{2,6},{6,2},{3,7},{7,3},{8,12},{12,8},{9,1... | collective-permute-start | bytes 1769480 | tf_op jit(solution)/shard_map/ppermute | solution.py:26
  57.2 30.7 %collective-permute-start.9 = (bf16[64,4608]{1,0:T(8,128)(2,1)}, bf16[64,4608]{1,0:T(8,128)(2,1)S(1)}, u32[]{:S(2)}, u32[]{:S(2)}) collective-permute-start(bf16[64,4608]{1,0:T(8,128)(2,1)} %refs_0_.1), channel_id=1, source_target_pairs={{1,0},{2,1},{3,2},{0,3},{5,4},{6,5},{7,6},{4,7},{9,8},{10,9},{11,1... | collective-permute-start | bytes 1769480 | tf_op jit(solution)/shard_map/ppermute | solution.py:26
  61.2 26.7 %copy-start.2 = (bf16[64,4608]{1,0:T(8,128)(2,1)}, bf16[64,4608]{1,0:T(8,128)(2,1)S(1)}, u32[]{:S(2)}) copy-start(bf16[64,4608]{1,0:T(8,128)(2,1)S(1)} %collective-permute-done.refs_4_) | copy-start | bytes 1769476
  61.2 26.7 %collective-permute-start.3 = (bf16[64,4608]{1,0:T(8,128)(2,1)S(1)}, bf16[64,4608]{1,0:T(8,128)(2,1)S(1)}, u32[]{:S(2)}, u32[]{:S(2)}) collective-permute-start(bf16[64,4608]{1,0:T(8,128)(2,1)S(1)} %collective-permute-done.refs_4_), channel_id=1, source_target_pairs={{3,0},{0,1},{1,2},{2,3},{7,4},{4,5},{5,6},{6,7},{11,8},{8,9},{9,10... | collective-permute-start | bytes 1769480 | tf_op jit(solution)/shard_map/ppermute | solution.py:26
  61.2 35.0 %collective-permute-start.2 = (bf16[64,4608]{1,0:T(8,128)(2,1)S(1)}, bf16[64,4608]{1,0:T(8,128)(2,1)S(1)}, u32[]{:S(2)}, u32[]{:S(2)}) collective-permute-start(bf16[64,4608]{1,0:T(8,128)(2,1)S(1)} %collective-permute-done.refs_4_), channel_id=1, source_target_pairs={{2,0},{3,1},{0,2},{1,3},{6,4},{7,5},{4,6},{5,7},{10,8},{11,9},{8,1... | collective-permute-start | bytes 1769480 | tf_op jit(solution)/shard_map/ppermute | solution.py:26
  73.4 24.3 %collective-permute-start.1 = (bf16[64,4608]{1,0:T(8,128)(2,1)S(1)}, bf16[64,4608]{1,0:T(8,128)(2,1)S(1)}, u32[]{:S(2)}, u32[]{:S(2)}) collective-permute-start(bf16[64,4608]{1,0:T(8,128)(2,1)S(1)} %collective-permute-done.refs_4_), channel_id=1, source_target_pairs={{1,0},{2,1},{3,2},{0,3},{5,4},{6,5},{7,6},{4,7},{9,8},{10,9},{11,1... | collective-permute-start | bytes 1769480 | tf_op jit(solution)/shard_map/ppermute | solution.py:26
  87.9 9.7 %copy-start.7 = (bf16[64,4608]{1,0:T(8,128)(2,1)}, bf16[64,4608]{1,0:T(8,128)(2,1)S(1)}, u32[]{:S(2)}) copy-start(bf16[64,4608]{1,0:T(8,128)(2,1)S(1)} %collective-permute-done.9.refs_5_.refs_1_) | copy-start | bytes 1769476
  87.9 9.7 %copy-start.3 = (bf16[64,4608]{1,0:T(8,128)(2,1)}, bf16[64,4608]{1,0:T(8,128)(2,1)S(1)}, u32[]{:S(2)}) copy-start(bf16[64,4608]{1,0:T(8,128)(2,1)S(1)} %collective-permute-done.3.refs_7_) | copy-start | bytes 1769476
  96.2 1.4 copy-start.4
  97.7 0.9 copy-start.5
  107.4 33.9 %collective-permute-start.18 = (bf16[128,4608]{1,0:T(8,128)(2,1)}, bf16[128,4608]{1,0:T(8,128)(2,1)S(1)}, u32[]{:S(2)}, u32[]{:S(2)}) collective-permute-start(bf16[128,4608]{1,0:T(8,128)(2,1)} %get-tuple-element.31), channel_id=1, source_target_pairs={{0,8},{8,0},{1,9},{9,1},{2,10},{10,2},{3,11},{11,3},{4,12},{12,4},... | collective-permute-start | bytes 3538952 | tf_op jit(solution)/shard_map/ppermute | solution.py:26
  139.0 5.6 %collective-permute-start.12 = (bf16[6,2,128,512]{3,2,1,0:T(8,128)(2,1)}, bf16[6,2,128,512]{3,2,1,0:T(8,128)(2,1)}, u32[]{:S(2)}, u32[]{:S(2)}) collective-permute-start(bf16[6,2,128,512]{3,2,1,0:T(8,128)(2,1)} %get-tuple-element.28), channel_id=1, source_target_pairs={{0,8},{8,0},{1,9},{9,1},{2,10},{10,2},{3,11},{11,3},{4,12},{12,4},... | collective-permute-start | bytes 4718600 | tf_op jit(solution)/shard_map/ppermute | solution.py:26
  141.3 3.4 %copy-start.6 = (bf16[6,2,128,512]{3,2,1,0:T(8,128)(2,1)S(1)}, bf16[6,2,128,512]{3,2,1,0:T(8,128)(2,1)}, u32[]{:S(2)}) copy-start(bf16[6,2,128,512]{3,2,1,0:T(8,128)(2,1)} %get-tuple-element.27) | copy-start | bytes 4718596
  146.7 10.1 %copy-start = (f32[6,2,128,512]{3,2,1,0:T(8,128)}, f32[6,2,128,512]{3,2,1,0:T(8,128)S(1)}, u32[]{:S(2)}) copy-start(f32[6,2,128,512]{3,2,1,0:T(8,128)S(1)} %get-tuple-element.37) | copy-start | bytes 9437188
  147.6 9.2 %collective-permute-start.15 = (bf16[2,128,512]{2,1,0:T(8,128)(2,1)S(1)}, bf16[2,128,512]{2,1,0:T(8,128)(2,1)S(1)}, u32[]{:S(2)}, u32[]{:S(2)}) collective-permute-start(bf16[2,128,512]{2,1,0:T(8,128)(2,1)S(1)} %get-tuple-element.39), channel_id=1, source_target_pairs={{0,16},{16,0},{1,17},{17,1},{2,18},{18,2},{3,19},{19,3},{4,20},{20... | collective-permute-start | bytes 786440 | tf_op jit(solution)/shard_map/ppermute | solution.py:26
  147.7 31.5 %collective-permute-start.19 = (bf16[64,4608]{1,0:T(8,128)(2,1)S(1)}, bf16[64,4608]{1,0:T(8,128)(2,1)S(1)}, u32[]{:S(2)}, u32[]{:S(2)}) collective-permute-start(bf16[64,4608]{1,0:T(8,128)(2,1)S(1)} %fusion.1), channel_id=1, source_target_pairs={{0,16},{16,0},{1,17},{17,1},{2,18},{18,2},{3,19},{19,3},{4,20},{20... | collective-permute-start | bytes 1769480 | tf_op jit(solution)/shard_map/ppermute | solution.py:26
  149.8 25.4 %collective-permute-start.14 = (bf16[2,128,512]{2,1,0:T(8,128)(2,1)}, bf16[2,128,512]{2,1,0:T(8,128)(2,1)}, u32[]{:S(2)}, u32[]{:S(2)}) collective-permute-start(bf16[2,128,512]{2,1,0:T(8,128)(2,1)} %get-tuple-element.40), channel_id=1, source_target_pairs={{0,16},{16,0},{1,17},{17,1},{2,18},{18,2},{3,19},{19,3},{4,20},{20... | collective-permute-start | bytes 786440 | tf_op jit(solution)/shard_map/ppermute | solution.py:26
  157.6 18.3 %collective-permute-start.16 = (bf16[2,128,512]{2,1,0:T(8,128)(2,1)}, bf16[2,128,512]{2,1,0:T(8,128)(2,1)}, u32[]{:S(2)}, u32[]{:S(2)}) collective-permute-start(bf16[2,128,512]{2,1,0:T(8,128)(2,1)} %fusion.4), channel_id=1, source_target_pairs={{32,0},{64,32},{96,64},{128,96},{160,128},{192,160},{224,192},{33,... | collective-permute-start | bytes 786440 | tf_op jit(solution)/shard_map/ppermute | solution.py:26
  158.9 40.2 %collective-permute-start.13 = (bf16[2,128,512]{2,1,0:T(8,128)(2,1)}, bf16[2,128,512]{2,1,0:T(8,128)(2,1)}, u32[]{:S(2)}, u32[]{:S(2)}) collective-permute-start(bf16[2,128,512]{2,1,0:T(8,128)(2,1)} %get-tuple-element.38), channel_id=1, source_target_pairs={{0,16},{16,0},{1,17},{17,1},{2,18},{18,2},{3,19},{19,3},{4,20},{20... | collective-permute-start | bytes 786440 | tf_op jit(solution)/shard_map/ppermute | solution.py:26
  177.9 21.1 %collective-permute-start.17 = (bf16[2,128,512]{2,1,0:T(8,128)(2,1)}, bf16[2,128,512]{2,1,0:T(8,128)(2,1)}, u32[]{:S(2)}, u32[]{:S(2)}) collective-permute-start(bf16[2,128,512]{2,1,0:T(8,128)(2,1)} %fusion.7), channel_id=1, source_target_pairs={{32,0},{64,32},{96,64},{128,96},{160,128},{192,160},{224,192},{33,... | collective-permute-start | bytes 786440 | tf_op jit(solution)/shard_map/ppermute | solution.py:26
  180.2 36.6 %all-to-all-start = ((bf16[8,8,4608]{2,1,0:T(8,128)(2,1)}), bf16[8,8,4608]{2,1,0:T(8,128)(2,1)S(1)}, u32[]{:S(2)}, u32[]{:S(2)}) async-start(bf16[8,8,4608]{2,1,0:T(8,128)(2,1)} %fusion.2), calls=%async_computation | async-start | bytes 1179648 | tf_op jit(solution)/shard_map/all_to_all | solution.py:392

commit v2 on v1

v2 whole, which is shorter than its diff:
```python
import jax
import jax.numpy as jnp
import numpy as np
from jax import lax
from jax.experimental import pallas as pl
from jax.experimental.pallas import tpu as pltpu
from jax.sharding import Mesh, PartitionSpec as P

SOFT_CAP = 50.0
QUERY_MULTIPLIER = 144.0 ** (-0.5)
ROPE_BASE = 10000.0
LOG2E = 1.4426950408889634
CTX = ("z", "xl", "c")
HEAD = ("xh", "y")
TOK = 512
HALF = 256
HD = 128
PANELS = 3
SLOTS = 12
TILES = 9
NT = (((1,), (1,)), ((), ()))
F32 = jnp.float32
BF16 = jnp.bfloat16


def permute(x, axis, pairs):
    return lax.ppermute(x, axis, pairs)


def from_y(x, d):
    return permute(x, "y", [((i + d) % 4, i) for i in range(4)])


def swap(x, axis):
    return permute(x, axis, [(0, 1), (1, 0)])


def along_z(x, step):
    return permute(x, "z", [(i, i + step) for i in range(8) if 0 <= i + step < 8])


FREQUENCY = np.asarray([ROPE_BASE ** (-2.0 * (n % (HD // 2)) / HD) for n in range(HD)], np.float32)
SIGN = np.asarray([-1.0 if n < HD // 2 else 1.0 for n in range(HD)], np.float32)


def tables(first_row):
    positions = first_row + jnp.arange(TOK, dtype=jnp.int32)
    angles = positions.astype(F32)[:, None] * FREQUENCY[None, :]
    return jnp.cos(angles), SIGN[None, :] * jnp.sin(angles)


def place_of(info, i):
    rel = (i & 3) ^ info[0]
    return ((rel & 1) << 1) | (rel >> 1)


def tile_of(info, i):
    return jnp.clip(i - info[0], 0, TILES - 1)


def flag_of(info, i):
    index = i - info[0]
    valid = (index >= 0) & (index < TILES) & (info[1] - (TILES - 1) + index >= 0)
    return jnp.where(valid, jnp.where(index == 0, 1, jnp.where(index == TILES - 1, 2, 3)), 0)


def half_of(info, which):
    return info[3] if which == 1 else 1 - info[3]


def ndot(a, b):
    return jnp.dot(a, b, preferred_element_type=F32)


def tdot(a, b):
    return lax.dot_general(a, b, NT, preferred_element_type=F32)


def turn_kernel(k_ref, v_ref, cos_ref, sin_ref, own_ref):
    x = k_ref[...].astype(F32)
    own_ref[0, 0] = (x * cos_ref[...] + pltpu.roll(x, HD // 2, 1) * sin_ref[...]).astype(BF16)
    own_ref[0, 1] = v_ref[...]


def turn(keys, values, cosf, sinf):
    whole = lambda *shape: pl.BlockSpec(shape, lambda i, *_: (0,) * len(shape))
    return pl.pallas_call(
        turn_kernel,
        out_shape=jax.ShapeDtypeStruct((1, 2, TOK, HD), BF16),
        grid=(1,),
        in_specs=[whole(TOK, HD)] * 4,
        out_specs=whole(1, 2, TOK, HD),
        compiler_params=pltpu.CompilerParams(dimension_semantics=("arbitrary",), vmem_limit_bytes=60 << 20),
        cost_estimate=pl.CostEstimate(flops=500_000, bytes_accessed=1_000_000, transcendentals=0),
        name="turn",
    )(keys, values, cosf, sinf)


def load_pair(place, refs, pair):
    for n, ref in enumerate(refs):

        @pl.when(place == n)
        def _():
            pair[...] = ref[0]


def forward_kernel(
    info, q_ref, cos_ref, sin_ref, r0, r2, r1, r3, e_ref, g_ref, qr_ref, at_ref, li_ref, pt_ref, acc, pair
):
    step = pl.program_id(0)
    flag = flag_of(info, step)

    @pl.when(step == 0)
    def _():
        acc[...] = jnp.zeros_like(acc)
        cosine = cos_ref[...]
        sine = sin_ref[...]
        for h in range(2):
            x = q_ref[:, h * HD : (h + 1) * HD].astype(F32)
            qr_ref[:, h * HD : (h + 1) * HD] = (x * cosine + pltpu.roll(x, HD // 2, 1) * sine).astype(BF16)

    load_pair(place_of(info, step), (r0, r2, r1, r3), pair)

    def body(mode):
        key = pair[0]
        value = jnp.concatenate([pair[1], jnp.ones((TOK, HD), BF16)], axis=1)
        rows = HALF
        for h in range(2):
            for part in range(TOK // rows):
                at = pl.ds(part * rows, rows)
                s = tdot(qr_ref[at, h * HD : (h + 1) * HD], key)
                th = jnp.tanh(s * (QUERY_MULTIPLIER / SOFT_CAP))
                ex = jnp.exp2(th * (SOFT_CAP * LOG2E))
                if mode:
                    t = lax.broadcasted_iota(jnp.int32, (rows, TOK), 0) + part * rows
                    u = lax.broadcasted_iota(jnp.int32, (rows, TOK), 1)
                    ex = jnp.where(u > t if mode == 1 else u <= t, ex, 0.0)
                eb = ex.astype(BF16)
                e_ref[0, h, at, :] = eb
                g_ref[0, h, at, :] = (ex * (1.0 - th * th)).astype(BF16)
                acc[h, at, :] += ndot(eb, value)

    @pl.when(flag == 1)
    def _():
        body(1)

    @pl.when(flag == 2)
    def _():
        body(2)

    @pl.when(flag == 3)
    def _():
        body(0)

    @pl.when(step == SLOTS - 1)
    def _():
        for h in range(2):
            inverse = 1.0 / acc[h, :, HD:]
            at_ref[:, h * HD : (h + 1) * HD] = (acc[h, :, :HD] * inverse).astype(BF16)
            li_ref[:, h * HD : (h + 1) * HD] = inverse
        row = lax.broadcasted_iota(jnp.int32, (2 * HD, 2 * HD), 0)
        col = lax.broadcasted_iota(jnp.int32, (2 * HD, 2 * HD), 1)
        core, left, plane, four, head = row // 128, (row // 64) % 2, (row // 8) % 8, (row // 2) % 4, row % 2
        source = head * HD + plane * 16 + left * 8 + core * 4 + four
        pick = jnp.where(col == source, 1.0, 0.0).astype(BF16)
        pt_ref[...] = tdot(pick, at_ref[...]).astype(BF16)


def forward(info, queries, cosf, sinf, panels):
    whole = lambda *shape: pl.BlockSpec(shape, lambda i, *_: (0,) * len(shape))
    sds = jax.ShapeDtypeStruct
    eg = pl.BlockSpec((1, 2, TOK, TOK), lambda i, f: (tile_of(f, i), 0, 0, 0))
    return pl.pallas_call(
        forward_kernel,
        out_shape=(
            sds((TILES, 2, TOK, TOK), BF16),
            sds((TILES, 2, TOK, TOK), BF16),
            sds((TOK, 2 * HD), BF16),
            sds((TOK, 2 * HD), BF16),
            sds((TOK, 2 * HD), F32),
            sds((2 * HD, TOK), BF16),
        ),
        grid_spec=pltpu.PrefetchScalarGridSpec(
            num_scalar_prefetch=1,
            grid=(SLOTS,),
            in_specs=[
                whole(TOK, 2 * HD),
                whole(TOK, HD),
                whole(TOK, HD),
                *([pl.BlockSpec((1, 2, TOK, HD), lambda i, f: (i // 4, 0, 0, 0))] * 4),
            ],
            out_specs=(
                eg,
                eg,
                whole(TOK, 2 * HD),
                whole(TOK, 2 * HD),
                whole(TOK, 2 * HD),
                whole(2 * HD, TOK),
            ),
            scratch_shapes=[pltpu.VMEM((2, TOK, 2 * HD), F32), pltpu.VMEM((2, TOK, HD), BF16)],
        ),
        compiler_params=pltpu.CompilerParams(dimension_semantics=("arbitrary",), vmem_limit_bytes=60 << 20),
        cost_estimate=pl.CostEstimate(flops=10_000_000_000, bytes_accessed=24_000_000, transcendentals=10_000_000),
        name="attend",
    )(info, queries, cosf, sinf, *panels)


CARRY = (
    ((HALF, 2 * HD), BF16),
    ((2, HALF, HD), F32),
    ((2, HD, HALF), BF16),
    ((2, HD, HALF), BF16),
    ((2, HALF, HD), F32),
)


def backward_kernel(base, count, has_cots, has_prev, final, info, *refs):
    refs = list(refs)
    take = lambda n: [refs.pop(0) for _ in range(n)]
    cots = take(5) if has_cots else []
    carry_in = [] if has_cots else take(5)
    q_ref, at_ref, li_ref, cos_ref, sin_ref = take(5)
    pairs = take(4)
    e_ref, g_ref = take(2)
    if has_prev:
        (prev_ref,) = take(1)
        if final:
            take(1)
        keep_ref, send_ref = take(2)
    else:
        (part_ref,) = take(1)
    qg_ref = take(1)[0] if final else None
    carry_out = [] if final else take(5)
    cs, do, dl, qt, dt, dq, pair = refs
    work = (do, dl, qt, dt, dq)
    step = pl.program_id(0)
    flag = flag_of(info, base + step)

    @pl.when(step == 0)
    def _():
        if has_cots:
            y = info[2]
            for d, ref in enumerate(cots[:4]):
                row = pl.multiple_of(lax.rem(y + d, 4) * 64, 64)
                cs[pl.ds(row, 64), :] = ref[...]
            do[...] = tdot(cs[...], cots[4][...]).astype(BF16)
            for h in range(2):
                col = slice(h * HD, (h + 1) * HD)
                grad = do[:, col].astype(F32)
                inverse = li_ref[:, col]
                total = jnp.sum(grad * at_ref[:, col].astype(F32), axis=1, keepdims=True)
                dl[h] = jnp.broadcast_to(total, (HALF, HD))
                dt[h] = (grad * inverse).T.astype(BF16)
                qt[h] = (q_ref[:, col].astype(F32) * (inverse * QUERY_MULTIPLIER)).T.astype(BF16)
            dq[...] = jnp.zeros_like(dq)
        else:
            for a, b in zip(work, carry_in):
                a[...] = b[...]

    place = place_of(info, base + step)
    load_pair(place, pairs, pair)

    def put(dk, dv):
        if not has_prev:
            part_ref[0, 0] = dk
            part_ref[0, 1] = dv
            return

        @pl.when(place < 2)
        def _():
            keep_ref[place, 0] = dk
            keep_ref[place, 1] = dv

        @pl.when(place >= 2)
        def _():
            send_ref[place - 2, 0] = dk
            send_ref[place - 2, 1] = dv

    @pl.when(flag > 0)
    def _():
        key = pair[0]
        value = pair[1]
        dk = jnp.zeros((HD, TOK), F32)
        dv = jnp.zeros((HD, TOK), F32)
        for h in range(2):
            dp = tdot(do[:, h * HD : (h + 1) * HD], value)
            x = (g_ref[0, h].astype(F32) * (dp - dl[h][:, :1])).astype(BF16)
            dq[h] += ndot(x, key)
            dk += ndot(qt[h], x)
            dv += ndot(dt[h], e_ref[0, h])
        if has_prev:
            dk = dk + prev_ref[0, 0].astype(F32)
            dv = dv + prev_ref[0, 1].astype(F32)
        put(dk.astype(BF16), dv.astype(BF16))

    if has_prev:

        @pl.when(flag == 0)
        def _():
            zero = jnp.zeros((HD, TOK), BF16)
            put(zero, zero)

    @pl.when(step == count - 1)
    def _():
        if final:
            cosine = cos_ref[...]
            sine = sin_ref[...]
            for h in range(2):
                col = slice(h * HD, (h + 1) * HD)
                g = dq[h] * (li_ref[:, col] * QUERY_MULTIPLIER)
                qg_ref[:, col] = g * cosine - pltpu.roll(g, HD // 2, 1) * sine
        else:
            for a, b in zip(carry_out, work):
                a[...] = b[...]


def backward(base, count, which, info, rows, panels, e, g, cots=None, w2=None, carry=None, prev=None, grad=None):
    has_cots, has_prev = cots is not None, prev is not None
    final = base + count == SLOTS
    sds = jax.ShapeDtypeStruct
    whole = lambda *shape: pl.BlockSpec(shape, lambda i, *_: (0,) * len(shape))
    tok = lambda width: pl.BlockSpec((HALF, width), lambda i, f: (half_of(f, which), 0))
    eg = pl.BlockSpec((1, 2, HALF, TOK), lambda i, f: (tile_of(f, base + i), 0, half_of(f, which), 0))
    part = pl.BlockSpec((1, 2, HD, TOK), lambda i, f: ((base + i) // 4 * 4 + place_of(f, base + i), 0, 0, 0))
    ins, args, alias = [], [], {}
    if has_cots:
        ins += [whole(64, 4608)] * 4 + [whole(2 * HD, 4608)]
        args += [*cots, w2]
    else:
        ins += [whole(*shape) for shape, _ in CARRY]
        args += list(carry)
    ins += [tok(2 * HD), tok(2 * HD), tok(2 * HD), tok(HD), tok(HD)]
    args += list(rows)
    ins += [pl.BlockSpec((1, 2, TOK, HD), lambda i, f: ((base + i) // 4, 0, 0, 0))] * 4 + [eg, eg]
    args += [*panels, e, g]
    if has_prev:
        ins += [part]
        args += [prev]
        outs = [whole(2, 2, HD, TOK)] * 2
        shapes = [sds((2, 2, HD, TOK), BF16)] * 2
    else:
        outs = [part]
        shapes = [sds((SLOTS, 2, HD, TOK), BF16)]
    if final:
        if grad is not None:
            ins += [pl.BlockSpec(memory_space=pl.ANY)]
            args += [grad]
            alias = {len(args): len(outs)}
        outs += [tok(2 * HD)]
        shapes += [sds((TOK, 2 * HD), F32)]
    else:
        outs += [whole(*shape) for shape, _ in CARRY]
        shapes += [sds(*c) for c in CARRY]

    def kernel(*refs):
        backward_kernel(base, count, has_cots, has_prev, final, *refs)

    return pl.pallas_call(
        kernel,
        out_shape=shapes,
        grid_spec=pltpu.PrefetchScalarGridSpec(
            num_scalar_prefetch=1,
            grid=(count,),
            in_specs=ins,
            out_specs=outs,
            scratch_shapes=[
                pltpu.VMEM((HALF, 4608) if has_cots else (16, 128), BF16),
                *(pltpu.VMEM(*c) for c in CARRY),
                pltpu.VMEM((2, TOK, HD), BF16),
            ],
        ),
        compiler_params=pltpu.CompilerParams(dimension_semantics=("arbitrary",), vmem_limit_bytes=60 << 20),
        input_output_aliases=alias,
        cost_estimate=pl.CostEstimate(flops=700_000_000 * count, bytes_accessed=2_000_000 * count, transcendentals=0),
    )(info, *args)


def weight_kernel(where, *refs):
    cots = refs[:8]
    at_ref, keep_ref, send_ref, cs = refs[8:]
    y, own, core = where[2], where[3], where[4]
    for n, ref in enumerate(cots):
        base = own if n < 4 else 1 - own
        row = pl.multiple_of(base * HALF + lax.rem(y + n % 4, 4) * 64, 64)
        cs[pl.ds(row, 64), :] = ref[...]
    rows = cs[...]
    mine = pl.multiple_of(core * HD, HD)
    other = pl.multiple_of((1 - core) * HD, HD)
    keep_ref[...] = ndot(at_ref[pl.ds(mine, HD), :], rows)
    send_ref[...] = ndot(at_ref[pl.ds(other, HD), :], rows).astype(BF16)


def weight(where, cots, attn_t):
    chunk = 1152
    sds = jax.ShapeDtypeStruct
    block = lambda rows: pl.BlockSpec((rows, chunk), lambda i, w: (0, i))
    return pl.pallas_call(
        weight_kernel,
        out_shape=(sds((HD, 4608), F32), sds((HD, 4608), BF16)),
        grid_spec=pltpu.PrefetchScalarGridSpec(
            num_scalar_prefetch=1,
            grid=(4608 // chunk,),
            in_specs=[block(64)] * 8 + [pl.BlockSpec((2 * HD, TOK), lambda i, w: (0, 0))],
            out_specs=(block(HD), block(HD)),
            scratch_shapes=[pltpu.VMEM((TOK, chunk), BF16)],
        ),
        compiler_params=pltpu.CompilerParams(dimension_semantics=("arbitrary",), vmem_limit_bytes=60 << 20),
        cost_estimate=pl.CostEstimate(flops=1_300_000_000, bytes_accessed=9_000_000, transcendentals=0),
        name="weigh",
    )(where, *cots, attn_t)


def settle_kernel(own_ref, left_ref, down_ref, cos_ref, sin_ref, kg_ref, vg_ref):
    both = own_ref[0] + left_ref[...].astype(F32) + down_ref[...].astype(F32)
    g = both[0].T
    kg_ref[...] = g * cos_ref[...] - pltpu.roll(g, HD // 2, 1) * sin_ref[...]
    vg_ref[...] = both[1].T


def settle(both, left, down, cosf, sinf):
    whole = lambda *shape: pl.BlockSpec(shape, lambda i, *_: (0,) * len(shape))
    sds = jax.ShapeDtypeStruct
    return pl.pallas_call(
        settle_kernel,
        out_shape=(sds((TOK, HD), F32), sds((TOK, HD), F32)),
        grid=(1,),
        in_specs=[whole(1, 2, HD, TOK), whole(2, HD, TOK), whole(2, HD, TOK), whole(TOK, HD), whole(TOK, HD)],
        out_specs=(whole(TOK, HD), whole(TOK, HD)),
        compiler_params=pltpu.CompilerParams(dimension_semantics=("arbitrary",), vmem_limit_bytes=60 << 20),
        cost_estimate=pl.CostEstimate(flops=500_000, bytes_accessed=2_000_000, transcendentals=0),
        name="settle",
    )(both, left, down, cosf, sinf)


def local(queries, keys, values, out_weight, cotangent):
    z, xl, c = (lax.axis_index(a) for a in CTX)
    xh, y = (lax.axis_index(a) for a in HEAD)
    lane = xl * 2 + c
    ctx = z * 4 + lane
    cosf, sinf = tables(ctx * TOK)

    info = jnp.stack([lane, ctx, y, xh, c]).astype(jnp.int32)

    own = turn(keys, values, cosf, sinf)
    behind1 = along_z(own, 1)
    behind2 = along_z(own, 2)
    across0 = swap(own, "xl")
    near1 = from_y(cotangent, 1)
    near3 = from_y(cotangent, 3)
    far0 = swap(cotangent, "xh")
    near2 = from_y(cotangent, 2)
    near = [cotangent, near1, near2, near3]
    far = [far0]
    for d in (1, 2, 3):
        far.append(from_y(far0, d))
    back = jnp.concatenate([behind2, behind1])
    across = swap(back, "xl")
    mine = jnp.concatenate([back, own])
    partner1 = swap(mine, "c")
    across = jnp.concatenate([across, across0])
    partner2 = swap(across, "c")
    panels = (mine, across, partner1, partner2)

    w2 = jnp.transpose(out_weight, (1, 0, 2)).reshape(2 * HD, 4608)

    e, g, qr, attn, linv, attn_t = forward(info, queries, cosf, sinf, panels)
    rows = (qr, attn, linv, cosf, sinf)
    prev, half = backward(0, SLOTS, 1, info, rows, panels, e, g, cots=near, w2=w2)

    wkeep, wsend = weight(info, near + far, attn_t)
    wgot = swap(wsend, "c")
    wsum = (wkeep + wgot.astype(F32)).reshape(2, 64, 4608)
    wgive = lax.dynamic_index_in_dim(wsum, 1 - xl, 0, False).astype(BF16)
    wown = lax.dynamic_index_in_dim(wsum, xl, 0, False)
    wback = swap(wgive, "xl")
    wz = (wown + wback.astype(F32)).astype(BF16).reshape(8, 8, 4608)
    wz = lax.all_to_all(wz, "z", 0, 0, tiled=True)
    weight_grad = jnp.sum(wz.astype(F32), axis=0).reshape(4, 2, 4608)

    total = []
    carry = None
    for p in range(PANELS):
        out = backward(
            p * 4, 4, 2, info, rows, panels, e, g,
            cots=far if p == 0 else None, w2=w2 if p == 0 else None, carry=carry, prev=prev,
            grad=half if p == PANELS - 1 else None,
        )
        keep, send, *carry = out
        got = swap(send, "c")
        both = keep.astype(F32) + got.astype(F32)
        give = both[1].astype(BF16)
        turned = swap(give, "xl")
        total.append((both, turned))
    (query_grad,) = carry
    down1 = along_z((total[0][0][0] + total[0][1].astype(F32)).astype(BF16), -1)
    down0 = along_z((total[1][0][0] + total[1][1].astype(F32) + down1.astype(F32)).astype(BF16), -1)
    key_grad, value_grad = settle(*total[2], down0, cosf, sinf)
    return query_grad, key_grad, value_grad, weight_grad


def solution(mesh):
    fine = Mesh(mesh.devices.reshape(8, 2, 2, 2, 4), CTX + HEAD)
    placed = (P(CTX, HEAD), P(CTX, HEAD), P(CTX, HEAD), P(None, HEAD, None), P(CTX + HEAD, None))
    return jax.shard_map(
        local,
        mesh=fine,
        in_specs=placed,
        out_specs=(P(CTX, HEAD), P(CTX, HEAD), P(CTX, HEAD), P(CTX, HEAD, None)),
        check_vma=False,
    )
```

time: 219 us -> 218 us (level)
  the two profiles are of different devices: /device:TPU:6 before, /device:TPU:96 now
where the time goes in v2:
time: 218 us; the launch traced here: 217 us
  waiting for transfers between devices  89.9 us (41%)
  Pallas kernels  69.2 us (32%)
  starting transfers between devices  40.7 us (19%)
  local copies, waits for them, and re-layouts  8.3 us (4%)
  other arithmetic  8.26 us (4%)
    ppermute x23, waiting for transfers between devices, permute(): return lax.ppermute(x, axis, pairs)  89.9 us
    pallas_call x4, Pallas kernels, backward(): pl.pallas_call(kernel, out_shape=shapes, grid_spec=pltpu.PrefetchScalarGr...  42.1 us
    ppermute x23, starting transfers between devices, permute(): return lax.ppermute(x, axis, pairs)  33.4 us
    pallas_call x1, Pallas kernels, forward(): pl.pallas_call(forward_kernel, out_shape=(sds((TILES, 2, TOK, TOK), BF16)...  16.1 us
    all_to_all x1, starting transfers between devices, local(): wz = lax.all_to_all(wz, 'z', 0, 0, tiled=True)  7.37 us
    pallas_call x1, Pallas kernels, weight(): pl.pallas_call(weight_kernel, out_shape=(sds((HD, 4608), F32), sds((HD, 4...  6.71 us
  transfers between devices with their start and end apart: 24, of which 12 were waited for; matrix products, arithmetic and copies ran while one was open for 5% of the time, Pallas kernels for 28%

profile of v2, /device:TPU:96, one launch (start us, length us, event | category | flops | bytes accessed | tf_op | source)
XLA Modules:
  0.0 217.3 jit_solution(15784564185633581412)
XLA Ops:
  0.7 2.5 %fusion.8 = (f32[512,128]{1,0:T(8,128)}, f32[512,128]{1,0:T(8,128)}) fusion(f32[128]{0:T(128)} %constant.49, f32[128]{0:T(128)} %constant.48, f32[512]{0:T(512)S(1)} %add_convert_fusion), kind=kLoop, calls=%fused_computation.24 | loop fusion | flops 131072 | bytes 527360 | tf_op jit(solution)/shard_map/mul | solution.py:49
  3.2 2.0 turn.1
  5.2 5.5 %collective-permute-start.4 = (bf16[1,2,512,128]{3,2,1,0:T(8,128)(2,1)}, bf16[1,2,512,128]{3,2,1,0:T(8,128)(2,1)S(1)}, u32[]{:S(2)}, u32[]{:S(2)}) collective-permute-start(bf16[1,2,512,128]{3,2,1,0:T(8,128)(2,1)} %turn.1), channel_id=1, source_target_pairs={{0,64},{32,96},{64,128},{96,160},{128,192},{160,224},{1,65},{33,97... | collective-permute-start | bytes 786440 | tf_op jit(solution)/shard_map/ppermute | solution.py:27
  10.6 2.9 %collective-permute-start.5 = (bf16[1,2,512,128]{3,2,1,0:T(8,128)(2,1)}, bf16[1,2,512,128]{3,2,1,0:T(8,128)(2,1)S(1)}, u32[]{:S(2)}, u32[]{:S(2)}) collective-permute-start(bf16[1,2,512,128]{3,2,1,0:T(8,128)(2,1)} %turn.1), channel_id=1, source_target_pairs={{0,32},{32,64},{64,96},{96,128},{128,160},{160,192},{192,224},{1,3... | collective-permute-start | bytes 786440 | tf_op jit(solution)/shard_map/ppermute | solution.py:27
  13.6 7.9 %collective-permute-done.4 = bf16[1,2,512,128]{3,2,1,0:T(8,128)(2,1)S(1)} collective-permute-done((bf16[1,2,512,128]{3,2,1,0:T(8,128)(2,1)}, bf16[1,2,512,128]{3,2,1,0:T(8,128)(2,1)S(1)}, u32[]{:S(2)}, u32[]{:S(2)}) %collective-permute-start.4) | collective-permute-done | bytes 262176 | tf_op jit(solution)/shard_map/ppermute | solution.py:27
  21.5 7.5 %collective-permute-done.5 = bf16[1,2,512,128]{3,2,1,0:T(8,128)(2,1)S(1)} collective-permute-done((bf16[1,2,512,128]{3,2,1,0:T(8,128)(2,1)}, bf16[1,2,512,128]{3,2,1,0:T(8,128)(2,1)S(1)}, u32[]{:S(2)}, u32[]{:S(2)}) %collective-permute-start.5) | collective-permute-done | bytes 262176 | tf_op jit(solution)/shard_map/ppermute | solution.py:27
  29.1 1.6 collective-permute-start.6
  32.4 11.6 %collective-permute-done.6 = bf16[2,2,512,128]{3,2,1,0:T(8,128)(2,1)S(1)} collective-permute-done((bf16[2,2,512,128]{3,2,1,0:T(8,128)(2,1)S(1)}, bf16[2,2,512,128]{3,2,1,0:T(8,128)(2,1)S(1)}, u32[]{:S(2)}, u32[]{:S(2)}) %collective-permute-start.6) | collective-permute-done | bytes 524320 | tf_op jit(solution)/shard_map/ppermute | solution.py:27
  44.0 3.6 %collective-permute-done.7 = bf16[1,2,512,128]{3,2,1,0:T(8,128)(2,1)S(1)} collective-permute-done((bf16[1,2,512,128]{3,2,1,0:T(8,128)(2,1)}, bf16[1,2,512,128]{3,2,1,0:T(8,128)(2,1)S(1)}, u32[]{:S(2)}, u32[]{:S(2)}) %collective-permute-start.7) | collective-permute-done | bytes 262176 | tf_op jit(solution)/shard_map/ppermute | solution.py:27
  47.8 3.1 %collective-permute-start = (bf16[64,4608]{1,0:T(8,128)(2,1)}, bf16[64,4608]{1,0:T(8,128)(2,1)}, u32[]{:S(2)}, u32[]{:S(2)}) collective-permute-start(bf16[64,4608]{1,0:T(8,128)(2,1)} %refs_0_.1), channel_id=1, source_target_pairs={{0,4},{4,0},{1,5},{5,1},{2,6},{6,2},{3,7},{7,3},{8,12},{12,8},{9,1... | collective-permute-start | bytes 1769480 | tf_op jit(solution)/shard_map/ppermute | solution.py:27
  50.9 3.0 %collective-permute-start.10 = (bf16[64,4608]{1,0:T(8,128)(2,1)}, bf16[64,4608]{1,0:T(8,128)(2,1)}, u32[]{:S(2)}, u32[]{:S(2)}) collective-permute-start(bf16[64,4608]{1,0:T(8,128)(2,1)} %refs_0_.1), channel_id=1, source_target_pairs={{1,0},{2,1},{3,2},{0,3},{5,4},{6,5},{7,6},{4,7},{9,8},{10,9},{11,1... | collective-permute-start | bytes 1769480 | tf_op jit(solution)/shard_map/ppermute | solution.py:27
  54.5 3.4 %copy.12 = bf16[2,128,4608]{2,1,0:T(8,128)(2,1)} copy(bf16[2,128,4608]{2,0,1:T(2,128)(2,1)} %bitcast.42) | data formatting | bytes 4718592 | tf_op jit(solution)/shard_map/transpose | solution.py:464
  58.6 6.8 %collective-permute-done.refs_1_.refs_4_ = bf16[64,4608]{1,0:T(8,128)(2,1)} collective-permute-done((bf16[64,4608]{1,0:T(8,128)(2,1)}, bf16[64,4608]{1,0:T(8,128)(2,1)}, u32[]{:S(2)}, u32[]{:S(2)}) %collective-permute-start) | collective-permute-done | bytes 589856 | tf_op jit(solution)/shard_map/ppermute | solution.py:27
  65.3 1.6 collective-permute-start.12
  66.9 12.8 %collective-permute-done.10.refs_2_.refs_1_ = bf16[64,4608]{1,0:T(8,128)(2,1)} collective-permute-done((bf16[64,4608]{1,0:T(8,128)(2,1)}, bf16[64,4608]{1,0:T(8,128)(2,1)}, u32[]{:S(2)}, u32[]{:S(2)}) %collective-permute-start.10) | collective-permute-done | bytes 589856 | tf_op jit(solution)/shard_map/ppermute | solution.py:27
  79.8 3.7 %collective-permute-start.1 = (bf16[64,4608]{1,0:T(8,128)(2,1)}, bf16[64,4608]{1,0:T(8,128)(2,1)}, u32[]{:S(2)}, u32[]{:S(2)}) collective-permute-start(bf16[64,4608]{1,0:T(8,128)(2,1)} %collective-permute-done.refs_1_.refs_4_), channel_id=1, source_target_pairs={{1,0},{2,1},{3,2},{0,3},{5,4},{6,5},{7,6},{4,7},{9,8},{10,9},{11,1... | collective-permute-start | bytes 1769480 | tf_op jit(solution)/shard_map/ppermute | solution.py:27
  84.6 16.1 %attend.1 = (bf16[9,2,512,512]{3,2,1,0:T(8,128)(2,1)}, bf16[9,2,512,512]{3,2,1,0:T(8,128)(2,1)}, bf16[512,256]{1,0:T(8,128)(2,1)}, bf16[512,256]{1,0:T(8,128)(2,...) custom-call(s32[5]{0:T(128)} %stack.23.info.refs_0_.where, bf16[512,256]{1,0:T(8,128)(2,1)} %q_ref.1, ...), custom_call_target="tpu_custom_call" | custom-call | flops 10000000000 | bytes 24000000 | tf_op jit(solution)/shard_map/attend/pallas_call | solution.py:173
  100.7 7.7 %collective-permute-done.1.refs_2_.refs_5_ = bf16[64,4608]{1,0:T(8,128)(2,1)} collective-permute-done((bf16[64,4608]{1,0:T(8,128)(2,1)}, bf16[64,4608]{1,0:T(8,128)(2,1)}, u32[]{:S(2)}, u32[]{:S(2)}) %collective-permute-start.1) | collective-permute-done | bytes 589856 | tf_op jit(solution)/shard_map/ppermute | solution.py:27
  108.4 3.4 %collective-permute-done.3.refs_4_.refs_7_ = bf16[64,4608]{1,0:T(8,128)(2,1)S(1)} collective-permute-done((bf16[64,4608]{1,0:T(8,128)(2,1)}, bf16[64,4608]{1,0:T(8,128)(2,1)S(1)}, u32[]{:S(2)}, u32[]{:S(2)}) %collective-permute-start.3) | collective-permute-done | bytes 589856 | tf_op jit(solution)/shard_map/ppermute | solution.py:27
  112.7 6.7 %weigh.1 = (f32[128,4608]{1,0:T(8,128)}, bf16[128,4608]{1,0:T(8,128)(2,1)}) custom-call(s32[5]{0:T(128)} %stack.23.info.refs_0_.where, bf16[64,4608]{1,0:T(8,128)(2,1)} %refs_0_.1, bf16[64,4608]{1,0:T(8,128)(2,1)} %collective-permute-done.10.refs_2_.refs_1_, bf16[64,4608]{1,0:T(8,128)(2,1)} %collective-permute-done.11.refs_3_.refs_2_, ...), custom_call_target="tpu_custom_call" | custom-call | flops 1300000000 | bytes 9000000 | tf_op jit(solution)/shard_map/weigh/pallas_call | solution.py:397
  119.6 16.9 %shard_map.102 = (bf16[12,2,128,512]{3,2,1,0:T(8,128)(2,1)}, f32[512,256]{1,0:T(8,128)}) custom-call(s32[5]{0:T(128)} %stack.23.info.refs_0_.where, bf16[64,4608]{1,0:T(8,128)(2,1)} %refs_0_.1, bf16[64,4608]{1,0:T(8,128)(2,1)} %collective-permute-done.10.refs_2_.refs_1_, bf16[64,4608]{1,0:T(8,128)(2,1)} %collective-permute-done.11.refs_3_.refs_2_, ...), custom_call_target="tpu_custom_call" | custom-call | flops 8400000000 | bytes 24000000 | tf_op jit(solution)/shard_map/pallas_call | solution.py:358
  136.5 10.6 %shard_map.103 = (bf16[2,2,128,512]{3,2,1,0:T(8,128)(2,1)}, bf16[2,2,128,512]{3,2,1,0:T(8,128)(2,1)}, bf16[256,256]{1,0:T(8,128)(2,1)}, f32[2,256,128]{2,1,0:T(8...) custom-call(s32[5]{0:T(128)} %stack.23.info.refs_0_.where, ...), custom_call_target="tpu_custom_call" | custom-call | flops 2800000000 | bytes 8000000 | tf_op jit(solution)/shard_map/pallas_call | solution.py:358
  147.2 8.3 %shard_map.104 = (bf16[2,2,128,512]{3,2,1,0:T(8,128)(2,1)}, bf16[2,2,128,512]{3,2,1,0:T(8,128)(2,1)}, bf16[256,256]{1,0:T(8,128)(2,1)}, f32[2,256,128]{2,1,0:T(8...) custom-call(s32[5]{0:T(128)} %stack.23.info.refs_0_.where, ...), custom_call_target="tpu_custom_call" | custom-call | flops 2800000000 | bytes 8000000 | tf_op jit(solution)/shard_map/pallas_call | solution.py:358
  156.0 6.4 %shard_map.105 = (bf16[2,2,128,512]{3,2,1,0:T(8,128)(2,1)}, bf16[2,2,128,512]{3,2,1,0:T(8,128)(2,1)}, f32[512,256]{1,0:T(8,128)}) custom-call(s32[5]{0:T(128)} %stack.23.info.refs_0_.where, bf16[256,256]{1,0:T(8,128)(2,1)} %get-tuple-element.44.refs_1_, f32[2,256,128]{2,1,0:T(8,128)} %get-tuple-element.45.refs_2_, ...), custom_call_target="tpu_custom_call", output_to_operand_aliasing={{2}: (18, {})} | custom-call | flops 2800000000 | bytes 8000000 | tf_op jit(solution)/shard_map/pallas_call | solution.py:358
  167.6 5.2 %collective-permute-done.18 = bf16[2,128,512]{2,1,0:T(8,128)(2,1)S(1)} collective-permute-done((bf16[2,128,512]{2,1,0:T(8,128)(2,1)S(1)}, bf16[2,128,512]{2,1,0:T(8,128)(2,1)S(1)}, u32[]{:S(2)}, u32[]{:S(2)}) %collective-permute-start.18) | collective-permute-done | bytes 262176 | tf_op jit(solution)/shard_map/ppermute | solution.py:27
  173.5 1.9 collective-permute-start.19
  175.4 9.9 %collective-permute-done.22 = bf16[64,4608]{1,0:T(8,128)(2,1)S(1)} collective-permute-done((bf16[64,4608]{1,0:T(8,128)(2,1)S(1)}, bf16[64,4608]{1,0:T(8,128)(2,1)S(1)}, u32[]{:S(2)}, u32[]{:S(2)}) %collective-permute-start.22) | collective-permute-done | bytes 589856 | tf_op jit(solution)/shard_map/ppermute | solution.py:27
  186.3 7.4 %all-to-all-start = ((bf16[8,8,4608]{2,1,0:T(8,128)(2,1)}), bf16[8,8,4608]{2,1,0:T(8,128)(2,1)S(1)}, u32[]{:S(2)}, u32[]{:S(2)}) async-start(bf16[8,8,4608]{2,1,0:T(8,128)(2,1)} %fusion.2), calls=%async_computation | async-start | bytes 1179648 | tf_op jit(solution)/shard_map/all_to_all | solution.py:477
  197.6 2.5 %collective-permute-start.20 = (bf16[2,128,512]{2,1,0:T(8,128)(2,1)S(1)}, bf16[2,128,512]{2,1,0:T(8,128)(2,1)S(1)}, u32[]{:S(2)}, u32[]{:S(2)}) collective-permute-start(bf16[2,128,512]{2,1,0:T(8,128)(2,1)S(1)} %fusion.7), channel_id=1, source_target_pairs={{32,0},{64,32},{96,64},{128,96},{160,128},{192,160},{224,192},{33,... | collective-permute-start | bytes 786440 | tf_op jit(solution)/shard_map/ppermute | solution.py:27
  200.1 2.2 collective-permute-done.14.left_ref
  202.2 11.2 %collective-permute-done.20.down_ref = bf16[2,128,512]{2,1,0:T(8,128)(2,1)S(1)} collective-permute-done((bf16[2,128,512]{2,1,0:T(8,128)(2,1)S(1)}, bf16[2,128,512]{2,1,0:T(8,128)(2,1)S(1)}, u32[]{:S(2)}, u32[]{:S(2)}) %collective-permute-start.20) | collective-permute-done | bytes 262176 | tf_op jit(solution)/shard_map/ppermute | solution.py:27
  214.1 2.4 %settle.1 = (f32[512,128]{1,0:T(8,128)}, f32[512,128]{1,0:T(8,128)}) custom-call(f32[2,2,128,512]{3,2,1,0:T(8,128)} %copy-done.4, bf16[2,128,512]{2,1,0:T(8,128)(2,1)} %copy-done.12, bf16[2,128,512]{2,1,0:T(8,128)(2,1)} %copy-done.13, f32[512,128]{1,0:T(8,128)} %get-tuple-element.63.cos_ref.refs_9_, f32[512,128]{1,0:T(8,128)} %get-tuple-element.62.sin_ref.refs_10_), custom_call_target="tpu_custom_call" | custom-call | flops 500000 | bytes 2000000 | tf_op jit(solution)/shard_map/settle/pallas_call | solution.py:423
  (73 shorter events, 18.3 us)
Async XLA Ops:
  5.2 16.3 %collective-permute-start.4 = (bf16[1,2,512,128]{3,2,1,0:T(8,128)(2,1)}, bf16[1,2,512,128]{3,2,1,0:T(8,128)(2,1)S(1)}, u32[]{:S(2)}, u32[]{:S(2)}) collective-permute-start(bf16[1,2,512,128]{3,2,1,0:T(8,128)(2,1)} %turn.1), channel_id=1, source_target_pairs={{0,64},{32,96},{64,128},{96,160},{128,192},{160,224},{1,65},{33,97... | collective-permute-start | bytes 786440 | tf_op jit(solution)/shard_map/ppermute | solution.py:27
  10.6 18.4 %collective-permute-start.5 = (bf16[1,2,512,128]{3,2,1,0:T(8,128)(2,1)}, bf16[1,2,512,128]{3,2,1,0:T(8,128)(2,1)S(1)}, u32[]{:S(2)}, u32[]{:S(2)}) collective-permute-start(bf16[1,2,512,128]{3,2,1,0:T(8,128)(2,1)} %turn.1), channel_id=1, source_target_pairs={{0,32},{32,64},{64,96},{96,128},{128,160},{160,192},{192,224},{1,3... | collective-permute-start | bytes 786440 | tf_op jit(solution)/shard_map/ppermute | solution.py:27
  29.1 14.9 %collective-permute-start.6 = (bf16[2,2,512,128]{3,2,1,0:T(8,128)(2,1)S(1)}, bf16[2,2,512,128]{3,2,1,0:T(8,128)(2,1)S(1)}, u32[]{:S(2)}, u32[]{:S(2)}) collective-permute-start(bf16[2,2,512,128]{3,2,1,0:T(8,128)(2,1)S(1)} %pad_maximum_fusion.1), channel_id=1, source_target_pairs={{0,16},{16,0},{1,17},{17,1},{2,18},{18,2},{3,19},{19,3},{4,20},{20... | collective-permute-start | bytes 1572872 | tf_op jit(solution)/shard_map/ppermute | solution.py:27
  30.7 17.0 %collective-permute-start.7 = (bf16[1,2,512,128]{3,2,1,0:T(8,128)(2,1)}, bf16[1,2,512,128]{3,2,1,0:T(8,128)(2,1)S(1)}, u32[]{:S(2)}, u32[]{:S(2)}) collective-permute-start(bf16[1,2,512,128]{3,2,1,0:T(8,128)(2,1)} %turn.1), channel_id=1, source_target_pairs={{0,16},{16,0},{1,17},{17,1},{2,18},{18,2},{3,19},{19,3},{4,20},{20... | collective-permute-start | bytes 786440 | tf_op jit(solution)/shard_map/ppermute | solution.py:27
  32.3 25.6 %copy-start = (bf16[3,2,512,128]{3,2,1,0:T(8,128)(2,1)}, bf16[3,2,512,128]{3,2,1,0:T(8,128)(2,1)S(1)}, u32[]{:S(2)}) copy-start(bf16[3,2,512,128]{3,2,1,0:T(8,128)(2,1)S(1)} %pad_maximum_fusion.r0.refs_11_) | copy-start | bytes 2359300
  32.3 51.2 %collective-permute-start.8 = (bf16[3,2,512,128]{3,2,1,0:T(8,128)(2,1)S(1)}, bf16[3,2,512,128]{3,2,1,0:T(8,128)(2,1)S(1)}, u32[]{:S(2)}, u32[]{:S(2)}) collective-permute-start(bf16[3,2,512,128]{3,2,1,0:T(8,128)(2,1)S(1)} %pad_maximum_fusion.r0.refs_11_), channel_id=1, source_target_pairs={{0,8},{8,0},{1,9},{9,1},{2,10},{10,2},{3,11},{11,3},{4,12},{12,4},... | collective-permute-start | bytes 2359304 | tf_op jit(solution)/shard_map/ppermute | solution.py:27
  47.7 10.2 %copy-start.1 = (bf16[3,2,512,128]{3,2,1,0:T(8,128)(2,1)}, bf16[3,2,512,128]{3,2,1,0:T(8,128)(2,1)S(1)}, u32[]{:S(2)}) copy-start(bf16[3,2,512,128]{3,2,1,0:T(8,128)(2,1)S(1)} %constant_dynamic-update-slice_fusion.r2.refs_12_) | copy-start | bytes 2359300
  47.7 35.8 %collective-permute-start.9 = (bf16[3,2,512,128]{3,2,1,0:T(8,128)(2,1)S(1)}, bf16[3,2,512,128]{3,2,1,0:T(8,128)(2,1)S(1)}, u32[]{:S(2)}, u32[]{:S(2)}) collective-permute-start(bf16[3,2,512,128]{3,2,1,0:T(8,128)(2,1)S(1)} %constant_dynamic-update-slice_fusion.r2.refs_12_), channel_id=1, source_target_pairs={{0,8},{8,0},{1,9},{9,1},{2,10},{10,2},{3,11},{11,3},{4,12},{12,4},... | collective-permute-start | bytes 2359304 | tf_op jit(solution)/shard_map/ppermute | solution.py:27
  47.8 17.6 %collective-permute-start = (bf16[64,4608]{1,0:T(8,128)(2,1)}, bf16[64,4608]{1,0:T(8,128)(2,1)}, u32[]{:S(2)}, u32[]{:S(2)}) collective-permute-start(bf16[64,4608]{1,0:T(8,128)(2,1)} %refs_0_.1), channel_id=1, source_target_pairs={{0,4},{4,0},{1,5},{5,1},{2,6},{6,2},{3,7},{7,3},{8,12},{12,8},{9,1... | collective-permute-start | bytes 1769480 | tf_op jit(solution)/shard_map/ppermute | solution.py:27
  50.9 28.9 %collective-permute-start.10 = (bf16[64,4608]{1,0:T(8,128)(2,1)}, bf16[64,4608]{1,0:T(8,128)(2,1)}, u32[]{:S(2)}, u32[]{:S(2)}) collective-permute-start(bf16[64,4608]{1,0:T(8,128)(2,1)} %refs_0_.1), channel_id=1, source_target_pairs={{1,0},{2,1},{3,2},{0,3},{5,4},{6,5},{7,6},{4,7},{9,8},{10,9},{11,1... | collective-permute-start | bytes 1769480 | tf_op jit(solution)/shard_map/ppermute | solution.py:27
  53.9 46.8 %collective-permute-start.11 = (bf16[64,4608]{1,0:T(8,128)(2,1)}, bf16[64,4608]{1,0:T(8,128)(2,1)}, u32[]{:S(2)}, u32[]{:S(2)}) collective-permute-start(bf16[64,4608]{1,0:T(8,128)(2,1)} %refs_0_.1), channel_id=1, source_target_pairs={{2,0},{3,1},{0,2},{1,3},{6,4},{7,5},{4,6},{5,7},{10,8},{11,9},{8,1... | collective-permute-start | bytes 1769480 | tf_op jit(solution)/shard_map/ppermute | solution.py:27
  65.3 35.3 %collective-permute-start.12 = (bf16[64,4608]{1,0:T(8,128)(2,1)}, bf16[64,4608]{1,0:T(8,128)(2,1)}, u32[]{:S(2)}, u32[]{:S(2)}) collective-permute-start(bf16[64,4608]{1,0:T(8,128)(2,1)} %refs_0_.1), channel_id=1, source_target_pairs={{3,0},{0,1},{1,2},{2,3},{7,4},{4,5},{5,6},{6,7},{11,8},{8,9},{9,10... | collective-permute-start | bytes 1769480 | tf_op jit(solution)/shard_map/ppermute | solution.py:27
  79.8 28.7 %collective-permute-start.1 = (bf16[64,4608]{1,0:T(8,128)(2,1)}, bf16[64,4608]{1,0:T(8,128)(2,1)}, u32[]{:S(2)}, u32[]{:S(2)}) collective-permute-start(bf16[64,4608]{1,0:T(8,128)(2,1)} %collective-permute-done.refs_1_.refs_4_), channel_id=1, source_target_pairs={{1,0},{2,1},{3,2},{0,3},{5,4},{6,5},{7,6},{4,7},{9,8},{10,9},{11,1... | collective-permute-start | bytes 1769480 | tf_op jit(solution)/shard_map/ppermute | solution.py:27
  83.4 25.0 %collective-permute-start.2 = (bf16[64,4608]{1,0:T(8,128)(2,1)}, bf16[64,4608]{1,0:T(8,128)(2,1)S(1)}, u32[]{:S(2)}, u32[]{:S(2)}) collective-permute-start(bf16[64,4608]{1,0:T(8,128)(2,1)} %collective-permute-done.refs_1_.refs_4_), channel_id=1, source_target_pairs={{2,0},{3,1},{0,2},{1,3},{6,4},{7,5},{4,6},{5,7},{10,8},{11,9},{8,1... | collective-permute-start | bytes 1769480 | tf_op jit(solution)/shard_map/ppermute | solution.py:27
  83.5 28.4 %collective-permute-start.3 = (bf16[64,4608]{1,0:T(8,128)(2,1)}, bf16[64,4608]{1,0:T(8,128)(2,1)S(1)}, u32[]{:S(2)}, u32[]{:S(2)}) collective-permute-start(bf16[64,4608]{1,0:T(8,128)(2,1)} %collective-permute-done.refs_1_.refs_4_), channel_id=1, source_target_pairs={{3,0},{0,1},{1,2},{2,3},{7,4},{4,5},{5,6},{6,7},{11,8},{8,9},{9,10... | collective-permute-start | bytes 1769480 | tf_op jit(solution)/shard_map/ppermute | solution.py:27
  108.4 3.4 %copy-start.6 = (bf16[64,4608]{1,0:T(8,128)(2,1)}, bf16[64,4608]{1,0:T(8,128)(2,1)S(1)}, u32[]{:S(2)}) copy-start(bf16[64,4608]{1,0:T(8,128)(2,1)S(1)} %collective-permute-done.2.refs_3_.refs_6_) | copy-start | bytes 1769476
  119.4 44.8 %collective-permute-start.21 = (bf16[128,4608]{1,0:T(8,128)(2,1)}, bf16[128,4608]{1,0:T(8,128)(2,1)S(1)}, u32[]{:S(2)}, u32[]{:S(2)}) collective-permute-start(bf16[128,4608]{1,0:T(8,128)(2,1)} %get-tuple-element.61), channel_id=1, source_target_pairs={{0,8},{8,0},{1,9},{9,1},{2,10},{10,2},{3,11},{11,3},{4,12},{12,4},... | collective-permute-start | bytes 3538952 | tf_op jit(solution)/shard_map/ppermute | solution.py:27
  147.1 16.2 %collective-permute-start.17 = (bf16[2,2,128,512]{3,2,1,0:T(8,128)(2,1)}, bf16[2,2,128,512]{3,2,1,0:T(8,128)(2,1)S(1)}, u32[]{:S(2)}, u32[]{:S(2)}) collective-permute-start(bf16[2,2,128,512]{3,2,1,0:T(8,128)(2,1)} %get-tuple-element.56), channel_id=1, source_target_pairs={{0,8},{8,0},{1,9},{9,1},{2,10},{10,2},{3,11},{11,3},{4,12},{12,4},... | collective-permute-start | bytes 1572872 | tf_op jit(solution)/shard_map/ppermute | solution.py:27
  155.5 10.6 %collective-permute-start.15 = (bf16[2,2,128,512]{3,2,1,0:T(8,128)(2,1)}, bf16[2,2,128,512]{3,2,1,0:T(8,128)(2,1)S(1)}, u32[]{:S(2)}, u32[]{:S(2)}) collective-permute-start(bf16[2,2,128,512]{3,2,1,0:T(8,128)(2,1)} %get-tuple-element.54), channel_id=1, source_target_pairs={{0,8},{8,0},{1,9},{9,1},{2,10},{10,2},{3,11},{11,3},{4,12},{12,4},... | collective-permute-start | bytes 1572872 | tf_op jit(solution)/shard_map/ppermute | solution.py:27
  156.0 7.3 %copy-start.11 = (bf16[2,2,128,512]{3,2,1,0:T(8,128)(2,1)S(1)}, bf16[2,2,128,512]{3,2,1,0:T(8,128)(2,1)}, u32[]{:S(2)}) copy-start(bf16[2,2,128,512]{3,2,1,0:T(8,128)(2,1)} %get-tuple-element.55) | copy-start | bytes 1572868
  162.4 31.3 %collective-permute-start.13 = (bf16[2,2,128,512]{3,2,1,0:T(8,128)(2,1)}, bf16[2,2,128,512]{3,2,1,0:T(8,128)(2,1)S(1)}, u32[]{:S(2)}, u32[]{:S(2)}) collective-permute-start(bf16[2,2,128,512]{3,2,1,0:T(8,128)(2,1)} %get-tuple-element.52), channel_id=1, source_target_pairs={{0,8},{8,0},{1,9},{9,1},{2,10},{10,2},{3,11},{11,3},{4,12},{12,4},... | collective-permute-start | bytes 1572872 | tf_op jit(solution)/shard_map/ppermute | solution.py:27
  163.5 9.3 %collective-permute-start.18 = (bf16[2,128,512]{2,1,0:T(8,128)(2,1)S(1)}, bf16[2,128,512]{2,1,0:T(8,128)(2,1)S(1)}, u32[]{:S(2)}, u32[]{:S(2)}) collective-permute-start(bf16[2,128,512]{2,1,0:T(8,128)(2,1)S(1)} %fusion.11), channel_id=1, source_target_pairs={{0,16},{16,0},{1,17},{17,1},{2,18},{18,2},{3,19},{19,3},{4,20},{20... | collective-permute-start | bytes 786440 | tf_op jit(solution)/shard_map/ppermute | solution.py:27
  164.2 1.8 copy-start.10
  164.6 20.8 %collective-permute-start.22 = (bf16[64,4608]{1,0:T(8,128)(2,1)S(1)}, bf16[64,4608]{1,0:T(8,128)(2,1)S(1)}, u32[]{:S(2)}, u32[]{:S(2)}) collective-permute-start(bf16[64,4608]{1,0:T(8,128)(2,1)S(1)} %fusion.1), channel_id=1, source_target_pairs={{0,16},{16,0},{1,17},{17,1},{2,18},{18,2},{3,19},{19,3},{4,20},{20... | collective-permute-start | bytes 1769480 | tf_op jit(solution)/shard_map/ppermute | solution.py:27
  167.0 27.6 %copy-start.8 = (bf16[2,2,128,512]{3,2,1,0:T(8,128)(2,1)S(1)}, bf16[2,2,128,512]{3,2,1,0:T(8,128)(2,1)}, u32[]{:S(2)}) copy-start(bf16[2,2,128,512]{3,2,1,0:T(8,128)(2,1)} %get-tuple-element.51) | copy-start | bytes 1572868
  167.0 29.6 %collective-permute-start.16 = (bf16[2,128,512]{2,1,0:T(8,128)(2,1)}, bf16[2,128,512]{2,1,0:T(8,128)(2,1)S(1)}, u32[]{:S(2)}, u32[]{:S(2)}) collective-permute-start(bf16[2,128,512]{2,1,0:T(8,128)(2,1)} %fusion.10), channel_id=1, source_target_pairs={{0,16},{16,0},{1,17},{17,1},{2,18},{18,2},{3,19},{19,3},{4,20},{20... | collective-permute-start | bytes 786440 | tf_op jit(solution)/shard_map/ppermute | solution.py:27
  173.5 23.0 %collective-permute-start.19 = (bf16[2,128,512]{2,1,0:T(8,128)(2,1)}, bf16[2,128,512]{2,1,0:T(8,128)(2,1)}, u32[]{:S(2)}, u32[]{:S(2)}) collective-permute-start(bf16[2,128,512]{2,1,0:T(8,128)(2,1)} %fusion.4), channel_id=1, source_target_pairs={{32,0},{64,32},{96,64},{128,96},{160,128},{192,160},{224,192},{33,... | collective-permute-start | bytes 786440 | tf_op jit(solution)/shard_map/ppermute | solution.py:27
  186.3 30.1 %all-to-all-start = ((bf16[8,8,4608]{2,1,0:T(8,128)(2,1)}), bf16[8,8,4608]{2,1,0:T(8,128)(2,1)S(1)}, u32[]{:S(2)}, u32[]{:S(2)}) async-start(bf16[8,8,4608]{2,1,0:T(8,128)(2,1)} %fusion.2), calls=%async_computation | async-start | bytes 1179648 | tf_op jit(solution)/shard_map/all_to_all | solution.py:477
  195.7 17.7 %copy-start.4 = (f32[2,2,128,512]{3,2,1,0:T(8,128)}, f32[2,2,128,512]{3,2,1,0:T(8,128)S(1)}, u32[]{:S(2)}) copy-start(f32[2,2,128,512]{3,2,1,0:T(8,128)S(1)} %convert_add_fusion.3.own_ref) | copy-start | bytes 3145732
  195.8 6.5 %collective-permute-start.14 = (bf16[2,128,512]{2,1,0:T(8,128)(2,1)S(1)}, bf16[2,128,512]{2,1,0:T(8,128)(2,1)S(1)}, u32[]{:S(2)}, u32[]{:S(2)}) collective-permute-start(bf16[2,128,512]{2,1,0:T(8,128)(2,1)S(1)} %fusion.9), channel_id=1, source_target_pairs={{0,16},{16,0},{1,17},{17,1},{2,18},{18,2},{3,19},{19,3},{4,20},{20... | collective-permute-start | bytes 786440 | tf_op jit(solution)/shard_map/ppermute | solution.py:27
  197.6 15.8 %collective-permute-start.20 = (bf16[2,128,512]{2,1,0:T(8,128)(2,1)S(1)}, bf16[2,128,512]{2,1,0:T(8,128)(2,1)S(1)}, u32[]{:S(2)}, u32[]{:S(2)}) collective-permute-start(bf16[2,128,512]{2,1,0:T(8,128)(2,1)S(1)} %fusion.7), channel_id=1, source_target_pairs={{32,0},{64,32},{96,64},{128,96},{160,128},{192,160},{224,192},{33,... | collective-permute-start | bytes 786440 | tf_op jit(solution)/shard_map/ppermute | solution.py:27
  202.2 11.2 %copy-start.12 = (bf16[2,128,512]{2,1,0:T(8,128)(2,1)}, bf16[2,128,512]{2,1,0:T(8,128)(2,1)S(1)}, u32[]{:S(2)}) copy-start(bf16[2,128,512]{2,1,0:T(8,128)(2,1)S(1)} %collective-permute-done.14.left_ref) | copy-start | bytes 786436
  (6 other events, 6.2 us)

commit v3 on v2

--- a/solution.py
+++ b/solution.py
@@ -18,6 +18,7 @@
 PANELS = 3
 SLOTS = 12
 TILES = 9
+PACK = 2
 NT = (((1,), (1,)), ((), ()))
 F32 = jnp.float32
 BF16 = jnp.bfloat16
@@ -52,10 +53,6 @@
 def place_of(info, i):
     rel = (i & 3) ^ info[0]
     return ((rel & 1) << 1) | (rel >> 1)
-
-
-def tile_of(info, i):
-    return jnp.clip(i - info[0], 0, TILES - 1)
 
 
 def flag_of(info, i):
@@ -90,7 +87,7 @@
         grid=(1,),
         in_specs=[whole(TOK, HD)] * 4,
         out_specs=whole(1, 2, TOK, HD),
-        compiler_params=pltpu.CompilerParams(dimension_semantics=("arbitrary",), vmem_limit_bytes=60 << 20),
+        compiler_params=pltpu.CompilerParams(dimension_semantics=("arbitrary",), vmem_limit_bytes=46 << 20),
         cost_estimate=pl.CostEstimate(flops=500_000, bytes_accessed=1_000_000, transcendentals=0),
         name="turn",
     )(keys, values, cosf, sinf)
@@ -105,10 +102,9 @@
 
 
 def forward_kernel(
-    info, q_ref, cos_ref, sin_ref, r0, r2, r1, r3, e_ref, g_ref, qr_ref, at_ref, li_ref, pt_ref, acc, pair
+    info, q_ref, cos_ref, sin_ref, r0, r2, r1, r3, eg_ref, qr_ref, at_ref, li_ref, pt_ref, acc, pair
 ):
     step = pl.program_id(0)
-    flag = flag_of(info, step)
 
     @pl.when(step == 0)
     def _():
@@ -119,40 +115,44 @@
             x = q_ref[:, h * HD : (h + 1) * HD].astype(F32)
             qr_ref[:, h * HD : (h + 1) * HD] = (x * cosine + pltpu.roll(x, HD // 2, 1) * sine).astype(BF16)
 
-    load_pair(place_of(info, step), (r0, r2, r1, r3), pair)
-
-    def body(mode):
-        key = pair[0]
-        value = jnp.concatenate([pair[1], jnp.ones((TOK, HD), BF16)], axis=1)
-        rows = HALF
-        for h in range(2):
-            for part in range(TOK // rows):
-                at = pl.ds(part * rows, rows)
-                s = tdot(qr_ref[at, h * HD : (h + 1) * HD], key)
-                th = jnp.tanh(s * (QUERY_MULTIPLIER / SOFT_CAP))
-                ex = jnp.exp2(th * (SOFT_CAP * LOG2E))
-                if mode:
-                    t = lax.broadcasted_iota(jnp.int32, (rows, TOK), 0) + part * rows
-                    u = lax.broadcasted_iota(jnp.int32, (rows, TOK), 1)
-                    ex = jnp.where(u > t if mode == 1 else u <= t, ex, 0.0)
-                eb = ex.astype(BF16)
-                e_ref[0, h, at, :] = eb
-                g_ref[0, h, at, :] = (ex * (1.0 - th * th)).astype(BF16)
-                acc[h, at, :] += ndot(eb, value)
-
-    @pl.when(flag == 1)
-    def _():
-        body(1)
-
-    @pl.when(flag == 2)
-    def _():
-        body(2)
-
-    @pl.when(flag == 3)
-    def _():
-        body(0)
-
-    @pl.when(step == SLOTS - 1)
+    def one(u, _):
+        slot = step * PACK + u
+        flag = flag_of(info, slot)
+
+        @pl.when(flag > 0)
+        def _():
+            load_pair(place_of(info, slot), (r0, r2, r1, r3), pair)
+
+        def body(mode):
+            key = pair[0]
+            value = jnp.concatenate([pair[1], jnp.ones((TOK, HD), BF16)], axis=1)
+            rows = HALF
+            for h in range(2):
+                for part in range(TOK // rows):
+                    at = pl.ds(part * rows, rows)
+                    s = tdot(qr_ref[at, h * HD : (h + 1) * HD], key)
+                    th = jnp.tanh(s * (QUERY_MULTIPLIER / SOFT_CAP))
+                    ex = jnp.exp2(th * (SOFT_CAP * LOG2E))
+                    if mode:
+                        t = lax.broadcasted_iota(jnp.int32, (rows, TOK), 0) + part * rows
+                        k = lax.broadcasted_iota(jnp.int32, (rows, TOK), 1)
+                        ex = jnp.where(k > t if mode == 1 else k <= t, ex, 0.0)
+                    eb = ex.astype(BF16)
+                    eg_ref[u, 0, h, at, :] = eb
+                    eg_ref[u, 1, h, at, :] = (ex * (1.0 - th * th)).astype(BF16)
+                    acc[h, at, :] += ndot(eb, value)
+
+        for want, mode in ((1, 1), (2, 2), (3, 0)):
+
+            @pl.when(flag == want)
+            def _():
+                body(mode)
+
+        return 0
+
+    lax.fori_loop(0, PACK, one, 0)
+
+    @pl.when(step == SLOTS // PACK - 1)
     def _():
         for h in range(2):
             inverse = 1.0 / acc[h, :, HD:]
@@ -169,12 +169,11 @@
 def forward(info, queries, cosf, sinf, panels):
     whole = lambda *shape: pl.BlockSpec(shape, lambda i, *_: (0,) * len(shape))
     sds = jax.ShapeDtypeStruct
-    eg = pl.BlockSpec((1, 2, TOK, TOK), lambda i, f: (tile_of(f, i), 0, 0, 0))
+    eg = pl.BlockSpec((PACK, 2, 2, TOK, TOK), lambda i, f: (i, 0, 0, 0, 0))
     return pl.pallas_call(
         forward_kernel,
         out_shape=(
-            sds((TILES, 2, TOK, TOK), BF16),
-            sds((TILES, 2, TOK, TOK), BF16),
+            sds((SLOTS, 2, 2, TOK, TOK), BF16),
             sds((TOK, 2 * HD), BF16),
             sds((TOK, 2 * HD), BF16),
             sds((TOK, 2 * HD), F32),
@@ -182,15 +181,14 @@
         ),
         grid_spec=pltpu.PrefetchScalarGridSpec(
             num_scalar_prefetch=1,
-            grid=(SLOTS,),
+            grid=(SLOTS // PACK,),
             in_specs=[
                 whole(TOK, 2 * HD),
                 whole(TOK, HD),
                 whole(TOK, HD),
-                *([pl.BlockSpec((1, 2, TOK, HD), lambda i, f: (i // 4, 0, 0, 0))] * 4),
+                *([pl.BlockSpec((1, 2, TOK, HD), lambda i, f: (i // (4 // PACK), 0, 0, 0))] * 4),
             ],
             out_specs=(
-                eg,
                 eg,
                 whole(TOK, 2 * HD),
                 whole(TOK, 2 * HD),
@@ -199,7 +197,7 @@
             ),
             scratch_shapes=[pltpu.VMEM((2, TOK, 2 * HD), F32), pltpu.VMEM((2, TOK, HD), BF16)],
         ),
-        compiler_params=pltpu.CompilerParams(dimension_semantics=("arbitrary",), vmem_limit_bytes=60 << 20),
+        compiler_params=pltpu.CompilerParams(dimension_semantics=("arbitrary",), vmem_limit_bytes=46 << 20),
         cost_estimate=pl.CostEstimate(flops=10_000_000_000, bytes_accessed=24_000_000, transcendentals=10_000_000),
         name="attend",
     )(info, queries, cosf, sinf, *panels)
@@ -219,9 +217,11 @@
     take = lambda n: [refs.pop(0) for _ in range(n)]
     cots = take(5) if has_cots else []
     carry_in = [] if has_cots else take(5)
-    q_ref, at_ref, li_ref, cos_ref, sin_ref = take(5)
+    q_ref, at_ref = take(2) if has_cots else (None, None)
+    li_ref = take(1)[0] if has_cots or final else None
+    cos_ref, sin_ref = take(2) if final else (None, None)
     pairs = take(4)
-    e_ref, g_ref = take(2)
+    (eg_ref,) = take(1)
     if has_prev:
         (prev_ref,) = take(1)
         if final:
@@ -230,11 +230,12 @@
     else:
         (part_ref,) = take(1)
     qg_ref = take(1)[0] if final else None
-    carry_out = [] if final else take(5)
+    carry_out = [] if final else take(5 if has_cots else 1)
     cs, do, dl, qt, dt, dq, pair = refs
     work = (do, dl, qt, dt, dq)
+    if not has_cots:
+        do, dl, qt, dt = carry_in[:4]
     step = pl.program_id(0)
-    flag = flag_of(info, base + step)
 
     @pl.when(step == 0)
     def _():
@@ -254,53 +255,59 @@
                 qt[h] = (q_ref[:, col].astype(F32) * (inverse * QUERY_MULTIPLIER)).T.astype(BF16)
             dq[...] = jnp.zeros_like(dq)
         else:
-            for a, b in zip(work, carry_in):
-                a[...] = b[...]
-
-    place = place_of(info, base + step)
-    load_pair(place, pairs, pair)
-
-    def put(dk, dv):
-        if not has_prev:
-            part_ref[0, 0] = dk
-            part_ref[0, 1] = dv
-            return
-
-        @pl.when(place < 2)
+            dq[...] = carry_in[4][...]
+
+    def one(u, _):
+        slot = base + step * PACK + u
+        place = place_of(info, slot)
+        flag = flag_of(info, slot)
+
+        def put(dk, dv):
+            if not has_prev:
+                part_ref[u, 0] = dk
+                part_ref[u, 1] = dv
+                return
+
+            @pl.when(place < 2)
+            def _():
+                keep_ref[place, 0] = dk
+                keep_ref[place, 1] = dv
+
+            @pl.when(place >= 2)
+            def _():
+                send_ref[place - 2, 0] = dk
+                send_ref[place - 2, 1] = dv
+
+        @pl.when(flag > 0)
         def _():
-            keep_ref[place, 0] = dk
-            keep_ref[place, 1] = dv
-
-        @pl.when(place >= 2)
-        def _():
-            send_ref[place - 2, 0] = dk
-            send_ref[place - 2, 1] = dv
-
-    @pl.when(flag > 0)
-    def _():
-        key = pair[0]
-        value = pair[1]
-        dk = jnp.zeros((HD, TOK), F32)
-        dv = jnp.zeros((HD, TOK), F32)
-        for h in range(2):
-            dp = tdot(do[:, h * HD : (h + 1) * HD], value)
-            x = (g_ref[0, h].astype(F32) * (dp - dl[h][:, :1])).astype(BF16)
-            dq[h] += ndot(x, key)
-            dk += ndot(qt[h], x)
-            dv += ndot(dt[h], e_ref[0, h])
+            load_pair(place, pairs, pair)
+            key = pair[0]
+            value = pair[1]
+            dk = jnp.zeros((HD, TOK), F32)
+            dv = jnp.zeros((HD, TOK), F32)
+            for h in range(2):
+                dp = tdot(do[:, h * HD : (h + 1) * HD], value)
+                x = (eg_ref[u, 1, h].astype(F32) * (dp - dl[h][:, :1])).astype(BF16)
+                dq[h] += ndot(x, key)
+                dk += ndot(qt[h], x)
+                dv += ndot(dt[h], eg_ref[u, 0, h])
+            if has_prev:
+                dk = dk + prev_ref[u, 0].astype(F32)
+                dv = dv + prev_ref[u, 1].astype(F32)
+            put(dk.astype(BF16), dv.astype(BF16))
+
         if has_prev:
-            dk = dk + prev_ref[0, 0].astype(F32)
-            dv = dv + prev_ref[0, 1].astype(F32)
-        put(dk.astype(BF16), dv.astype(BF16))
-
-    if has_prev:
-
-        @pl.when(flag == 0)
-        def _():
-            zero = jnp.zeros((HD, TOK), BF16)
-            put(zero, zero)
-
-    @pl.when(step == count - 1)
+
+            @pl.when(flag == 0)
+            def _():
+                zero = jnp.zeros((HD, TOK), BF16)
+                put(zero, zero)
+
+        return 0
+
+    lax.fori_loop(0, PACK, one, 0)
+
+    @pl.when(step == count // PACK - 1)
     def _():
         if final:
             cosine = cos_ref[...]
@@ -310,18 +317,18 @@
                 g = dq[h] * (li_ref[:, col] * QUERY_MULTIPLIER)
                 qg_ref[:, col] = g * cosine - pltpu.roll(g, HD // 2, 1) * sine
         else:
-            for a, b in zip(carry_out, work):
+            for a, b in zip(carry_out, work if has_cots else work[4:]):
                 a[...] = b[...]
 
 
-def backward(base, count, which, info, rows, panels, e, g, cots=None, w2=None, carry=None, prev=None, grad=None):
+def backward(base, count, which, info, rows, panels, eg_all, cots=None, w2=None, carry=None, prev=None, grad=None):
     has_cots, has_prev = cots is not None, prev is not None
     final = base + count == SLOTS
     sds = jax.ShapeDtypeStruct
     whole = lambda *shape: pl.BlockSpec(shape, lambda i, *_: (0,) * len(shape))
     tok = lambda width: pl.BlockSpec((HALF, width), lambda i, f: (half_of(f, which), 0))
-    eg = pl.BlockSpec((1, 2, HALF, TOK), lambda i, f: (tile_of(f, base + i), 0, half_of(f, which), 0))
-    part = pl.BlockSpec((1, 2, HD, TOK), lambda i, f: ((base + i) // 4 * 4 + place_of(f, base + i), 0, 0, 0))
+    eg = pl.BlockSpec((PACK, 2, 2, HALF, TOK), lambda i, f: (base // PACK + i, 0, 0, half_of(f, which), 0))
+    part = pl.BlockSpec((PACK, 2, HD, TOK), lambda i, f: (base // PACK + i, 0, 0, 0))
     ins, args, alias = [], [], {}
     if has_cots:
         ins += [whole(64, 4608)] * 4 + [whole(2 * HD, 4608)]
@@ -329,10 +336,12 @@
     else:
         ins += [whole(*shape) for shape, _ in CARRY]
         args += list(carry)
-    ins += [tok(2 * HD), tok(2 * HD), tok(2 * HD), tok(HD), tok(HD)]
-    args += list(rows)
-    ins += [pl.BlockSpec((1, 2, TOK, HD), lambda i, f: ((base + i) // 4, 0, 0, 0))] * 4 + [eg, eg]
-    args += [*panels, e, g]
+    wanted = [has_cots, has_cots, has_cots or final, final, final]
+    widths = [2 * HD, 2 * HD, 2 * HD, HD, HD]
+    ins += [tok(n) for n, use in zip(widths, wanted) if use]
+    args += [a for a, use in zip(rows, wanted) if use]
+    ins += [pl.BlockSpec((1, 2, TOK, HD), lambda i, f: (base // 4 + i // (4 // PACK), 0, 0, 0))] * 4 + [eg]
+    args += [*panels, eg_all]
     if has_prev:
         ins += [part]
         args += [prev]
@@ -349,8 +358,9 @@
         outs += [tok(2 * HD)]
         shapes += [sds((TOK, 2 * HD), F32)]
     else:
-        outs += [whole(*shape) for shape, _ in CARRY]
-        shapes += [sds(*c) for c in CARRY]
+        left = CARRY if has_cots else CARRY[4:]
+        outs += [whole(*shape) for shape, _ in left]
+        shapes += [sds(*c) for c in left]
 
     def kernel(*refs):
         backward_kernel(base, count, has_cots, has_prev, final, *refs)
@@ -360,7 +370,7 @@
         out_shape=shapes,
         grid_spec=pltpu.PrefetchScalarGridSpec(
             num_scalar_prefetch=1,
-            grid=(count,),
+            grid=(count // PACK,),
             in_specs=ins,
             out_specs=outs,
             scratch_shapes=[
@@ -369,7 +379,7 @@
                 pltpu.VMEM((2, TOK, HD), BF16),
             ],
         ),
-        compiler_params=pltpu.CompilerParams(dimension_semantics=("arbitrary",), vmem_limit_bytes=60 << 20),
+        compiler_params=pltpu.CompilerParams(dimension_semantics=("arbitrary",), vmem_limit_bytes=(60 if has_prev else 46) << 20),
         input_output_aliases=alias,
         cost_estimate=pl.CostEstimate(flops=700_000_000 * count, bytes_accessed=2_000_000 * count, transcendentals=0),
     )(info, *args)
@@ -404,7 +414,7 @@
             out_specs=(block(HD), block(HD)),
             scratch_shapes=[pltpu.VMEM((TOK, chunk), BF16)],
         ),
-        compiler_params=pltpu.CompilerParams(dimension_semantics=("arbitrary",), vmem_limit_bytes=60 << 20),
+        compiler_params=pltpu.CompilerParams(dimension_semantics=("arbitrary",), vmem_limit_bytes=46 << 20),
         cost_estimate=pl.CostEstimate(flops=1_300_000_000, bytes_accessed=9_000_000, transcendentals=0),
         name="weigh",
     )(where, *cots, attn_t)
@@ -426,7 +436,7 @@
         grid=(1,),
         in_specs=[whole(1, 2, HD, TOK), whole(2, HD, TOK), whole(2, HD, TOK), whole(TOK, HD), whole(TOK, HD)],
         out_specs=(whole(TOK, HD), whole(TOK, HD)),
-        compiler_params=pltpu.CompilerParams(dimension_semantics=("arbitrary",), vmem_limit_bytes=60 << 20),
+        compiler_params=pltpu.CompilerParams(dimension_semantics=("arbitrary",), vmem_limit_bytes=46 << 20),
         cost_estimate=pl.CostEstimate(flops=500_000, bytes_accessed=2_000_000, transcendentals=0),
         name="settle",
     )(both, left, down, cosf, sinf)
@@ -463,9 +473,9 @@
 
     w2 = jnp.transpose(out_weight, (1, 0, 2)).reshape(2 * HD, 4608)
 
-    e, g, qr, attn, linv, attn_t = forward(info, queries, cosf, sinf, panels)
+    eg, qr, attn, linv, attn_t = forward(info, queries, cosf, sinf, panels)
     rows = (qr, attn, linv, cosf, sinf)
-    prev, half = backward(0, SLOTS, 1, info, rows, panels, e, g, cots=near, w2=w2)
+    prev, half = backward(0, SLOTS, 1, info, rows, panels, eg, cots=near, w2=w2)
 
     wkeep, wsend = weight(info, near + far, attn_t)
     wgot = swap(wsend, "c")
@@ -481,11 +491,12 @@
     carry = None
     for p in range(PANELS):
         out = backward(
-            p * 4, 4, 2, info, rows, panels, e, g,
+            p * 4, 4, 2, info, rows, panels, eg,
             cots=far if p == 0 else None, w2=w2 if p == 0 else None, carry=carry, prev=prev,
             grad=half if p == PANELS - 1 else None,
         )
-        keep, send, *carry = out
+        keep, send, *after = out
+        carry = after if len(after) != 1 or p == PANELS - 1 else [*carry[:4], *after]
         got = swap(send, "c")
         both = keep.astype(F32) + got.astype(F32)
         give = both[1].astype(BF16)

time: 218 us -> 209 us (0.959)
  Pallas kernels: 69.2 us -> 56.9 us
  waiting for transfers between devices: 89.9 us -> 93.9 us
    pallas_call x4, Pallas kernels: 42.1 us -> 36.9 us  [backward(): pl.pallas_call(kernel, out_shape=shapes, grid_spec=pltpu.PrefetchScalarGr...]
    ppermute x23, waiting for transfers between devices: 89.9 us -> 93.9 us  [permute(): return lax.ppermute(x, axis, pairs)]
    pallas_call x1, Pallas kernels: 16.1 us -> 13.2 us  [forward(): pl.pallas_call(forward_kernel, out_shape=(sds((SLOTS, 2, 2, TOK, TOK), BF...]
  transfers between devices with their start and end apart: 24 -> 24, of which waited for: 12 -> 12; matrix products, arithmetic and copies ran while one was open for 5% -> 4% of each run, Pallas kernels for 28% -> 25%
where the time goes in v3:
time: 209 us; the launch traced here: 208 us
  waiting for transfers between devices  93.9 us (45%)
  Pallas kernels  56.9 us (27%)
  starting transfers between devices  40.1 us (19%)
  local copies, waits for them, and re-layouts  9.07 us (4%)
  other arithmetic  6.68 us (3%)
    ppermute x23, waiting for transfers between devices, permute(): return lax.ppermute(x, axis, pairs)  93.9 us
    pallas_call x4, Pallas kernels, backward(): pl.pallas_call(kernel, out_shape=shapes, grid_spec=pltpu.PrefetchScalarGr...  36.9 us
    ppermute x23, starting transfers between devices, permute(): return lax.ppermute(x, axis, pairs)  32.6 us
    pallas_call x1, Pallas kernels, forward(): pl.pallas_call(forward_kernel, out_shape=(sds((SLOTS, 2, 2, TOK, TOK), BF...  13.2 us
    all_to_all x1, starting transfers between devices, local(): wz = lax.all_to_all(wz, 'z', 0, 0, tiled=True)  7.51 us
    pallas_call x1, Pallas kernels, weight(): pl.pallas_call(weight_kernel, out_shape=(sds((HD, 4608), F32), sds((HD, 4...  5.67 us
  transfers between devices with their start and end apart: 24, of which 12 were waited for; matrix products, arithmetic and copies ran while one was open for 4% of the time, Pallas kernels for 25%

profile of v3, /device:TPU:96, one launch (start us, length us, event | category | flops | bytes accessed | tf_op | source)
XLA Modules:
  0.0 207.7 jit_solution(4624932319605399095)
XLA Ops:
  0.7 1.7 fusion.8
  4.4 5.5 %collective-permute-start.4 = (bf16[1,2,512,128]{3,2,1,0:T(8,128)(2,1)S(1)}, bf16[1,2,512,128]{3,2,1,0:T(8,128)(2,1)S(1)}, u32[]{:S(2)}, u32[]{:S(2)}) collective-permute-start(bf16[1,2,512,128]{3,2,1,0:T(8,128)(2,1)S(1)} %turn.1), channel_id=1, source_target_pairs={{0,64},{32,96},{64,128},{96,160},{128,192},{160,224},{1,65},{33,97... | collective-permute-start | bytes 786440 | tf_op jit(solution)/shard_map/ppermute | solution.py:28
  9.9 2.9 %collective-permute-start.5 = (bf16[1,2,512,128]{3,2,1,0:T(8,128)(2,1)S(1)}, bf16[1,2,512,128]{3,2,1,0:T(8,128)(2,1)S(1)}, u32[]{:S(2)}, u32[]{:S(2)}) collective-permute-start(bf16[1,2,512,128]{3,2,1,0:T(8,128)(2,1)S(1)} %turn.1), channel_id=1, source_target_pairs={{0,32},{32,64},{64,96},{96,128},{128,160},{160,192},{192,224},{1,3... | collective-permute-start | bytes 786440 | tf_op jit(solution)/shard_map/ppermute | solution.py:28
  12.9 7.7 %collective-permute-done.4 = bf16[1,2,512,128]{3,2,1,0:T(8,128)(2,1)S(1)} collective-permute-done((bf16[1,2,512,128]{3,2,1,0:T(8,128)(2,1)S(1)}, bf16[1,2,512,128]{3,2,1,0:T(8,128)(2,1)S(1)}, u32[]{:S(2)}, u32[]{:S(2)}) %collective-permute-start.4) | collective-permute-done | bytes 262176 | tf_op jit(solution)/shard_map/ppermute | solution.py:28
  20.6 7.5 %collective-permute-done.5 = bf16[1,2,512,128]{3,2,1,0:T(8,128)(2,1)S(1)} collective-permute-done((bf16[1,2,512,128]{3,2,1,0:T(8,128)(2,1)S(1)}, bf16[1,2,512,128]{3,2,1,0:T(8,128)(2,1)S(1)}, u32[]{:S(2)}, u32[]{:S(2)}) %collective-permute-start.5) | collective-permute-done | bytes 262176 | tf_op jit(solution)/shard_map/ppermute | solution.py:28
  28.2 1.6 collective-permute-start.6
  30.5 12.6 %collective-permute-done.6 = bf16[2,2,512,128]{3,2,1,0:T(8,128)(2,1)S(1)} collective-permute-done((bf16[2,2,512,128]{3,2,1,0:T(8,128)(2,1)S(1)}, bf16[2,2,512,128]{3,2,1,0:T(8,128)(2,1)S(1)}, u32[]{:S(2)}, u32[]{:S(2)}) %collective-permute-start.6) | collective-permute-done | bytes 524320 | tf_op jit(solution)/shard_map/ppermute | solution.py:28
  43.1 3.6 %collective-permute-done.7 = bf16[1,2,512,128]{3,2,1,0:T(8,128)(2,1)S(1)} collective-permute-done((bf16[1,2,512,128]{3,2,1,0:T(8,128)(2,1)S(1)}, bf16[1,2,512,128]{3,2,1,0:T(8,128)(2,1)S(1)}, u32[]{:S(2)}, u32[]{:S(2)}) %collective-permute-start.7) | collective-permute-done | bytes 262176 | tf_op jit(solution)/shard_map/ppermute | solution.py:28
  46.9 3.1 %collective-permute-start = (bf16[64,4608]{1,0:T(8,128)(2,1)}, bf16[64,4608]{1,0:T(8,128)(2,1)}, u32[]{:S(2)}, u32[]{:S(2)}) collective-permute-start(bf16[64,4608]{1,0:T(8,128)(2,1)} %refs_0_.1), channel_id=1, source_target_pairs={{0,4},{4,0},{1,5},{5,1},{2,6},{6,2},{3,7},{7,3},{8,12},{12,8},{9,1... | collective-permute-start | bytes 1769480 | tf_op jit(solution)/shard_map/ppermute | solution.py:28
  50.0 3.0 %collective-permute-start.10 = (bf16[64,4608]{1,0:T(8,128)(2,1)}, bf16[64,4608]{1,0:T(8,128)(2,1)}, u32[]{:S(2)}, u32[]{:S(2)}) collective-permute-start(bf16[64,4608]{1,0:T(8,128)(2,1)} %refs_0_.1), channel_id=1, source_target_pairs={{1,0},{2,1},{3,2},{0,3},{5,4},{6,5},{7,6},{4,7},{9,8},{10,9},{11,1... | collective-permute-start | bytes 1769480 | tf_op jit(solution)/shard_map/ppermute | solution.py:28
  53.6 3.3 %copy.12 = bf16[2,128,4608]{2,1,0:T(8,128)(2,1)} copy(bf16[2,128,4608]{2,0,1:T(2,128)(2,1)} %bitcast.42) | data formatting | bytes 4718592 | tf_op jit(solution)/shard_map/transpose | solution.py:474
  57.0 7.4 %collective-permute-done.refs_1_.refs_4_ = bf16[64,4608]{1,0:T(8,128)(2,1)} collective-permute-done((bf16[64,4608]{1,0:T(8,128)(2,1)}, bf16[64,4608]{1,0:T(8,128)(2,1)}, u32[]{:S(2)}, u32[]{:S(2)}) %collective-permute-start) | collective-permute-done | bytes 589856 | tf_op jit(solution)/shard_map/ppermute | solution.py:28
  64.4 1.6 collective-permute-start.12
  66.0 12.8 %collective-permute-done.10.refs_2_.refs_1_ = bf16[64,4608]{1,0:T(8,128)(2,1)} collective-permute-done((bf16[64,4608]{1,0:T(8,128)(2,1)}, bf16[64,4608]{1,0:T(8,128)(2,1)}, u32[]{:S(2)}, u32[]{:S(2)}) %collective-permute-start.10) | collective-permute-done | bytes 589856 | tf_op jit(solution)/shard_map/ppermute | solution.py:28
  78.8 3.7 %collective-permute-start.1 = (bf16[64,4608]{1,0:T(8,128)(2,1)}, bf16[64,4608]{1,0:T(8,128)(2,1)S(1)}, u32[]{:S(2)}, u32[]{:S(2)}) collective-permute-start(bf16[64,4608]{1,0:T(8,128)(2,1)} %collective-permute-done.refs_1_.refs_4_), channel_id=1, source_target_pairs={{1,0},{2,1},{3,2},{0,3},{5,4},{6,5},{7,6},{4,7},{9,8},{10,9},{11,1... | collective-permute-start | bytes 1769480 | tf_op jit(solution)/shard_map/ppermute | solution.py:28
  85.4 13.2 %attend.1 = (bf16[12,2,2,512,512]{4,3,2,1,0:T(8,128)(2,1)}, bf16[512,256]{1,0:T(8,128)(2,1)S(1)}, bf16[512,256]{1,0:T(8,128)(2,1)S(1)}, f32[512,256]{1,0:T(8,128)S(1)}, bf16[256,512]{1,0:T(8,128)(2,1)S(1)}) custom-call(s32[5]{0:T(128)S(1)} %stack.23.info.refs_0_.where, bf16[512,256]{1,0:T(8,128)(2,1)S(1)} %copy-done.19, f32[512,128]{1,0:T(8,128)S(1)} %copy-done.7, ...), custom_call_target="tpu_custom_call" | custom-call | flops 10000000000 | bytes 24000000 | tf_op jit(solution)/shard_map/attend/pallas_call | solution.py:173
  98.6 8.9 %collective-permute-done.1.refs_2_.refs_5_ = bf16[64,4608]{1,0:T(8,128)(2,1)S(1)} collective-permute-done((bf16[64,4608]{1,0:T(8,128)(2,1)}, bf16[64,4608]{1,0:T(8,128)(2,1)S(1)}, u32[]{:S(2)}, u32[]{:S(2)}) %collective-permute-start.1) | collective-permute-done | bytes 589856 | tf_op jit(solution)/shard_map/ppermute | solution.py:28
  107.5 3.6 %collective-permute-done.3.refs_4_.refs_7_ = bf16[64,4608]{1,0:T(8,128)(2,1)S(1)} collective-permute-done((bf16[64,4608]{1,0:T(8,128)(2,1)}, bf16[64,4608]{1,0:T(8,128)(2,1)S(1)}, u32[]{:S(2)}, u32[]{:S(2)}) %collective-permute-start.3) | collective-permute-done | bytes 589856 | tf_op jit(solution)/shard_map/ppermute | solution.py:28
  111.1 5.7 %weigh.1 = (f32[128,4608]{1,0:T(8,128)}, bf16[128,4608]{1,0:T(8,128)(2,1)}) custom-call(s32[5]{0:T(128)S(1)} %stack.23.info.refs_0_.where, bf16[64,4608]{1,0:T(8,128)(2,1)} %refs_0_.1, bf16[64,4608]{1,0:T(8,128)(2,1)} %collective-permute-done.10.refs_2_.refs_1_, bf16[64,4608]{1,0:T(8,128)(2,1)} %collective-permute-done.11.refs_3_.refs_2_, ...), custom_call_target="tpu_custom_call" | custom-call | flops 1300000000 | bytes 9000000 | tf_op jit(solution)/shard_map/weigh/pallas_call | solution.py:407
  117.0 14.0 %shard_map.102 = (bf16[12,2,128,512]{3,2,1,0:T(8,128)(2,1)}, f32[512,256]{1,0:T(8,128)}) custom-call(s32[5]{0:T(128)S(1)} %stack.23.info.refs_0_.where, bf16[64,4608]{1,0:T(8,128)(2,1)} %refs_0_.1, bf16[64,4608]{1,0:T(8,128)(2,1)} %collective-permute-done.10.refs_2_.refs_1_, bf16[64,4608]{1,0:T(8,128)(2,1)} %collective-permute-done.11.refs_3_.refs_2_, ...), custom_call_target="tpu_custom_call" | custom-call | flops 8400000000 | bytes 24000000 | tf_op jit(solution)/shard_map/pallas_call | solution.py:368
  131.0 10.1 %shard_map.103 = (bf16[2,2,128,512]{3,2,1,0:T(8,128)(2,1)}, bf16[2,2,128,512]{3,2,1,0:T(8,128)(2,1)}, bf16[256,256]{1,0:T(8,128)(2,1)}, f32[2,256,128]{2,1,0:T(8...) custom-call(s32[5]{0:T(128)} %copy-done.18, ...), custom_call_target="tpu_custom_call" | custom-call | flops 2800000000 | bytes 8000000 | tf_op jit(solution)/shard_map/pallas_call | solution.py:368
  141.2 7.3 %shard_map.104 = (bf16[2,2,128,512]{3,2,1,0:T(8,128)(2,1)}, bf16[2,2,128,512]{3,2,1,0:T(8,128)(2,1)}, f32[2,256,128]{2,1,0:T(8,128)}) custom-call(s32[5]{0:T(128)} %copy-done.18, bf16[256,256]{1,0:T(8,128)(2,1)} %get-tuple-element.33.refs_1_, f32[2,256,128]{2,1,0:T(8,128)} %get-tuple-element.34.refs_2_, bf16[2,128,256]{2,1,0:T(8,128)(2,1)} %get-tuple-element.35.refs_3_, ...), custom_call_target="tpu_custom_call" | custom-call | flops 2800000000 | bytes 8000000 | tf_op jit(solution)/shard_map/pallas_call | solution.py:368
  149.0 5.5 %shard_map.105 = (bf16[2,2,128,512]{3,2,1,0:T(8,128)(2,1)}, bf16[2,2,128,512]{3,2,1,0:T(8,128)(2,1)}, f32[512,256]{1,0:T(8,128)}) custom-call(s32[5]{0:T(128)} %copy-done.18, bf16[256,256]{1,0:T(8,128)(2,1)} %get-tuple-element.33.refs_1_, f32[2,256,128]{2,1,0:T(8,128)} %get-tuple-element.34.refs_2_, ...), custom_call_target="tpu_custom_call", output_to_operand_aliasing={{2}: (15, {})} | custom-call | flops 2800000000 | bytes 8000000 | tf_op jit(solution)/shard_map/pallas_call | solution.py:368
  156.2 1.6 convert_add_fusion
  157.9 1.8 collective-permute-start.22
  160.9 4.2 %collective-permute-done.18 = bf16[2,128,512]{2,1,0:T(8,128)(2,1)S(1)} collective-permute-done((bf16[2,128,512]{2,1,0:T(8,128)(2,1)S(1)}, bf16[2,128,512]{2,1,0:T(8,128)(2,1)S(1)}, u32[]{:S(2)}, u32[]{:S(2)}) %collective-permute-start.18) | collective-permute-done | bytes 262176 | tf_op jit(solution)/shard_map/ppermute | solution.py:28
  165.9 1.9 collective-permute-start.19
  167.8 9.9 %collective-permute-done.22 = bf16[64,4608]{1,0:T(8,128)(2,1)S(1)} collective-permute-done((bf16[64,4608]{1,0:T(8,128)(2,1)S(1)}, bf16[64,4608]{1,0:T(8,128)(2,1)S(1)}, u32[]{:S(2)}, u32[]{:S(2)}) %collective-permute-start.22) | collective-permute-done | bytes 589856 | tf_op jit(solution)/shard_map/ppermute | solution.py:28
  178.7 7.5 %all-to-all-start = ((bf16[8,8,4608]{2,1,0:T(8,128)(2,1)}), bf16[8,8,4608]{2,1,0:T(8,128)(2,1)S(1)}, u32[]{:S(2)}, u32[]{:S(2)}) async-start(bf16[8,8,4608]{2,1,0:T(8,128)(2,1)} %fusion.2), calls=%async_computation | async-start | bytes 1179648 | tf_op jit(solution)/shard_map/all_to_all | solution.py:487
  187.8 2.5 %collective-permute-start.20 = (bf16[2,128,512]{2,1,0:T(8,128)(2,1)S(1)}, bf16[2,128,512]{2,1,0:T(8,128)(2,1)S(1)}, u32[]{:S(2)}, u32[]{:S(2)}) collective-permute-start(bf16[2,128,512]{2,1,0:T(8,128)(2,1)S(1)} %fusion.7), channel_id=1, source_target_pairs={{32,0},{64,32},{96,64},{128,96},{160,128},{192,160},{224,192},{33,... | collective-permute-start | bytes 786440 | tf_op jit(solution)/shard_map/ppermute | solution.py:28
  190.3 2.6 %collective-permute-done.14.left_ref = bf16[2,128,512]{2,1,0:T(8,128)(2,1)S(1)} collective-permute-done((bf16[2,128,512]{2,1,0:T(8,128)(2,1)S(1)}, bf16[2,128,512]{2,1,0:T(8,128)(2,1)S(1)}, u32[]{:S(2)}, u32[]{:S(2)}) %collective-permute-start.14) | collective-permute-done | bytes 262176 | tf_op jit(solution)/shard_map/ppermute | solution.py:28
  192.9 13.0 %collective-permute-done.20.down_ref = bf16[2,128,512]{2,1,0:T(8,128)(2,1)S(1)} collective-permute-done((bf16[2,128,512]{2,1,0:T(8,128)(2,1)S(1)}, bf16[2,128,512]{2,1,0:T(8,128)(2,1)S(1)}, u32[]{:S(2)}, u32[]{:S(2)}) %collective-permute-start.20) | collective-permute-done | bytes 262176 | tf_op jit(solution)/shard_map/ppermute | solution.py:28
  (93 shorter events, 15.4 us)
Async XLA Ops:
  2.3 40.8 %copy-start.6 = (f32[512,128]{1,0:T(8,128)}, f32[512,128]{1,0:T(8,128)S(1)}, u32[]{:S(2)}) copy-start(f32[512,128]{1,0:T(8,128)S(1)} %get-tuple-element.53.cos_ref.refs_9_.refs_7_) | copy-start | bytes 786436
  2.3 114.6 %copy-start.4 = (f32[512,128]{1,0:T(8,128)}, f32[512,128]{1,0:T(8,128)S(1)}, u32[]{:S(2)}) copy-start(f32[512,128]{1,0:T(8,128)S(1)} %get-tuple-element.52.sin_ref.refs_10_.refs_8_) | copy-start | bytes 786436
  4.4 16.1 %collective-permute-start.4 = (bf16[1,2,512,128]{3,2,1,0:T(8,128)(2,1)S(1)}, bf16[1,2,512,128]{3,2,1,0:T(8,128)(2,1)S(1)}, u32[]{:S(2)}, u32[]{:S(2)}) collective-permute-start(bf16[1,2,512,128]{3,2,1,0:T(8,128)(2,1)S(1)} %turn.1), channel_id=1, source_target_pairs={{0,64},{32,96},{64,128},{96,160},{128,192},{160,224},{1,65},{33,97... | collective-permute-start | bytes 786440 | tf_op jit(solution)/shard_map/ppermute | solution.py:28
  9.9 18.2 %collective-permute-start.5 = (bf16[1,2,512,128]{3,2,1,0:T(8,128)(2,1)S(1)}, bf16[1,2,512,128]{3,2,1,0:T(8,128)(2,1)S(1)}, u32[]{:S(2)}, u32[]{:S(2)}) collective-permute-start(bf16[1,2,512,128]{3,2,1,0:T(8,128)(2,1)S(1)} %turn.1), channel_id=1, source_target_pairs={{0,32},{32,64},{64,96},{96,128},{128,160},{160,192},{192,224},{1,3... | collective-permute-start | bytes 786440 | tf_op jit(solution)/shard_map/ppermute | solution.py:28
  28.2 14.9 %collective-permute-start.6 = (bf16[2,2,512,128]{3,2,1,0:T(8,128)(2,1)S(1)}, bf16[2,2,512,128]{3,2,1,0:T(8,128)(2,1)S(1)}, u32[]{:S(2)}, u32[]{:S(2)}) collective-permute-start(bf16[2,2,512,128]{3,2,1,0:T(8,128)(2,1)S(1)} %pad_maximum_fusion.1), channel_id=1, source_target_pairs={{0,16},{16,0},{1,17},{17,1},{2,18},{18,2},{3,19},{19,3},{4,20},{20... | collective-permute-start | bytes 1572872 | tf_op jit(solution)/shard_map/ppermute | solution.py:28
  29.8 17.0 %collective-permute-start.7 = (bf16[1,2,512,128]{3,2,1,0:T(8,128)(2,1)S(1)}, bf16[1,2,512,128]{3,2,1,0:T(8,128)(2,1)S(1)}, u32[]{:S(2)}, u32[]{:S(2)}) collective-permute-start(bf16[1,2,512,128]{3,2,1,0:T(8,128)(2,1)S(1)} %turn.1), channel_id=1, source_target_pairs={{0,16},{16,0},{1,17},{17,1},{2,18},{18,2},{3,19},{19,3},{4,20},{20... | collective-permute-start | bytes 786440 | tf_op jit(solution)/shard_map/ppermute | solution.py:28
  30.4 86.5 %copy-start = (bf16[3,2,512,128]{3,2,1,0:T(8,128)(2,1)}, bf16[3,2,512,128]{3,2,1,0:T(8,128)(2,1)S(1)}, u32[]{:S(2)}) copy-start(bf16[3,2,512,128]{3,2,1,0:T(8,128)(2,1)S(1)} %pad_maximum_fusion.r0.refs_11_.refs_9_.refs_6_) | copy-start | bytes 2359300
  30.4 52.1 %collective-permute-start.8 = (bf16[3,2,512,128]{3,2,1,0:T(8,128)(2,1)S(1)}, bf16[3,2,512,128]{3,2,1,0:T(8,128)(2,1)S(1)}, u32[]{:S(2)}, u32[]{:S(2)}) collective-permute-start(bf16[3,2,512,128]{3,2,1,0:T(8,128)(2,1)S(1)} %pad_maximum_fusion.r0.refs_11_.refs_9_.refs_6_), channel_id=1, source_target_pairs={{0,8},{8,0},{1,9},{9,1},{2,10},{10,2},{3,11},{11,3},{4,12},{12,4},... | collective-permute-start | bytes 2359304 | tf_op jit(solution)/shard_map/ppermute | solution.py:28
  46.8 70.2 %copy-start.1 = (bf16[3,2,512,128]{3,2,1,0:T(8,128)(2,1)}, bf16[3,2,512,128]{3,2,1,0:T(8,128)(2,1)S(1)}, u32[]{:S(2)}) copy-start(bf16[3,2,512,128]{3,2,1,0:T(8,128)(2,1)S(1)} %constant_dynamic-update-slice_fusion.r2.refs_12_.refs_10_.refs_7_) | copy-start | bytes 2359300
  46.8 35.8 %collective-permute-start.9 = (bf16[3,2,512,128]{3,2,1,0:T(8,128)(2,1)S(1)}, bf16[3,2,512,128]{3,2,1,0:T(8,128)(2,1)S(1)}, u32[]{:S(2)}, u32[]{:S(2)}) collective-permute-start(bf16[3,2,512,128]{3,2,1,0:T(8,128)(2,1)S(1)} %constant_dynamic-update-slice_fusion.r2.refs_12_.refs_10_.refs_7_), channel_id=1, source_target_pairs={{0,8},{8,0},{1,9},{9,1},{2,10},{10,2},{3,11},{11,3},{4,12},{12,4},... | collective-permute-start | bytes 2359304 | tf_op jit(solution)/shard_map/ppermute | solution.py:28
  46.9 17.6 %collective-permute-start = (bf16[64,4608]{1,0:T(8,128)(2,1)}, bf16[64,4608]{1,0:T(8,128)(2,1)}, u32[]{:S(2)}, u32[]{:S(2)}) collective-permute-start(bf16[64,4608]{1,0:T(8,128)(2,1)} %refs_0_.1), channel_id=1, source_target_pairs={{0,4},{4,0},{1,5},{5,1},{2,6},{6,2},{3,7},{7,3},{8,12},{12,8},{9,1... | collective-permute-start | bytes 1769480 | tf_op jit(solution)/shard_map/ppermute | solution.py:28
  50.0 28.9 %collective-permute-start.10 = (bf16[64,4608]{1,0:T(8,128)(2,1)}, bf16[64,4608]{1,0:T(8,128)(2,1)}, u32[]{:S(2)}, u32[]{:S(2)}) collective-permute-start(bf16[64,4608]{1,0:T(8,128)(2,1)} %refs_0_.1), channel_id=1, source_target_pairs={{1,0},{2,1},{3,2},{0,3},{5,4},{6,5},{7,6},{4,7},{9,8},{10,9},{11,1... | collective-permute-start | bytes 1769480 | tf_op jit(solution)/shard_map/ppermute | solution.py:28
  53.0 45.6 %collective-permute-start.11 = (bf16[64,4608]{1,0:T(8,128)(2,1)}, bf16[64,4608]{1,0:T(8,128)(2,1)}, u32[]{:S(2)}, u32[]{:S(2)}) collective-permute-start(bf16[64,4608]{1,0:T(8,128)(2,1)} %refs_0_.1), channel_id=1, source_target_pairs={{2,0},{3,1},{0,2},{1,3},{6,4},{7,5},{4,6},{5,7},{10,8},{11,9},{8,1... | collective-permute-start | bytes 1769480 | tf_op jit(solution)/shard_map/ppermute | solution.py:28
  57.0 59.9 %copy-start.18 = (s32[5]{0:T(128)}, s32[5]{0:T(128)S(1)}, u32[]{:S(2)}) copy-start(s32[5]{0:T(128)S(1)} %stack.23.info.refs_0_.where) | copy-start | bytes 64
  64.4 34.2 %collective-permute-start.12 = (bf16[64,4608]{1,0:T(8,128)(2,1)}, bf16[64,4608]{1,0:T(8,128)(2,1)S(1)}, u32[]{:S(2)}, u32[]{:S(2)}) collective-permute-start(bf16[64,4608]{1,0:T(8,128)(2,1)} %refs_0_.1), channel_id=1, source_target_pairs={{3,0},{0,1},{1,2},{2,3},{7,4},{4,5},{5,6},{6,7},{11,8},{8,9},{9,10... | collective-permute-start | bytes 1769480 | tf_op jit(solution)/shard_map/ppermute | solution.py:28
  78.8 28.7 %collective-permute-start.1 = (bf16[64,4608]{1,0:T(8,128)(2,1)}, bf16[64,4608]{1,0:T(8,128)(2,1)S(1)}, u32[]{:S(2)}, u32[]{:S(2)}) collective-permute-start(bf16[64,4608]{1,0:T(8,128)(2,1)} %collective-permute-done.refs_1_.refs_4_), channel_id=1, source_target_pairs={{1,0},{2,1},{3,2},{0,3},{5,4},{6,5},{7,6},{4,7},{9,8},{10,9},{11,1... | collective-permute-start | bytes 1769480 | tf_op jit(solution)/shard_map/ppermute | solution.py:28
  82.5 34.4 %copy-start.2 = (bf16[3,2,512,128]{3,2,1,0:T(8,128)(2,1)}, bf16[3,2,512,128]{3,2,1,0:T(8,128)(2,1)S(1)}, u32[]{:S(2)}) copy-start(bf16[3,2,512,128]{3,2,1,0:T(8,128)(2,1)S(1)} %collective-permute-done.8.r1.refs_13_.refs_11_.refs_8_) | copy-start | bytes 2359300
  82.5 25.0 %collective-permute-start.2 = (bf16[64,4608]{1,0:T(8,128)(2,1)}, bf16[64,4608]{1,0:T(8,128)(2,1)S(1)}, u32[]{:S(2)}, u32[]{:S(2)}) collective-permute-start(bf16[64,4608]{1,0:T(8,128)(2,1)} %collective-permute-done.refs_1_.refs_4_), channel_id=1, source_target_pairs={{2,0},{3,1},{0,2},{1,3},{6,4},{7,5},{4,6},{5,7},{10,8},{11,9},{8,1... | collective-permute-start | bytes 1769480 | tf_op jit(solution)/shard_map/ppermute | solution.py:28
  82.6 34.4 %copy-start.3 = (bf16[3,2,512,128]{3,2,1,0:T(8,128)(2,1)}, bf16[3,2,512,128]{3,2,1,0:T(8,128)(2,1)S(1)}, u32[]{:S(2)}) copy-start(bf16[3,2,512,128]{3,2,1,0:T(8,128)(2,1)S(1)} %collective-permute-done.9.r3.refs_14_.refs_12_.refs_9_) | copy-start | bytes 2359300
  82.6 28.5 %collective-permute-start.3 = (bf16[64,4608]{1,0:T(8,128)(2,1)}, bf16[64,4608]{1,0:T(8,128)(2,1)S(1)}, u32[]{:S(2)}, u32[]{:S(2)}) collective-permute-start(bf16[64,4608]{1,0:T(8,128)(2,1)} %collective-permute-done.refs_1_.refs_4_), channel_id=1, source_target_pairs={{3,0},{0,1},{1,2},{2,3},{7,4},{4,5},{5,6},{6,7},{11,8},{8,9},{9,10... | collective-permute-start | bytes 1769480 | tf_op jit(solution)/shard_map/ppermute | solution.py:28
  116.8 39.4 %collective-permute-start.21 = (bf16[128,4608]{1,0:T(8,128)(2,1)}, bf16[128,4608]{1,0:T(8,128)(2,1)}, u32[]{:S(2)}, u32[]{:S(2)}) collective-permute-start(bf16[128,4608]{1,0:T(8,128)(2,1)} %get-tuple-element.51), channel_id=1, source_target_pairs={{0,8},{8,0},{1,9},{9,1},{2,10},{10,2},{3,11},{11,3},{4,12},{12,4},... | collective-permute-start | bytes 3538952 | tf_op jit(solution)/shard_map/ppermute | solution.py:28
  141.1 14.3 %collective-permute-start.17 = (bf16[2,2,128,512]{3,2,1,0:T(8,128)(2,1)}, bf16[2,2,128,512]{3,2,1,0:T(8,128)(2,1)S(1)}, u32[]{:S(2)}, u32[]{:S(2)}) collective-permute-start(bf16[2,2,128,512]{3,2,1,0:T(8,128)(2,1)} %get-tuple-element.46), channel_id=1, source_target_pairs={{0,8},{8,0},{1,9},{9,1},{2,10},{10,2},{3,11},{11,3},{4,12},{12,4},... | collective-permute-start | bytes 1572872 | tf_op jit(solution)/shard_map/ppermute | solution.py:28
  148.5 11.2 %collective-permute-start.15 = (bf16[2,2,128,512]{3,2,1,0:T(8,128)(2,1)}, bf16[2,2,128,512]{3,2,1,0:T(8,128)(2,1)S(1)}, u32[]{:S(2)}, u32[]{:S(2)}) collective-permute-start(bf16[2,2,128,512]{3,2,1,0:T(8,128)(2,1)} %get-tuple-element.44), channel_id=1, source_target_pairs={{0,8},{8,0},{1,9},{9,1},{2,10},{10,2},{3,11},{11,3},{4,12},{12,4},... | collective-permute-start | bytes 1572872 | tf_op jit(solution)/shard_map/ppermute | solution.py:28
  154.5 31.6 %collective-permute-start.13 = (bf16[2,2,128,512]{3,2,1,0:T(8,128)(2,1)}, bf16[2,2,128,512]{3,2,1,0:T(8,128)(2,1)S(1)}, u32[]{:S(2)}, u32[]{:S(2)}) collective-permute-start(bf16[2,2,128,512]{3,2,1,0:T(8,128)(2,1)} %get-tuple-element.42), channel_id=1, source_target_pairs={{0,8},{8,0},{1,9},{9,1},{2,10},{10,2},{3,11},{11,3},{4,12},{12,4},... | collective-permute-start | bytes 1572872 | tf_op jit(solution)/shard_map/ppermute | solution.py:28
  155.6 9.5 %collective-permute-start.18 = (bf16[2,128,512]{2,1,0:T(8,128)(2,1)S(1)}, bf16[2,128,512]{2,1,0:T(8,128)(2,1)S(1)}, u32[]{:S(2)}, u32[]{:S(2)}) collective-permute-start(bf16[2,128,512]{2,1,0:T(8,128)(2,1)S(1)} %fusion.11), channel_id=1, source_target_pairs={{0,16},{16,0},{1,17},{17,1},{2,18},{18,2},{3,19},{19,3},{4,20},{20... | collective-permute-start | bytes 786440 | tf_op jit(solution)/shard_map/ppermute | solution.py:28
  157.9 19.9 %collective-permute-start.22 = (bf16[64,4608]{1,0:T(8,128)(2,1)S(1)}, bf16[64,4608]{1,0:T(8,128)(2,1)S(1)}, u32[]{:S(2)}, u32[]{:S(2)}) collective-permute-start(bf16[64,4608]{1,0:T(8,128)(2,1)S(1)} %fusion.1), channel_id=1, source_target_pairs={{0,16},{16,0},{1,17},{17,1},{2,18},{18,2},{3,19},{19,3},{4,20},{20... | collective-permute-start | bytes 1769480 | tf_op jit(solution)/shard_map/ppermute | solution.py:28
  160.7 26.1 %collective-permute-start.16 = (bf16[2,128,512]{2,1,0:T(8,128)(2,1)}, bf16[2,128,512]{2,1,0:T(8,128)(2,1)S(1)}, u32[]{:S(2)}, u32[]{:S(2)}) collective-permute-start(bf16[2,128,512]{2,1,0:T(8,128)(2,1)} %fusion.10), channel_id=1, source_target_pairs={{0,16},{16,0},{1,17},{17,1},{2,18},{18,2},{3,19},{19,3},{4,20},{20... | collective-permute-start | bytes 786440 | tf_op jit(solution)/shard_map/ppermute | solution.py:28
  165.9 20.8 %collective-permute-start.19 = (bf16[2,128,512]{2,1,0:T(8,128)(2,1)}, bf16[2,128,512]{2,1,0:T(8,128)(2,1)}, u32[]{:S(2)}, u32[]{:S(2)}) collective-permute-start(bf16[2,128,512]{2,1,0:T(8,128)(2,1)} %fusion.4), channel_id=1, source_target_pairs={{32,0},{64,32},{96,64},{128,96},{160,128},{192,160},{224,192},{33,... | collective-permute-start | bytes 786440 | tf_op jit(solution)/shard_map/ppermute | solution.py:28
  178.7 27.2 %copy-start.9 = (f32[512,128]{1,0:T(8,128)S(1)}, f32[512,128]{1,0:T(8,128)}, u32[]{:S(2)}) copy-start(f32[512,128]{1,0:T(8,128)} %copy-done.6) | copy-start | bytes 786436
  178.7 28.2 %all-to-all-start = ((bf16[8,8,4608]{2,1,0:T(8,128)(2,1)}), bf16[8,8,4608]{2,1,0:T(8,128)(2,1)S(1)}, u32[]{:S(2)}, u32[]{:S(2)}) async-start(bf16[8,8,4608]{2,1,0:T(8,128)(2,1)} %fusion.2), calls=%async_computation | async-start | bytes 1179648 | tf_op jit(solution)/shard_map/all_to_all | solution.py:487
  186.4 6.5 %collective-permute-start.14 = (bf16[2,128,512]{2,1,0:T(8,128)(2,1)S(1)}, bf16[2,128,512]{2,1,0:T(8,128)(2,1)S(1)}, u32[]{:S(2)}, u32[]{:S(2)}) collective-permute-start(bf16[2,128,512]{2,1,0:T(8,128)(2,1)S(1)} %fusion.9), channel_id=1, source_target_pairs={{0,16},{16,0},{1,17},{17,1},{2,18},{18,2},{3,19},{19,3},{4,20},{20... | collective-permute-start | bytes 786440 | tf_op jit(solution)/shard_map/ppermute | solution.py:28
  187.8 18.1 %collective-permute-start.20 = (bf16[2,128,512]{2,1,0:T(8,128)(2,1)S(1)}, bf16[2,128,512]{2,1,0:T(8,128)(2,1)S(1)}, u32[]{:S(2)}, u32[]{:S(2)}) collective-permute-start(bf16[2,128,512]{2,1,0:T(8,128)(2,1)S(1)} %fusion.7), channel_id=1, source_target_pairs={{32,0},{64,32},{96,64},{128,96},{160,128},{192,160},{224,192},{33,... | collective-permute-start | bytes 786440 | tf_op jit(solution)/shard_map/ppermute | solution.py:28
  (16 other events, 153.5 us)

commit v4 on v3

--- a/solution.py
+++ b/solution.py
@@ -212,11 +212,29 @@
 )
 
 
+def stack_rows(info, cots, first, cs):
+    for d, ref in enumerate(cots):
+        row = pl.multiple_of(first + lax.rem(info[2] + d, 4) * 64, 64)
+        cs[pl.ds(row, 64), :] = ref[...]
+
+
+def prepare(full, q_ref, at_ref, li_ref, do, dl, qt, dt):
+    do[...] = full.astype(BF16)
+    for h in range(2):
+        col = slice(h * HD, (h + 1) * HD)
+        grad = full[:, col].astype(BF16).astype(F32)
+        inverse = li_ref[:, col]
+        total = jnp.sum(grad * at_ref[:, col].astype(F32), axis=1, keepdims=True)
+        dl[h] = jnp.broadcast_to(total, (HALF, HD))
+        dt[h] = (grad * inverse).T.astype(BF16)
+        qt[h] = (q_ref[:, col].astype(F32) * (inverse * QUERY_MULTIPLIER)).T.astype(BF16)
+
+
 def backward_kernel(base, count, has_cots, has_prev, final, info, *refs):
     refs = list(refs)
     take = lambda n: [refs.pop(0) for _ in range(n)]
     cots = take(5) if has_cots else []
-    carry_in = [] if has_cots else take(5)
+    carry_in = [] if has_cots else take(4 if base == 0 else 5)
     q_ref, at_ref = take(2) if has_cots else (None, None)
     li_ref = take(1)[0] if has_cots or final else None
     cos_ref, sin_ref = take(2) if final else (None, None)
@@ -230,9 +248,8 @@
     else:
         (part_ref,) = take(1)
     qg_ref = take(1)[0] if final else None
-    carry_out = [] if final else take(5 if has_cots else 1)
+    carry_out = [] if final else take(1)
     cs, do, dl, qt, dt, dq, pair = refs
-    work = (do, dl, qt, dt, dq)
     if not has_cots:
         do, dl, qt, dt = carry_in[:4]
     step = pl.program_id(0)
@@ -240,19 +257,9 @@
     @pl.when(step == 0)
     def _():
         if has_cots:
-            y = info[2]
-            for d, ref in enumerate(cots[:4]):
-                row = pl.multiple_of(lax.rem(y + d, 4) * 64, 64)
-                cs[pl.ds(row, 64), :] = ref[...]
-            do[...] = tdot(cs[...], cots[4][...]).astype(BF16)
-            for h in range(2):
-                col = slice(h * HD, (h + 1) * HD)
-                grad = do[:, col].astype(F32)
-                inverse = li_ref[:, col]
-                total = jnp.sum(grad * at_ref[:, col].astype(F32), axis=1, keepdims=True)
-                dl[h] = jnp.broadcast_to(total, (HALF, HD))
-                dt[h] = (grad * inverse).T.astype(BF16)
-                qt[h] = (q_ref[:, col].astype(F32) * (inverse * QUERY_MULTIPLIER)).T.astype(BF16)
+            stack_rows(info, cots[:4], 0, cs)
+            prepare(tdot(cs[...], cots[4][...]), q_ref, at_ref, li_ref, do, dl, qt, dt)
+        if base == 0:
             dq[...] = jnp.zeros_like(dq)
         else:
             dq[...] = carry_in[4][...]
@@ -317,8 +324,7 @@
                 g = dq[h] * (li_ref[:, col] * QUERY_MULTIPLIER)
                 qg_ref[:, col] = g * cosine - pltpu.roll(g, HD // 2, 1) * sine
         else:
-            for a, b in zip(carry_out, work if has_cots else work[4:]):
-                a[...] = b[...]
+            carry_out[0][...] = dq[...]
 
 
 def backward(base, count, which, info, rows, panels, eg_all, cots=None, w2=None, carry=None, prev=None, grad=None):
@@ -334,7 +340,7 @@
         ins += [whole(64, 4608)] * 4 + [whole(2 * HD, 4608)]
         args += [*cots, w2]
     else:
-        ins += [whole(*shape) for shape, _ in CARRY]
+        ins += [whole(*shape) for shape, _ in CARRY[: len(carry)]]
         args += list(carry)
     wanted = [has_cots, has_cots, has_cots or final, final, final]
     widths = [2 * HD, 2 * HD, 2 * HD, HD, HD]
@@ -358,9 +364,8 @@
         outs += [tok(2 * HD)]
         shapes += [sds((TOK, 2 * HD), F32)]
     else:
-        left = CARRY if has_cots else CARRY[4:]
-        outs += [whole(*shape) for shape, _ in left]
-        shapes += [sds(*c) for c in left]
+        outs += [whole(*CARRY[4][0])]
+        shapes += [sds(*CARRY[4])]
 
     def kernel(*refs):
         backward_kernel(base, count, has_cots, has_prev, final, *refs)
@@ -385,39 +390,54 @@
     )(info, *args)
 
 
-def weight_kernel(where, *refs):
+def weight_kernel(info, *refs):
     cots = refs[:8]
-    at_ref, keep_ref, send_ref, cs = refs[8:]
-    y, own, core = where[2], where[3], where[4]
-    for n, ref in enumerate(cots):
-        base = own if n < 4 else 1 - own
-        row = pl.multiple_of(base * HALF + lax.rem(y + n % 4, 4) * 64, 64)
-        cs[pl.ds(row, 64), :] = ref[...]
+    pt_ref, w_ref, q_ref, at_ref, li_ref, keep_ref, send_ref, do, dl, qt, dt, cs, full = refs[8:]
+    own, core = info[3], info[4]
+    near = pl.multiple_of(own * HALF, HALF)
+    away = pl.multiple_of((1 - own) * HALF, HALF)
+    stack_rows(info, cots[:4], near, cs)
+    stack_rows(info, cots[4:], away, cs)
     rows = cs[...]
     mine = pl.multiple_of(core * HD, HD)
     other = pl.multiple_of((1 - core) * HD, HD)
-    keep_ref[...] = ndot(at_ref[pl.ds(mine, HD), :], rows)
-    send_ref[...] = ndot(at_ref[pl.ds(other, HD), :], rows).astype(BF16)
-
-
-def weight(where, cots, attn_t):
+    keep_ref[...] = ndot(pt_ref[pl.ds(mine, HD), :], rows)
+    send_ref[...] = ndot(pt_ref[pl.ds(other, HD), :], rows).astype(BF16)
+    part = tdot(cs[pl.ds(away, HALF), :], w_ref[...])
+
+    @pl.when(pl.program_id(0) == 0)
+    def _():
+        full[...] = part
+
+    @pl.when(pl.program_id(0) > 0)
+    def _():
+        full[...] += part
+
+    @pl.when(pl.program_id(0) == pl.num_programs(0) - 1)
+    def _():
+        prepare(full[...], q_ref, at_ref, li_ref, do, dl, qt, dt)
+
+
+def weight(info, cots, attn_t, w2, rows):
     chunk = 1152
     sds = jax.ShapeDtypeStruct
-    block = lambda rows: pl.BlockSpec((rows, chunk), lambda i, w: (0, i))
+    block = lambda n: pl.BlockSpec((n, chunk), lambda i, f: (0, i))
+    whole = lambda *shape: pl.BlockSpec(shape, lambda i, *_: (0,) * len(shape))
+    tok = pl.BlockSpec((HALF, 2 * HD), lambda i, f: (1 - f[3], 0))
     return pl.pallas_call(
         weight_kernel,
-        out_shape=(sds((HD, 4608), F32), sds((HD, 4608), BF16)),
+        out_shape=(sds((HD, 4608), F32), sds((HD, 4608), BF16), *(sds(*c) for c in CARRY[:4])),
         grid_spec=pltpu.PrefetchScalarGridSpec(
             num_scalar_prefetch=1,
             grid=(4608 // chunk,),
-            in_specs=[block(64)] * 8 + [pl.BlockSpec((2 * HD, TOK), lambda i, w: (0, 0))],
-            out_specs=(block(HD), block(HD)),
-            scratch_shapes=[pltpu.VMEM((TOK, chunk), BF16)],
+            in_specs=[block(64)] * 8 + [whole(2 * HD, TOK), block(2 * HD), tok, tok, tok],
+            out_specs=(block(HD), block(HD), *(whole(*shape) for shape, _ in CARRY[:4])),
+            scratch_shapes=[pltpu.VMEM((TOK, chunk), BF16), pltpu.VMEM((HALF, 2 * HD), F32)],
         ),
-        compiler_params=pltpu.CompilerParams(dimension_semantics=("arbitrary",), vmem_limit_bytes=46 << 20),
-        cost_estimate=pl.CostEstimate(flops=1_300_000_000, bytes_accessed=9_000_000, transcendentals=0),
+        compiler_params=pltpu.CompilerParams(dimension_semantics=("arbitrary",), vmem_limit_bytes=60 << 20),
+        cost_estimate=pl.CostEstimate(flops=1_900_000_000, bytes_accessed=11_000_000, transcendentals=0),
         name="weigh",
-    )(where, *cots, attn_t)
+    )(info, *cots, attn_t, w2, *rows[:3])
 
 
 def settle_kernel(own_ref, left_ref, down_ref, cos_ref, sin_ref, kg_ref, vg_ref):
@@ -477,32 +497,30 @@
     rows = (qr, attn, linv, cosf, sinf)
     prev, half = backward(0, SLOTS, 1, info, rows, panels, eg, cots=near, w2=w2)
 
-    wkeep, wsend = weight(info, near + far, attn_t)
+    wkeep, wsend, *carry = weight(info, near + far, attn_t, w2, rows)
     wgot = swap(wsend, "c")
-    wsum = (wkeep + wgot.astype(F32)).reshape(2, 64, 4608)
-    wgive = lax.dynamic_index_in_dim(wsum, 1 - xl, 0, False).astype(BF16)
-    wown = lax.dynamic_index_in_dim(wsum, xl, 0, False)
+    wkeep, wgot = wkeep.reshape(2, 64, 4608), wgot.reshape(2, 64, 4608)
+    half_at = lambda a, n: lax.dynamic_index_in_dim(a, n, 0, False).astype(F32)
+    wgive = (half_at(wkeep, 1 - xl) + half_at(wgot, 1 - xl)).astype(BF16)
     wback = swap(wgive, "xl")
-    wz = (wown + wback.astype(F32)).astype(BF16).reshape(8, 8, 4608)
+    wz = (half_at(wkeep, xl) + half_at(wgot, xl) + wback.astype(F32)).astype(BF16).reshape(8, 8, 4608)
     wz = lax.all_to_all(wz, "z", 0, 0, tiled=True)
     weight_grad = jnp.sum(wz.astype(F32), axis=0).reshape(4, 2, 4608)
 
     total = []
-    carry = None
     for p in range(PANELS):
         out = backward(
             p * 4, 4, 2, info, rows, panels, eg,
-            cots=far if p == 0 else None, w2=w2 if p == 0 else None, carry=carry, prev=prev,
-            grad=half if p == PANELS - 1 else None,
+            carry=carry, prev=prev, grad=half if p == PANELS - 1 else None,
         )
-        keep, send, *after = out
-        carry = after if len(after) != 1 or p == PANELS - 1 else [*carry[:4], *after]
+        keep, send, last = out
+        carry = [*carry[:4], last]
         got = swap(send, "c")
         both = keep.astype(F32) + got.astype(F32)
         give = both[1].astype(BF16)
         turned = swap(give, "xl")
         total.append((both, turned))
-    (query_grad,) = carry
+    query_grad = last
     down1 = along_z((total[0][0][0] + total[0][1].astype(F32)).astype(BF16), -1)
     down0 = along_z((total[1][0][0] + total[1][1].astype(F32) + down1.astype(F32)).astype(BF16), -1)
     key_grad, value_grad = settle(*total[2], down0, cosf, sinf)

time: 209 us -> 214 us (1.024)
  local copies, waits for them, and re-layouts: 9.07 us -> 15.5 us
  waiting for transfers between devices: 93.9 us -> 91.2 us
    unnamed x49 -> x63, local copies, waits for them, and re-layouts: 4 us -> 11.3 us
    pallas_call x1, Pallas kernels: 5.67 us -> 8.67 us  [weight(): pl.pallas_call(weight_kernel, out_shape=(sds((HD, 4608), F32), sds((HD, 4...]
    pallas_call x4, Pallas kernels: 36.9 us -> 34.1 us  [backward(): pl.pallas_call(kernel, out_shape=shapes, grid_spec=pltpu.PrefetchScalarGr...]
    ppermute x23, waiting for transfers between devices: 93.9 us -> 91.2 us  [permute(): return lax.ppermute(x, axis, pairs)]
  transfers between devices with their start and end apart: 24 -> 24, of which waited for: 12 -> 12; matrix products, arithmetic and copies ran while one was open for 4% -> 4% of each run, Pallas kernels for 25% -> 23%
where the time goes in v4:
time: 214 us; the launch traced here: 213 us
  waiting for transfers between devices  91.2 us (43%)
  Pallas kernels  57 us (27%)
  starting transfers between devices  41.3 us (19%)
  local copies, waits for them, and re-layouts  15.5 us (7%)
  other arithmetic  6.56 us (3%)
    ppermute x23, waiting for transfers between devices, permute(): return lax.ppermute(x, axis, pairs)  91.2 us
    pallas_call x4, Pallas kernels, backward(): pl.pallas_call(kernel, out_shape=shapes, grid_spec=pltpu.PrefetchScalarGr...  34.1 us
    ppermute x23, starting transfers between devices, permute(): return lax.ppermute(x, axis, pairs)  33.8 us
    pallas_call x1, Pallas kernels, forward(): pl.pallas_call(forward_kernel, out_shape=(sds((SLOTS, 2, 2, TOK, TOK), BF...  13.1 us
    unnamed x63, local copies, waits for them, and re-layouts  11.3 us
    pallas_call x1, Pallas kernels, weight(): pl.pallas_call(weight_kernel, out_shape=(sds((HD, 4608), F32), sds((HD, 4...  8.67 us
    all_to_all x1, starting transfers between devices, local(): wz = lax.all_to_all(wz, 'z', 0, 0, tiled=True)  7.54 us
  transfers between devices with their start and end apart: 24, of which 12 were waited for; matrix products, arithmetic and copies ran while one was open for 4% of the time, Pallas kernels for 23%

profile of v4, /device:TPU:96, one launch (start us, length us, event | category | flops | bytes accessed | tf_op | source)
XLA Modules:
  0.0 212.6 jit_solution(12218365070926724118)
XLA Ops:
  0.7 1.7 fusion.8
  4.4 5.5 %collective-permute-start.7 = (bf16[1,2,512,128]{3,2,1,0:T(8,128)(2,1)S(1)}, bf16[1,2,512,128]{3,2,1,0:T(8,128)(2,1)S(1)}, u32[]{:S(2)}, u32[]{:S(2)}) collective-permute-start(bf16[1,2,512,128]{3,2,1,0:T(8,128)(2,1)S(1)} %turn.1), channel_id=1, source_target_pairs={{0,64},{32,96},{64,128},{96,160},{128,192},{160,224},{1,65},{33,97... | collective-permute-start | bytes 786440 | tf_op jit(solution)/shard_map/ppermute | solution.py:28
  9.9 2.9 %collective-permute-start.8 = (bf16[1,2,512,128]{3,2,1,0:T(8,128)(2,1)S(1)}, bf16[1,2,512,128]{3,2,1,0:T(8,128)(2,1)S(1)}, u32[]{:S(2)}, u32[]{:S(2)}) collective-permute-start(bf16[1,2,512,128]{3,2,1,0:T(8,128)(2,1)S(1)} %turn.1), channel_id=1, source_target_pairs={{0,32},{32,64},{64,96},{96,128},{128,160},{160,192},{192,224},{1,3... | collective-permute-start | bytes 786440 | tf_op jit(solution)/shard_map/ppermute | solution.py:28
  12.9 7.7 %collective-permute-done.7 = bf16[1,2,512,128]{3,2,1,0:T(8,128)(2,1)S(1)} collective-permute-done((bf16[1,2,512,128]{3,2,1,0:T(8,128)(2,1)S(1)}, bf16[1,2,512,128]{3,2,1,0:T(8,128)(2,1)S(1)}, u32[]{:S(2)}, u32[]{:S(2)}) %collective-permute-start.7) | collective-permute-done | bytes 262176 | tf_op jit(solution)/shard_map/ppermute | solution.py:28
  20.6 7.5 %collective-permute-done.8 = bf16[1,2,512,128]{3,2,1,0:T(8,128)(2,1)S(1)} collective-permute-done((bf16[1,2,512,128]{3,2,1,0:T(8,128)(2,1)S(1)}, bf16[1,2,512,128]{3,2,1,0:T(8,128)(2,1)S(1)}, u32[]{:S(2)}, u32[]{:S(2)}) %collective-permute-start.8) | collective-permute-done | bytes 262176 | tf_op jit(solution)/shard_map/ppermute | solution.py:28
  28.2 1.6 collective-permute-start.9
  30.5 12.6 %collective-permute-done.9 = bf16[2,2,512,128]{3,2,1,0:T(8,128)(2,1)S(1)} collective-permute-done((bf16[2,2,512,128]{3,2,1,0:T(8,128)(2,1)S(1)}, bf16[2,2,512,128]{3,2,1,0:T(8,128)(2,1)S(1)}, u32[]{:S(2)}, u32[]{:S(2)}) %collective-permute-start.9) | collective-permute-done | bytes 524320 | tf_op jit(solution)/shard_map/ppermute | solution.py:28
  43.1 3.6 %collective-permute-done.10 = bf16[1,2,512,128]{3,2,1,0:T(8,128)(2,1)S(1)} collective-permute-done((bf16[1,2,512,128]{3,2,1,0:T(8,128)(2,1)S(1)}, bf16[1,2,512,128]{3,2,1,0:T(8,128)(2,1)S(1)}, u32[]{:S(2)}, u32[]{:S(2)}) %collective-permute-start.10) | collective-permute-done | bytes 262176 | tf_op jit(solution)/shard_map/ppermute | solution.py:28
  46.9 3.1 %collective-permute-start.3 = (bf16[64,4608]{1,0:T(8,128)(2,1)}, bf16[64,4608]{1,0:T(8,128)(2,1)}, u32[]{:S(2)}, u32[]{:S(2)}) collective-permute-start(bf16[64,4608]{1,0:T(8,128)(2,1)} %refs_1_.1), channel_id=1, source_target_pairs={{0,4},{4,0},{1,5},{5,1},{2,6},{6,2},{3,7},{7,3},{8,12},{12,8},{9,1... | collective-permute-start | bytes 1769480 | tf_op jit(solution)/shard_map/ppermute | solution.py:28
  50.0 3.0 %collective-permute-start = (bf16[64,4608]{1,0:T(8,128)(2,1)}, bf16[64,4608]{1,0:T(8,128)(2,1)}, u32[]{:S(2)}, u32[]{:S(2)}) collective-permute-start(bf16[64,4608]{1,0:T(8,128)(2,1)} %refs_1_.1), channel_id=1, source_target_pairs={{1,0},{2,1},{3,2},{0,3},{5,4},{6,5},{7,6},{4,7},{9,8},{10,9},{11,1... | collective-permute-start | bytes 1769480 | tf_op jit(solution)/shard_map/ppermute | solution.py:28
  53.6 3.3 %copy.12 = bf16[2,128,4608]{2,1,0:T(8,128)(2,1)} copy(bf16[2,128,4608]{2,0,1:T(2,128)(2,1)} %bitcast.43) | data formatting | bytes 4718592 | tf_op jit(solution)/shard_map/transpose | solution.py:494
  57.0 7.4 %collective-permute-done.3.refs_4_ = bf16[64,4608]{1,0:T(8,128)(2,1)} collective-permute-done((bf16[64,4608]{1,0:T(8,128)(2,1)}, bf16[64,4608]{1,0:T(8,128)(2,1)}, u32[]{:S(2)}, u32[]{:S(2)}) %collective-permute-start.3) | collective-permute-done | bytes 589856 | tf_op jit(solution)/shard_map/ppermute | solution.py:28
  64.4 1.6 collective-permute-start.2
  66.0 12.8 %collective-permute-done.refs_1_.refs_2_ = bf16[64,4608]{1,0:T(8,128)(2,1)} collective-permute-done((bf16[64,4608]{1,0:T(8,128)(2,1)}, bf16[64,4608]{1,0:T(8,128)(2,1)}, u32[]{:S(2)}, u32[]{:S(2)}) %collective-permute-start) | collective-permute-done | bytes 589856 | tf_op jit(solution)/shard_map/ppermute | solution.py:28
  78.8 3.7 %collective-permute-start.4 = (bf16[64,4608]{1,0:T(8,128)(2,1)}, bf16[64,4608]{1,0:T(8,128)(2,1)S(1)}, u32[]{:S(2)}, u32[]{:S(2)}) collective-permute-start(bf16[64,4608]{1,0:T(8,128)(2,1)} %collective-permute-done.3.refs_4_), channel_id=1, source_target_pairs={{1,0},{2,1},{3,2},{0,3},{5,4},{6,5},{7,6},{4,7},{9,8},{10,9},{11,1... | collective-permute-start | bytes 1769480 | tf_op jit(solution)/shard_map/ppermute | solution.py:28
  85.4 13.1 %attend.1 = (bf16[12,2,2,512,512]{4,3,2,1,0:T(8,128)(2,1)}, bf16[512,256]{1,0:T(8,128)(2,1)S(1)}, bf16[512,256]{1,0:T(8,128)(2,1)S(1)}, f32[512,256]{1,0:T(8,128)S(1)}, bf16[256,512]{1,0:T(8,128)(2,1)S(1)}) custom-call(s32[5]{0:T(128)S(1)} %stack.23.info.refs_0_, bf16[512,256]{1,0:T(8,128)(2,1)S(1)} %copy-done.23, f32[512,128]{1,0:T(8,128)S(1)} %copy-done.7, ...), custom_call_target="tpu_custom_call" | custom-call | flops 10000000000 | bytes 24000000 | tf_op jit(solution)/shard_map/attend/pallas_call | solution.py:173
  101.4 6.1 %collective-permute-done.4.refs_5_ = bf16[64,4608]{1,0:T(8,128)(2,1)S(1)} collective-permute-done((bf16[64,4608]{1,0:T(8,128)(2,1)}, bf16[64,4608]{1,0:T(8,128)(2,1)S(1)}, u32[]{:S(2)}, u32[]{:S(2)}) %collective-permute-start.4) | collective-permute-done | bytes 589856 | tf_op jit(solution)/shard_map/ppermute | solution.py:28
  107.5 3.6 %collective-permute-done.6.refs_7_ = bf16[64,4608]{1,0:T(8,128)(2,1)S(1)} collective-permute-done((bf16[64,4608]{1,0:T(8,128)(2,1)}, bf16[64,4608]{1,0:T(8,128)(2,1)S(1)}, u32[]{:S(2)}, u32[]{:S(2)}) %collective-permute-start.6) | collective-permute-done | bytes 589856 | tf_op jit(solution)/shard_map/ppermute | solution.py:28
  111.9 8.7 %weigh.1 = (f32[128,4608]{1,0:T(8,128)}, bf16[128,4608]{1,0:T(8,128)(2,1)}, bf16[256,256]{1,0:T(8,128)(2,1)}, f32[2,256,128]{2,1,0:T(8,128)}, bf16[2,128,256]{2,...) custom-call(s32[5]{0:T(128)} %copy-done.21, bf16[64,4608]{1,0:T(8,128)(2,1)} %refs_1_.1, ...), custom_call_target="tpu_custom_call" | custom-call | flops 1900000000 | bytes 11000000 | tf_op jit(solution)/shard_map/weigh/pallas_call | solution.py:427
  123.9 13.9 %shard_map.102 = (bf16[12,2,128,512]{3,2,1,0:T(8,128)(2,1)}, f32[512,256]{1,0:T(8,128)}) custom-call(s32[5]{0:T(128)S(1)} %copy-done.22, bf16[64,4608]{1,0:T(8,128)(2,1)} %refs_1_.1, bf16[64,4608]{1,0:T(8,128)(2,1)} %collective-permute-done.refs_1_.refs_2_, bf16[64,4608]{1,0:T(8,128)(2,1)} %collective-permute-done.1.refs_2_.refs_3_, ...), custom_call_target="tpu_custom_call" | custom-call | flops 8400000000 | bytes 24000000 | tf_op jit(solution)/shard_map/pallas_call | solution.py:373
  137.8 7.2 %shard_map.103 = (bf16[2,2,128,512]{3,2,1,0:T(8,128)(2,1)}, bf16[2,2,128,512]{3,2,1,0:T(8,128)(2,1)}, f32[2,256,128]{2,1,0:T(8,128)}) custom-call(s32[5]{0:T(128)} %copy-done.21, bf16[256,256]{1,0:T(8,128)(2,1)} %get-tuple-element.32.refs_1_, f32[2,256,128]{2,1,0:T(8,128)} %get-tuple-element.33.refs_2_, bf16[2,128,256]{2,1,0:T(8,128)(2,1)} %get-tuple-element.34.refs_3_, ...), custom_call_target="tpu_custom_call" | custom-call | flops 2800000000 | bytes 8000000 | tf_op jit(solution)/shard_map/pallas_call | solution.py:373
  145.1 7.4 %shard_map.104 = (bf16[2,2,128,512]{3,2,1,0:T(8,128)(2,1)}, bf16[2,2,128,512]{3,2,1,0:T(8,128)(2,1)}, f32[2,256,128]{2,1,0:T(8,128)}) custom-call(s32[5]{0:T(128)} %copy-done.21, bf16[256,256]{1,0:T(8,128)(2,1)} %get-tuple-element.32.refs_1_, f32[2,256,128]{2,1,0:T(8,128)} %get-tuple-element.33.refs_2_, bf16[2,128,256]{2,1,0:T(8,128)(2,1)} %get-tuple-element.34.refs_3_, ...), custom_call_target="tpu_custom_call" | custom-call | flops 2800000000 | bytes 8000000 | tf_op jit(solution)/shard_map/pallas_call | solution.py:373
  153.0 5.5 %shard_map.105 = (bf16[2,2,128,512]{3,2,1,0:T(8,128)(2,1)}, bf16[2,2,128,512]{3,2,1,0:T(8,128)(2,1)}, f32[512,256]{1,0:T(8,128)}) custom-call(s32[5]{0:T(128)} %copy-done.21, bf16[256,256]{1,0:T(8,128)(2,1)} %get-tuple-element.32.refs_1_, f32[2,256,128]{2,1,0:T(8,128)} %get-tuple-element.33.refs_2_, ...), custom_call_target="tpu_custom_call", output_to_operand_aliasing={{2}: (15, {})} | custom-call | flops 2800000000 | bytes 8000000 | tf_op jit(solution)/shard_map/pallas_call | solution.py:373
  163.6 1.3 collective-permute-start.16
  164.9 3.9 %collective-permute-done.18 = bf16[2,128,512]{2,1,0:T(8,128)(2,1)S(1)} collective-permute-done((bf16[2,128,512]{2,1,0:T(8,128)(2,1)S(1)}, bf16[2,128,512]{2,1,0:T(8,128)(2,1)S(1)}, u32[]{:S(2)}, u32[]{:S(2)}) %collective-permute-start.18) | collective-permute-done | bytes 262176 | tf_op jit(solution)/shard_map/ppermute | solution.py:28
  169.6 1.9 collective-permute-start.19
  171.5 10.0 %collective-permute-done.22 = bf16[64,4608]{1,0:T(8,128)(2,1)S(1)} collective-permute-done((bf16[64,4608]{1,0:T(8,128)(2,1)S(1)}, bf16[64,4608]{1,0:T(8,128)(2,1)S(1)}, u32[]{:S(2)}, u32[]{:S(2)}) %collective-permute-start.22) | collective-permute-done | bytes 589856 | tf_op jit(solution)/shard_map/ppermute | solution.py:28
  181.5 2.1 fusion.2
  183.6 7.5 %all-to-all-start = ((bf16[8,8,4608]{2,1,0:T(8,128)(2,1)}), bf16[8,8,4608]{2,1,0:T(8,128)(2,1)S(1)}, u32[]{:S(2)}, u32[]{:S(2)}) async-start(bf16[8,8,4608]{2,1,0:T(8,128)(2,1)} %fusion.2), calls=%async_computation | async-start | bytes 1179648 | tf_op jit(solution)/shard_map/all_to_all | solution.py:507
  192.3 2.5 %collective-permute-start.20 = (bf16[2,128,512]{2,1,0:T(8,128)(2,1)S(1)}, bf16[2,128,512]{2,1,0:T(8,128)(2,1)S(1)}, u32[]{:S(2)}, u32[]{:S(2)}) collective-permute-start(bf16[2,128,512]{2,1,0:T(8,128)(2,1)S(1)} %fusion.7), channel_id=1, source_target_pairs={{32,0},{64,32},{96,64},{128,96},{160,128},{192,160},{224,192},{33,... | collective-permute-start | bytes 786440 | tf_op jit(solution)/shard_map/ppermute | solution.py:28
  194.8 3.0 %collective-permute-done.14.left_ref = bf16[2,128,512]{2,1,0:T(8,128)(2,1)S(1)} collective-permute-done((bf16[2,128,512]{2,1,0:T(8,128)(2,1)S(1)}, bf16[2,128,512]{2,1,0:T(8,128)(2,1)S(1)}, u32[]{:S(2)}, u32[]{:S(2)}) %collective-permute-start.14) | collective-permute-done | bytes 262176 | tf_op jit(solution)/shard_map/ppermute | solution.py:28
  197.8 13.0 %collective-permute-done.20.down_ref = bf16[2,128,512]{2,1,0:T(8,128)(2,1)S(1)} collective-permute-done((bf16[2,128,512]{2,1,0:T(8,128)(2,1)S(1)}, bf16[2,128,512]{2,1,0:T(8,128)(2,1)S(1)}, u32[]{:S(2)}, u32[]{:S(2)}) %collective-permute-start.20) | collective-permute-done | bytes 262176 | tf_op jit(solution)/shard_map/ppermute | solution.py:28
  (106 shorter events, 22.9 us)
Async XLA Ops:
  2.3 28.1 %copy-start.6 = (f32[512,128]{1,0:T(8,128)}, f32[512,128]{1,0:T(8,128)S(1)}, u32[]{:S(2)}) copy-start(f32[512,128]{1,0:T(8,128)S(1)} %get-tuple-element.53.cos_ref.refs_9_.refs_7_) | copy-start | bytes 786436
  2.3 118.4 %copy-start.4 = (f32[512,128]{1,0:T(8,128)}, f32[512,128]{1,0:T(8,128)S(1)}, u32[]{:S(2)}) copy-start(f32[512,128]{1,0:T(8,128)S(1)} %get-tuple-element.52.sin_ref.refs_10_.refs_8_) | copy-start | bytes 786436
  4.4 16.1 %collective-permute-start.7 = (bf16[1,2,512,128]{3,2,1,0:T(8,128)(2,1)S(1)}, bf16[1,2,512,128]{3,2,1,0:T(8,128)(2,1)S(1)}, u32[]{:S(2)}, u32[]{:S(2)}) collective-permute-start(bf16[1,2,512,128]{3,2,1,0:T(8,128)(2,1)S(1)} %turn.1), channel_id=1, source_target_pairs={{0,64},{32,96},{64,128},{96,160},{128,192},{160,224},{1,65},{33,97... | collective-permute-start | bytes 786440 | tf_op jit(solution)/shard_map/ppermute | solution.py:28
  9.9 18.2 %collective-permute-start.8 = (bf16[1,2,512,128]{3,2,1,0:T(8,128)(2,1)S(1)}, bf16[1,2,512,128]{3,2,1,0:T(8,128)(2,1)S(1)}, u32[]{:S(2)}, u32[]{:S(2)}) collective-permute-start(bf16[1,2,512,128]{3,2,1,0:T(8,128)(2,1)S(1)} %turn.1), channel_id=1, source_target_pairs={{0,32},{32,64},{64,96},{96,128},{128,160},{160,192},{192,224},{1,3... | collective-permute-start | bytes 786440 | tf_op jit(solution)/shard_map/ppermute | solution.py:28
  28.2 14.9 %collective-permute-start.9 = (bf16[2,2,512,128]{3,2,1,0:T(8,128)(2,1)S(1)}, bf16[2,2,512,128]{3,2,1,0:T(8,128)(2,1)S(1)}, u32[]{:S(2)}, u32[]{:S(2)}) collective-permute-start(bf16[2,2,512,128]{3,2,1,0:T(8,128)(2,1)S(1)} %pad_maximum_fusion.1), channel_id=1, source_target_pairs={{0,16},{16,0},{1,17},{17,1},{2,18},{18,2},{3,19},{19,3},{4,20},{20... | collective-permute-start | bytes 1572872 | tf_op jit(solution)/shard_map/ppermute | solution.py:28
  29.8 17.0 %collective-permute-start.10 = (bf16[1,2,512,128]{3,2,1,0:T(8,128)(2,1)S(1)}, bf16[1,2,512,128]{3,2,1,0:T(8,128)(2,1)S(1)}, u32[]{:S(2)}, u32[]{:S(2)}) collective-permute-start(bf16[1,2,512,128]{3,2,1,0:T(8,128)(2,1)S(1)} %turn.1), channel_id=1, source_target_pairs={{0,16},{16,0},{1,17},{17,1},{2,18},{18,2},{3,19},{19,3},{4,20},{20... | collective-permute-start | bytes 786440 | tf_op jit(solution)/shard_map/ppermute | solution.py:28
  30.4 90.4 %copy-start = (bf16[3,2,512,128]{3,2,1,0:T(8,128)(2,1)}, bf16[3,2,512,128]{3,2,1,0:T(8,128)(2,1)S(1)}, u32[]{:S(2)}) copy-start(bf16[3,2,512,128]{3,2,1,0:T(8,128)(2,1)S(1)} %pad_maximum_fusion.r0.refs_11_.refs_5_.refs_6_.refs_9_) | copy-start | bytes 2359300
  30.4 52.1 %collective-permute-start.11 = (bf16[3,2,512,128]{3,2,1,0:T(8,128)(2,1)S(1)}, bf16[3,2,512,128]{3,2,1,0:T(8,128)(2,1)S(1)}, u32[]{:S(2)}, u32[]{:S(2)}) collective-permute-start(bf16[3,2,512,128]{3,2,1,0:T(8,128)(2,1)S(1)} %pad_maximum_fusion.r0.refs_11_.refs_5_.refs_6_.refs_9_), channel_id=1, source_target_pairs={{0,8},{8,0},{1,9},{9,1},{2,10},{10,2},{3,11},{11,3},{4,12},{12,4},... | collective-permute-start | bytes 2359304 | tf_op jit(solution)/shard_map/ppermute | solution.py:28
  46.8 74.0 %copy-start.1 = (bf16[3,2,512,128]{3,2,1,0:T(8,128)(2,1)}, bf16[3,2,512,128]{3,2,1,0:T(8,128)(2,1)S(1)}, u32[]{:S(2)}) copy-start(bf16[3,2,512,128]{3,2,1,0:T(8,128)(2,1)S(1)} %constant_dynamic-update-slice_fusion.r2.refs_12_.refs_6_.refs_7_.refs_10_) | copy-start | bytes 2359300
  46.8 35.8 %collective-permute-start.12 = (bf16[3,2,512,128]{3,2,1,0:T(8,128)(2,1)S(1)}, bf16[3,2,512,128]{3,2,1,0:T(8,128)(2,1)S(1)}, u32[]{:S(2)}, u32[]{:S(2)}) collective-permute-start(bf16[3,2,512,128]{3,2,1,0:T(8,128)(2,1)S(1)} %constant_dynamic-update-slice_fusion.r2.refs_12_.refs_6_.refs_7_.refs_10_), channel_id=1, source_target_pairs={{0,8},{8,0},{1,9},{9,1},{2,10},{10,2},{3,11},{11,3},{4,12},{12,4},... | collective-permute-start | bytes 2359304 | tf_op jit(solution)/shard_map/ppermute | solution.py:28
  46.9 17.6 %collective-permute-start.3 = (bf16[64,4608]{1,0:T(8,128)(2,1)}, bf16[64,4608]{1,0:T(8,128)(2,1)}, u32[]{:S(2)}, u32[]{:S(2)}) collective-permute-start(bf16[64,4608]{1,0:T(8,128)(2,1)} %refs_1_.1), channel_id=1, source_target_pairs={{0,4},{4,0},{1,5},{5,1},{2,6},{6,2},{3,7},{7,3},{8,12},{12,8},{9,1... | collective-permute-start | bytes 1769480 | tf_op jit(solution)/shard_map/ppermute | solution.py:28
  50.0 28.9 %collective-permute-start = (bf16[64,4608]{1,0:T(8,128)(2,1)}, bf16[64,4608]{1,0:T(8,128)(2,1)}, u32[]{:S(2)}, u32[]{:S(2)}) collective-permute-start(bf16[64,4608]{1,0:T(8,128)(2,1)} %refs_1_.1), channel_id=1, source_target_pairs={{1,0},{2,1},{3,2},{0,3},{5,4},{6,5},{7,6},{4,7},{9,8},{10,9},{11,1... | collective-permute-start | bytes 1769480 | tf_op jit(solution)/shard_map/ppermute | solution.py:28
  53.0 48.4 %collective-permute-start.1 = (bf16[64,4608]{1,0:T(8,128)(2,1)}, bf16[64,4608]{1,0:T(8,128)(2,1)}, u32[]{:S(2)}, u32[]{:S(2)}) collective-permute-start(bf16[64,4608]{1,0:T(8,128)(2,1)} %refs_1_.1), channel_id=1, source_target_pairs={{2,0},{3,1},{0,2},{1,3},{6,4},{7,5},{4,6},{5,7},{10,8},{11,9},{8,1... | collective-permute-start | bytes 1769480 | tf_op jit(solution)/shard_map/ppermute | solution.py:28
  57.0 41.5 %copy-start.21 = (s32[5]{0:T(128)}, s32[5]{0:T(128)S(1)}, u32[]{:S(2)}) copy-start(s32[5]{0:T(128)S(1)} %stack.23.info.refs_0_) | copy-start | bytes 64
  64.4 37.0 %collective-permute-start.2 = (bf16[64,4608]{1,0:T(8,128)(2,1)}, bf16[64,4608]{1,0:T(8,128)(2,1)S(1)}, u32[]{:S(2)}, u32[]{:S(2)}) collective-permute-start(bf16[64,4608]{1,0:T(8,128)(2,1)} %refs_1_.1), channel_id=1, source_target_pairs={{3,0},{0,1},{1,2},{2,3},{7,4},{4,5},{5,6},{6,7},{11,8},{8,9},{9,10... | collective-permute-start | bytes 1769480 | tf_op jit(solution)/shard_map/ppermute | solution.py:28
  78.8 28.7 %collective-permute-start.4 = (bf16[64,4608]{1,0:T(8,128)(2,1)}, bf16[64,4608]{1,0:T(8,128)(2,1)S(1)}, u32[]{:S(2)}, u32[]{:S(2)}) collective-permute-start(bf16[64,4608]{1,0:T(8,128)(2,1)} %collective-permute-done.3.refs_4_), channel_id=1, source_target_pairs={{1,0},{2,1},{3,2},{0,3},{5,4},{6,5},{7,6},{4,7},{9,8},{10,9},{11,1... | collective-permute-start | bytes 1769480 | tf_op jit(solution)/shard_map/ppermute | solution.py:28
  82.5 38.2 %copy-start.2 = (bf16[3,2,512,128]{3,2,1,0:T(8,128)(2,1)}, bf16[3,2,512,128]{3,2,1,0:T(8,128)(2,1)S(1)}, u32[]{:S(2)}) copy-start(bf16[3,2,512,128]{3,2,1,0:T(8,128)(2,1)S(1)} %collective-permute-done.11.r1.refs_13_.refs_7_.refs_8_.refs_11_) | copy-start | bytes 2359300
  82.5 25.0 %collective-permute-start.5 = (bf16[64,4608]{1,0:T(8,128)(2,1)}, bf16[64,4608]{1,0:T(8,128)(2,1)S(1)}, u32[]{:S(2)}, u32[]{:S(2)}) collective-permute-start(bf16[64,4608]{1,0:T(8,128)(2,1)} %collective-permute-done.3.refs_4_), channel_id=1, source_target_pairs={{2,0},{3,1},{0,2},{1,3},{6,4},{7,5},{4,6},{5,7},{10,8},{11,9},{8,1... | collective-permute-start | bytes 1769480 | tf_op jit(solution)/shard_map/ppermute | solution.py:28
  82.6 38.2 %copy-start.3 = (bf16[3,2,512,128]{3,2,1,0:T(8,128)(2,1)}, bf16[3,2,512,128]{3,2,1,0:T(8,128)(2,1)S(1)}, u32[]{:S(2)}) copy-start(bf16[3,2,512,128]{3,2,1,0:T(8,128)(2,1)S(1)} %collective-permute-done.12.r3.refs_14_.refs_8_.refs_9_.refs_12_) | copy-start | bytes 2359300
  82.6 28.5 %collective-permute-start.6 = (bf16[64,4608]{1,0:T(8,128)(2,1)}, bf16[64,4608]{1,0:T(8,128)(2,1)S(1)}, u32[]{:S(2)}, u32[]{:S(2)}) collective-permute-start(bf16[64,4608]{1,0:T(8,128)(2,1)} %collective-permute-done.3.refs_4_), channel_id=1, source_target_pairs={{3,0},{0,1},{1,2},{2,3},{7,4},{4,5},{5,6},{6,7},{11,8},{8,9},{9,10... | collective-permute-start | bytes 1769480 | tf_op jit(solution)/shard_map/ppermute | solution.py:28
  120.6 39.9 %collective-permute-start.21 = (bf16[128,4608]{1,0:T(8,128)(2,1)}, bf16[128,4608]{1,0:T(8,128)(2,1)}, u32[]{:S(2)}, u32[]{:S(2)}) collective-permute-start(bf16[128,4608]{1,0:T(8,128)(2,1)} %get-tuple-element.51), channel_id=1, source_target_pairs={{0,8},{8,0},{1,9},{9,1},{2,10},{10,2},{3,11},{11,3},{4,12},{12,4},... | collective-permute-start | bytes 3538952 | tf_op jit(solution)/shard_map/ppermute | solution.py:28
  145.0 14.3 %collective-permute-start.17 = (bf16[2,2,128,512]{3,2,1,0:T(8,128)(2,1)}, bf16[2,2,128,512]{3,2,1,0:T(8,128)(2,1)S(1)}, u32[]{:S(2)}, u32[]{:S(2)}) collective-permute-start(bf16[2,2,128,512]{3,2,1,0:T(8,128)(2,1)} %get-tuple-element.47), channel_id=1, source_target_pairs={{0,8},{8,0},{1,9},{9,1},{2,10},{10,2},{3,11},{11,3},{4,12},{12,4},... | collective-permute-start | bytes 1572872 | tf_op jit(solution)/shard_map/ppermute | solution.py:28
  152.5 11.0 %collective-permute-start.15 = (bf16[2,2,128,512]{3,2,1,0:T(8,128)(2,1)}, bf16[2,2,128,512]{3,2,1,0:T(8,128)(2,1)S(1)}, u32[]{:S(2)}, u32[]{:S(2)}) collective-permute-start(bf16[2,2,128,512]{3,2,1,0:T(8,128)(2,1)} %get-tuple-element.45), channel_id=1, source_target_pairs={{0,8},{8,0},{1,9},{9,1},{2,10},{10,2},{3,11},{11,3},{4,12},{12,4},... | collective-permute-start | bytes 1572872 | tf_op jit(solution)/shard_map/ppermute | solution.py:28
  158.5 32.6 %collective-permute-start.13 = (bf16[2,2,128,512]{3,2,1,0:T(8,128)(2,1)}, bf16[2,2,128,512]{3,2,1,0:T(8,128)(2,1)S(1)}, u32[]{:S(2)}, u32[]{:S(2)}) collective-permute-start(bf16[2,2,128,512]{3,2,1,0:T(8,128)(2,1)} %get-tuple-element.43), channel_id=1, source_target_pairs={{0,8},{8,0},{1,9},{9,1},{2,10},{10,2},{3,11},{11,3},{4,12},{12,4},... | collective-permute-start | bytes 1572872 | tf_op jit(solution)/shard_map/ppermute | solution.py:28
  159.5 9.3 %collective-permute-start.18 = (bf16[2,128,512]{2,1,0:T(8,128)(2,1)S(1)}, bf16[2,128,512]{2,1,0:T(8,128)(2,1)S(1)}, u32[]{:S(2)}, u32[]{:S(2)}) collective-permute-start(bf16[2,128,512]{2,1,0:T(8,128)(2,1)S(1)} %fusion.11), channel_id=1, source_target_pairs={{0,16},{16,0},{1,17},{17,1},{2,18},{18,2},{3,19},{19,3},{4,20},{20... | collective-permute-start | bytes 786440 | tf_op jit(solution)/shard_map/ppermute | solution.py:28
  162.3 19.2 %collective-permute-start.22 = (bf16[64,4608]{1,0:T(8,128)(2,1)S(1)}, bf16[64,4608]{1,0:T(8,128)(2,1)S(1)}, u32[]{:S(2)}, u32[]{:S(2)}) collective-permute-start(bf16[64,4608]{1,0:T(8,128)(2,1)S(1)} %fusion.1), channel_id=1, source_target_pairs={{0,16},{16,0},{1,17},{17,1},{2,18},{18,2},{3,19},{19,3},{4,20},{20... | collective-permute-start | bytes 1769480 | tf_op jit(solution)/shard_map/ppermute | solution.py:28
  163.6 28.6 %collective-permute-start.16 = (bf16[2,128,512]{2,1,0:T(8,128)(2,1)S(1)}, bf16[2,128,512]{2,1,0:T(8,128)(2,1)S(1)}, u32[]{:S(2)}, u32[]{:S(2)}) collective-permute-start(bf16[2,128,512]{2,1,0:T(8,128)(2,1)S(1)} %fusion.10), channel_id=1, source_target_pairs={{0,16},{16,0},{1,17},{17,1},{2,18},{18,2},{3,19},{19,3},{4,20},{20... | collective-permute-start | bytes 786440 | tf_op jit(solution)/shard_map/ppermute | solution.py:28
  169.6 22.6 %collective-permute-start.19 = (bf16[2,128,512]{2,1,0:T(8,128)(2,1)}, bf16[2,128,512]{2,1,0:T(8,128)(2,1)S(1)}, u32[]{:S(2)}, u32[]{:S(2)}) collective-permute-start(bf16[2,128,512]{2,1,0:T(8,128)(2,1)} %fusion.4), channel_id=1, source_target_pairs={{32,0},{64,32},{96,64},{128,96},{160,128},{192,160},{224,192},{33,... | collective-permute-start | bytes 786440 | tf_op jit(solution)/shard_map/ppermute | solution.py:28
  183.6 28.2 %all-to-all-start = ((bf16[8,8,4608]{2,1,0:T(8,128)(2,1)}), bf16[8,8,4608]{2,1,0:T(8,128)(2,1)S(1)}, u32[]{:S(2)}, u32[]{:S(2)}) async-start(bf16[8,8,4608]{2,1,0:T(8,128)(2,1)} %fusion.2), calls=%async_computation | async-start | bytes 1179648 | tf_op jit(solution)/shard_map/all_to_all | solution.py:507
  191.3 19.5 %copy-start.5 = (f32[512,128]{1,0:T(8,128)S(1)}, f32[512,128]{1,0:T(8,128)}, u32[]{:S(2)}) copy-start(f32[512,128]{1,0:T(8,128)} %copy-done.4) | copy-start | bytes 786436
  191.3 6.5 %collective-permute-start.14 = (bf16[2,128,512]{2,1,0:T(8,128)(2,1)S(1)}, bf16[2,128,512]{2,1,0:T(8,128)(2,1)S(1)}, u32[]{:S(2)}, u32[]{:S(2)}) collective-permute-start(bf16[2,128,512]{2,1,0:T(8,128)(2,1)S(1)} %fusion.9), channel_id=1, source_target_pairs={{0,16},{16,0},{1,17},{17,1},{2,18},{18,2},{3,19},{19,3},{4,20},{20... | collective-permute-start | bytes 786440 | tf_op jit(solution)/shard_map/ppermute | solution.py:28
  192.3 18.4 %collective-permute-start.20 = (bf16[2,128,512]{2,1,0:T(8,128)(2,1)S(1)}, bf16[2,128,512]{2,1,0:T(8,128)(2,1)S(1)}, u32[]{:S(2)}, u32[]{:S(2)}) collective-permute-start(bf16[2,128,512]{2,1,0:T(8,128)(2,1)S(1)} %fusion.7), channel_id=1, source_target_pairs={{32,0},{64,32},{96,64},{128,96},{160,128},{192,160},{224,192},{33,... | collective-permute-start | bytes 786440 | tf_op jit(solution)/shard_map/ppermute | solution.py:28
  (23 other events, 91.6 us)

commit v5 on v4

--- a/solution.py
+++ b/solution.py
@@ -102,18 +102,13 @@
 
 
 def forward_kernel(
-    info, q_ref, cos_ref, sin_ref, r0, r2, r1, r3, eg_ref, qr_ref, at_ref, li_ref, pt_ref, acc, pair
+    info, qr_ref, r0, r2, r1, r3, eg_ref, at_ref, li_ref, pt_ref, acc, pair
 ):
     step = pl.program_id(0)
 
     @pl.when(step == 0)
     def _():
         acc[...] = jnp.zeros_like(acc)
-        cosine = cos_ref[...]
-        sine = sin_ref[...]
-        for h in range(2):
-            x = q_ref[:, h * HD : (h + 1) * HD].astype(F32)
-            qr_ref[:, h * HD : (h + 1) * HD] = (x * cosine + pltpu.roll(x, HD // 2, 1) * sine).astype(BF16)
 
     def one(u, _):
         slot = step * PACK + u
@@ -166,7 +161,28 @@
         pt_ref[...] = tdot(pick, at_ref[...]).astype(BF16)
 
 
-def forward(info, queries, cosf, sinf, panels):
+def spin_kernel(q_ref, cos_ref, sin_ref, qr_ref):
+    for h in range(2):
+        col = slice(h * HD, (h + 1) * HD)
+        x = q_ref[:, col].astype(F32)
+        qr_ref[:, col] = (x * cos_ref[...] + pltpu.roll(x, HD // 2, 1) * sin_ref[...]).astype(BF16)
+
+
+def spin(queries, cosf, sinf):
+    whole = lambda *shape: pl.BlockSpec(shape, lambda i, *_: (0,) * len(shape))
+    return pl.pallas_call(
+        spin_kernel,
+        out_shape=jax.ShapeDtypeStruct((TOK, 2 * HD), BF16),
+        grid=(1,),
+        in_specs=[whole(TOK, 2 * HD), whole(TOK, HD), whole(TOK, HD)],
+        out_specs=whole(TOK, 2 * HD),
+        compiler_params=pltpu.CompilerParams(dimension_semantics=("arbitrary",), vmem_limit_bytes=60 << 20),
+        cost_estimate=pl.CostEstimate(flops=500_000, bytes_accessed=1_000_000, transcendentals=0),
+        name="spin",
+    )(queries, cosf, sinf)
+
+
+def forward(info, qr, panels):
     whole = lambda *shape: pl.BlockSpec(shape, lambda i, *_: (0,) * len(shape))
     sds = jax.ShapeDtypeStruct
     eg = pl.BlockSpec((PACK, 2, 2, TOK, TOK), lambda i, f: (i, 0, 0, 0, 0))
@@ -174,7 +190,6 @@
         forward_kernel,
         out_shape=(
             sds((SLOTS, 2, 2, TOK, TOK), BF16),
-            sds((TOK, 2 * HD), BF16),
             sds((TOK, 2 * HD), BF16),
             sds((TOK, 2 * HD), F32),
             sds((2 * HD, TOK), BF16),
@@ -184,13 +199,10 @@
             grid=(SLOTS // PACK,),
             in_specs=[
                 whole(TOK, 2 * HD),
-                whole(TOK, HD),
-                whole(TOK, HD),
                 *([pl.BlockSpec((1, 2, TOK, HD), lambda i, f: (i // (4 // PACK), 0, 0, 0))] * 4),
             ],
             out_specs=(
                 eg,
-                whole(TOK, 2 * HD),
                 whole(TOK, 2 * HD),
                 whole(TOK, 2 * HD),
                 whole(2 * HD, TOK),
@@ -200,7 +212,7 @@
         compiler_params=pltpu.CompilerParams(dimension_semantics=("arbitrary",), vmem_limit_bytes=46 << 20),
         cost_estimate=pl.CostEstimate(flops=10_000_000_000, bytes_accessed=24_000_000, transcendentals=10_000_000),
         name="attend",
-    )(info, queries, cosf, sinf, *panels)
+    )(info, qr, *panels)
 
 
 CARRY = (
@@ -401,8 +413,9 @@
     rows = cs[...]
     mine = pl.multiple_of(core * HD, HD)
     other = pl.multiple_of((1 - core) * HD, HD)
-    keep_ref[...] = ndot(pt_ref[pl.ds(mine, HD), :], rows)
-    send_ref[...] = ndot(pt_ref[pl.ds(other, HD), :], rows).astype(BF16)
+    both = ndot(jnp.concatenate([pt_ref[pl.ds(mine, HD), :], pt_ref[pl.ds(other, HD), :]]), rows)
+    keep_ref[...] = both[:HD]
+    send_ref[...] = both[HD:].astype(BF16)
     part = tdot(cs[pl.ds(away, HALF), :], w_ref[...])
 
     @pl.when(pl.program_id(0) == 0)
@@ -419,7 +432,7 @@
 
 
 def weight(info, cots, attn_t, w2, rows):
-    chunk = 1152
+    chunk = 2304
     sds = jax.ShapeDtypeStruct
     block = lambda n: pl.BlockSpec((n, chunk), lambda i, f: (0, i))
     whole = lambda *shape: pl.BlockSpec(shape, lambda i, *_: (0,) * len(shape))
@@ -483,17 +496,18 @@
     far = [far0]
     for d in (1, 2, 3):
         far.append(from_y(far0, d))
-    back = jnp.concatenate([behind2, behind1])
-    across = swap(back, "xl")
-    mine = jnp.concatenate([back, own])
+    beside1 = along_z(across0, 1)
+    across = swap(behind2, "xl")
+    mine = jnp.concatenate([behind2, behind1, own])
     partner1 = swap(mine, "c")
-    across = jnp.concatenate([across, across0])
+    across = jnp.concatenate([across, beside1, across0])
     partner2 = swap(across, "c")
     panels = (mine, across, partner1, partner2)
 
     w2 = jnp.transpose(out_weight, (1, 0, 2)).reshape(2 * HD, 4608)
 
-    eg, qr, attn, linv, attn_t = forward(info, queries, cosf, sinf, panels)
+    qr = spin(queries, cosf, sinf)
+    eg, attn, linv, attn_t = forward(info, qr, panels)
     rows = (qr, attn, linv, cosf, sinf)
     prev, half = backward(0, SLOTS, 1, info, rows, panels, eg, cots=near, w2=w2)
 

time: 214 us -> 200 us (0.935)
  waiting for transfers between devices: 91.2 us -> 70.9 us
  starting transfers between devices: 41.3 us -> 49.8 us
  local copies, waits for them, and re-layouts: 15.5 us -> 13 us
    ppermute x23 -> x24, waiting for transfers between devices: 91.2 us -> 70.9 us  [permute(): return lax.ppermute(x, axis, pairs)]
    ppermute x23 -> x24, starting transfers between devices: 33.8 us -> 41.9 us  [permute(): return lax.ppermute(x, axis, pairs)]
    unnamed x63 -> x62, local copies, waits for them, and re-layouts: 11.3 us -> 8.73 us
  transfers between devices with their start and end apart: 24 -> 25, of which waited for: 12 -> 10; matrix products, arithmetic and copies ran while one was open for 4% -> 4% of each run, Pallas kernels for 23% -> 25%
where the time goes in v5:
time: 200 us; the launch traced here: 199 us
  waiting for transfers between devices  70.9 us (35%)
  Pallas kernels  57.7 us (29%)
  starting transfers between devices  49.8 us (25%)
  local copies, waits for them, and re-layouts  13 us (6%)
  other arithmetic  6.5 us (3%)
    ppermute x24, waiting for transfers between devices, permute(): return lax.ppermute(x, axis, pairs)  70.9 us
    ppermute x24, starting transfers between devices, permute(): return lax.ppermute(x, axis, pairs)  41.9 us
    pallas_call x4, Pallas kernels, backward(): pl.pallas_call(kernel, out_shape=shapes, grid_spec=pltpu.PrefetchScalarGr...  34.1 us
    pallas_call x1, Pallas kernels, forward(): pl.pallas_call(forward_kernel, out_shape=(sds((SLOTS, 2, 2, TOK, TOK), BF...  12.9 us
    unnamed x62, local copies, waits for them, and re-layouts  8.73 us
    all_to_all x1, starting transfers between devices, local(): wz = lax.all_to_all(wz, 'z', 0, 0, tiled=True)  7.88 us
    pallas_call x1, Pallas kernels, weight(): pl.pallas_call(weight_kernel, out_shape=(sds((HD, 4608), F32), sds((HD, 4...  7.64 us
  transfers between devices with their start and end apart: 25, of which 10 were waited for; matrix products, arithmetic and copies ran while one was open for 4% of the time, Pallas kernels for 25%

profile of v5, /device:TPU:96, one launch (start us, length us, event | category | flops | bytes accessed | tf_op | source)
XLA Modules:
  0.0 199.0 jit_solution(16455487089866117627)
XLA Ops:
  0.7 1.7 fusion.8
  4.4 5.5 %collective-permute-start.7 = (bf16[1,2,512,128]{3,2,1,0:T(8,128)(2,1)S(1)}, bf16[1,2,512,128]{3,2,1,0:T(8,128)(2,1)S(1)}, u32[]{:S(2)}, u32[]{:S(2)}) collective-permute-start(bf16[1,2,512,128]{3,2,1,0:T(8,128)(2,1)S(1)} %turn.1), channel_id=1, source_target_pairs={{0,64},{32,96},{64,128},{96,160},{128,192},{160,224},{1,65},{33,97... | collective-permute-start | bytes 786440 | tf_op jit(solution)/shard_map/ppermute | solution.py:28
  9.9 1.6 collective-permute-start.10
  11.5 2.9 %collective-permute-start.8 = (bf16[1,2,512,128]{3,2,1,0:T(8,128)(2,1)S(1)}, bf16[1,2,512,128]{3,2,1,0:T(8,128)(2,1)S(1)}, u32[]{:S(2)}, u32[]{:S(2)}) collective-permute-start(bf16[1,2,512,128]{3,2,1,0:T(8,128)(2,1)S(1)} %turn.1), channel_id=1, source_target_pairs={{0,32},{32,64},{64,96},{96,128},{128,160},{160,192},{192,224},{1,3... | collective-permute-start | bytes 786440 | tf_op jit(solution)/shard_map/ppermute | solution.py:28
  14.4 6.1 %collective-permute-done.7 = bf16[1,2,512,128]{3,2,1,0:T(8,128)(2,1)S(1)} collective-permute-done((bf16[1,2,512,128]{3,2,1,0:T(8,128)(2,1)S(1)}, bf16[1,2,512,128]{3,2,1,0:T(8,128)(2,1)S(1)}, u32[]{:S(2)}, u32[]{:S(2)}) %collective-permute-start.7) | collective-permute-done | bytes 262176 | tf_op jit(solution)/shard_map/ppermute | solution.py:28
  20.6 1.5 collective-permute-start.9
  22.1 7.6 %collective-permute-start.11 = (bf16[1,2,512,128]{3,2,1,0:T(8,128)(2,1)S(1)}, bf16[1,2,512,128]{3,2,1,0:T(8,128)(2,1)S(1)}, u32[]{:S(2)}, u32[]{:S(2)}) collective-permute-start(bf16[1,2,512,128]{3,2,1,0:T(8,128)(2,1)S(1)} %collective-permute-done.10), channel_id=1, source_target_pairs={{0,32},{32,64},{64,96},{96,128},{128,160},{160,192},{192,224},{1,3... | collective-permute-start | bytes 786440 | tf_op jit(solution)/shard_map/ppermute | solution.py:28
  29.9 3.8 %collective-permute-done.11 = bf16[1,2,512,128]{3,2,1,0:T(8,128)(2,1)S(1)} collective-permute-done((bf16[1,2,512,128]{3,2,1,0:T(8,128)(2,1)S(1)}, bf16[1,2,512,128]{3,2,1,0:T(8,128)(2,1)S(1)}, u32[]{:S(2)}, u32[]{:S(2)}) %collective-permute-start.11) | collective-permute-done | bytes 262176 | tf_op jit(solution)/shard_map/ppermute | solution.py:28
  33.9 3.1 %collective-permute-start.3 = (bf16[64,4608]{1,0:T(8,128)(2,1)}, bf16[64,4608]{1,0:T(8,128)(2,1)}, u32[]{:S(2)}, u32[]{:S(2)}) collective-permute-start(bf16[64,4608]{1,0:T(8,128)(2,1)} %refs_1_.1), channel_id=1, source_target_pairs={{0,4},{4,0},{1,5},{5,1},{2,6},{6,2},{3,7},{7,3},{8,12},{12,8},{9,1... | collective-permute-start | bytes 1769480 | tf_op jit(solution)/shard_map/ppermute | solution.py:28
  37.0 3.0 %collective-permute-start = (bf16[64,4608]{1,0:T(8,128)(2,1)}, bf16[64,4608]{1,0:T(8,128)(2,1)}, u32[]{:S(2)}, u32[]{:S(2)}) collective-permute-start(bf16[64,4608]{1,0:T(8,128)(2,1)} %refs_1_.1), channel_id=1, source_target_pairs={{1,0},{2,1},{3,2},{0,3},{5,4},{6,5},{7,6},{4,7},{9,8},{10,9},{11,1... | collective-permute-start | bytes 1769480 | tf_op jit(solution)/shard_map/ppermute | solution.py:28
  40.7 2.0 spin.1.qr_ref.refs_10_.refs_6_
  42.7 3.3 %copy.12 = bf16[2,128,4608]{2,1,0:T(8,128)(2,1)} copy(bf16[2,128,4608]{2,0,1:T(2,128)(2,1)} %bitcast.43) | data formatting | bytes 4718592 | tf_op jit(solution)/shard_map/transpose | solution.py:507
  46.1 5.4 %collective-permute-done.3.refs_4_ = bf16[64,4608]{1,0:T(8,128)(2,1)} collective-permute-done((bf16[64,4608]{1,0:T(8,128)(2,1)}, bf16[64,4608]{1,0:T(8,128)(2,1)}, u32[]{:S(2)}, u32[]{:S(2)}) %collective-permute-start.3) | collective-permute-done | bytes 589856 | tf_op jit(solution)/shard_map/ppermute | solution.py:28
  51.5 1.6 collective-permute-start.2
  53.1 12.8 %collective-permute-done.refs_1_.refs_2_ = bf16[64,4608]{1,0:T(8,128)(2,1)} collective-permute-done((bf16[64,4608]{1,0:T(8,128)(2,1)}, bf16[64,4608]{1,0:T(8,128)(2,1)}, u32[]{:S(2)}, u32[]{:S(2)}) %collective-permute-start) | collective-permute-done | bytes 589856 | tf_op jit(solution)/shard_map/ppermute | solution.py:28
  65.9 3.7 %collective-permute-start.4 = (bf16[64,4608]{1,0:T(8,128)(2,1)}, bf16[64,4608]{1,0:T(8,128)(2,1)S(1)}, u32[]{:S(2)}, u32[]{:S(2)}) collective-permute-start(bf16[64,4608]{1,0:T(8,128)(2,1)} %collective-permute-done.3.refs_4_), channel_id=1, source_target_pairs={{1,0},{2,1},{3,2},{0,3},{5,4},{6,5},{7,6},{4,7},{9,8},{10,9},{11,1... | collective-permute-start | bytes 1769480 | tf_op jit(solution)/shard_map/ppermute | solution.py:28
  70.6 12.9 %attend.1 = (bf16[12,2,2,512,512]{4,3,2,1,0:T(8,128)(2,1)}, bf16[512,256]{1,0:T(8,128)(2,1)S(1)}, f32[512,256]{1,0:T(8,128)S(1)}, bf16[256,512]{1,0:T(8,128)(2,1)S(1)}) custom-call(s32[5]{0:T(128)S(1)} %stack.23.info.refs_0_, bf16[512,256]{1,0:T(8,128)(2,1)S(1)} %copy-done.12, ...), custom_call_target="tpu_custom_call" | custom-call | flops 10000000000 | bytes 24000000 | tf_op jit(solution)/shard_map/attend/pallas_call | solution.py:189
  85.7 8.9 %collective-permute-done.4.refs_5_ = bf16[64,4608]{1,0:T(8,128)(2,1)S(1)} collective-permute-done((bf16[64,4608]{1,0:T(8,128)(2,1)}, bf16[64,4608]{1,0:T(8,128)(2,1)S(1)}, u32[]{:S(2)}, u32[]{:S(2)}) %collective-permute-start.4) | collective-permute-done | bytes 589856 | tf_op jit(solution)/shard_map/ppermute | solution.py:28
  94.6 3.6 %collective-permute-done.6.refs_7_ = bf16[64,4608]{1,0:T(8,128)(2,1)S(1)} collective-permute-done((bf16[64,4608]{1,0:T(8,128)(2,1)}, bf16[64,4608]{1,0:T(8,128)(2,1)S(1)}, u32[]{:S(2)}, u32[]{:S(2)}) %collective-permute-start.6) | collective-permute-done | bytes 589856 | tf_op jit(solution)/shard_map/ppermute | solution.py:28
  99.0 7.6 %weigh.1 = (f32[128,4608]{1,0:T(8,128)}, bf16[128,4608]{1,0:T(8,128)(2,1)}, bf16[256,256]{1,0:T(8,128)(2,1)}, f32[2,256,128]{2,1,0:T(8,128)}, bf16[2,128,256]{2,...) custom-call(s32[5]{0:T(128)} %copy-done.21, bf16[64,4608]{1,0:T(8,128)(2,1)} %refs_1_.1, ...), custom_call_target="tpu_custom_call" | custom-call | flops 1900000000 | bytes 11000000 | tf_op jit(solution)/shard_map/weigh/pallas_call | solution.py:440
  109.9 13.9 %shard_map.102 = (bf16[12,2,128,512]{3,2,1,0:T(8,128)(2,1)}, f32[512,256]{1,0:T(8,128)}) custom-call(s32[5]{0:T(128)S(1)} %copy-done.22, bf16[64,4608]{1,0:T(8,128)(2,1)} %refs_1_.1, bf16[64,4608]{1,0:T(8,128)(2,1)} %collective-permute-done.refs_1_.refs_2_, bf16[64,4608]{1,0:T(8,128)(2,1)} %collective-permute-done.1.refs_2_.refs_3_, ...), custom_call_target="tpu_custom_call" | custom-call | flops 8400000000 | bytes 24000000 | tf_op jit(solution)/shard_map/pallas_call | solution.py:385
  123.8 7.2 %shard_map.103 = (bf16[2,2,128,512]{3,2,1,0:T(8,128)(2,1)}, bf16[2,2,128,512]{3,2,1,0:T(8,128)(2,1)}, f32[2,256,128]{2,1,0:T(8,128)}) custom-call(s32[5]{0:T(128)} %copy-done.21, bf16[256,256]{1,0:T(8,128)(2,1)} %get-tuple-element.30.refs_1_, f32[2,256,128]{2,1,0:T(8,128)} %get-tuple-element.31.refs_2_, bf16[2,128,256]{2,1,0:T(8,128)(2,1)} %get-tuple-element.32.refs_3_, ...), custom_call_target="tpu_custom_call" | custom-call | flops 2800000000 | bytes 8000000 | tf_op jit(solution)/shard_map/pallas_call | solution.py:385
  131.1 7.4 %shard_map.104 = (bf16[2,2,128,512]{3,2,1,0:T(8,128)(2,1)}, bf16[2,2,128,512]{3,2,1,0:T(8,128)(2,1)}, f32[2,256,128]{2,1,0:T(8,128)}) custom-call(s32[5]{0:T(128)} %copy-done.21, bf16[256,256]{1,0:T(8,128)(2,1)} %get-tuple-element.30.refs_1_, f32[2,256,128]{2,1,0:T(8,128)} %get-tuple-element.31.refs_2_, bf16[2,128,256]{2,1,0:T(8,128)(2,1)} %get-tuple-element.32.refs_3_, ...), custom_call_target="tpu_custom_call" | custom-call | flops 2800000000 | bytes 8000000 | tf_op jit(solution)/shard_map/pallas_call | solution.py:385
  139.0 5.5 %shard_map.105 = (bf16[2,2,128,512]{3,2,1,0:T(8,128)(2,1)}, bf16[2,2,128,512]{3,2,1,0:T(8,128)(2,1)}, f32[512,256]{1,0:T(8,128)}) custom-call(s32[5]{0:T(128)} %copy-done.21, bf16[256,256]{1,0:T(8,128)(2,1)} %get-tuple-element.30.refs_1_, f32[2,256,128]{2,1,0:T(8,128)} %get-tuple-element.31.refs_2_, ...), custom_call_target="tpu_custom_call", output_to_operand_aliasing={{2}: (15, {})} | custom-call | flops 2800000000 | bytes 8000000 | tf_op jit(solution)/shard_map/pallas_call | solution.py:385
  150.9 3.9 %collective-permute-done.19 = bf16[2,128,512]{2,1,0:T(8,128)(2,1)S(1)} collective-permute-done((bf16[2,128,512]{2,1,0:T(8,128)(2,1)S(1)}, bf16[2,128,512]{2,1,0:T(8,128)(2,1)S(1)}, u32[]{:S(2)}, u32[]{:S(2)}) %collective-permute-start.19) | collective-permute-done | bytes 262176 | tf_op jit(solution)/shard_map/ppermute | solution.py:28
  155.6 1.9 collective-permute-start.20
  157.5 10.0 %collective-permute-done.23 = bf16[64,4608]{1,0:T(8,128)(2,1)S(1)} collective-permute-done((bf16[64,4608]{1,0:T(8,128)(2,1)S(1)}, bf16[64,4608]{1,0:T(8,128)(2,1)S(1)}, u32[]{:S(2)}, u32[]{:S(2)}) %collective-permute-start.23) | collective-permute-done | bytes 589856 | tf_op jit(solution)/shard_map/ppermute | solution.py:28
  167.5 2.1 %fusion.2 = bf16[8,8,4608]{2,1,0:T(8,128)(2,1)} fusion(bf16[64,4608]{1,0:T(8,128)(2,1)S(1)} %collective-permute-done.23, f32[2,64,4608]{2,1,0:T(8,128)S(1)} %bitcast.42, s32[]{:T(128)S(6)} %select_n.10, bf16[2,64,4608]{2,1,0:T(8,128)(2,1)} %bitcast.13), kind=kLoop, calls=%fused_computation.9 | loop fusion | flops 1474560 | bytes 2949124 | tf_op jit(solution)/shard_map/reshape | solution.py:520
  169.6 7.9 %all-to-all-start = ((bf16[8,8,4608]{2,1,0:T(8,128)(2,1)}), bf16[8,8,4608]{2,1,0:T(8,128)(2,1)S(1)}, u32[]{:S(2)}, u32[]{:S(2)}) async-start(bf16[8,8,4608]{2,1,0:T(8,128)(2,1)} %fusion.2), calls=%async_computation | async-start | bytes 1179648 | tf_op jit(solution)/shard_map/all_to_all | solution.py:521
  178.4 2.5 %collective-permute-start.21 = (bf16[2,128,512]{2,1,0:T(8,128)(2,1)S(1)}, bf16[2,128,512]{2,1,0:T(8,128)(2,1)S(1)}, u32[]{:S(2)}, u32[]{:S(2)}) collective-permute-start(bf16[2,128,512]{2,1,0:T(8,128)(2,1)S(1)} %fusion.7), channel_id=1, source_target_pairs={{32,0},{64,32},{96,64},{128,96},{160,128},{192,160},{224,192},{33,... | collective-permute-start | bytes 786440 | tf_op jit(solution)/shard_map/ppermute | solution.py:28
  180.8 3.3 %collective-permute-done.15.left_ref = bf16[2,128,512]{2,1,0:T(8,128)(2,1)S(1)} collective-permute-done((bf16[2,128,512]{2,1,0:T(8,128)(2,1)S(1)}, bf16[2,128,512]{2,1,0:T(8,128)(2,1)S(1)}, u32[]{:S(2)}, u32[]{:S(2)}) %collective-permute-start.15) | collective-permute-done | bytes 262176 | tf_op jit(solution)/shard_map/ppermute | solution.py:28
  184.2 13.0 %collective-permute-done.21.down_ref = bf16[2,128,512]{2,1,0:T(8,128)(2,1)S(1)} collective-permute-done((bf16[2,128,512]{2,1,0:T(8,128)(2,1)S(1)}, bf16[2,128,512]{2,1,0:T(8,128)(2,1)S(1)}, u32[]{:S(2)}, u32[]{:S(2)}) %collective-permute-start.21) | collective-permute-done | bytes 262176 | tf_op jit(solution)/shard_map/ppermute | solution.py:28
  (107 shorter events, 20.7 us)
Async XLA Ops:
  2.3 27.5 %copy-start.4 = (f32[512,128]{1,0:T(8,128)}, f32[512,128]{1,0:T(8,128)S(1)}, u32[]{:S(2)}) copy-start(f32[512,128]{1,0:T(8,128)S(1)} %get-tuple-element.50.sin_ref.refs_10_.refs_8_) | copy-start | bytes 786436
  4.4 16.1 %collective-permute-start.7 = (bf16[1,2,512,128]{3,2,1,0:T(8,128)(2,1)S(1)}, bf16[1,2,512,128]{3,2,1,0:T(8,128)(2,1)S(1)}, u32[]{:S(2)}, u32[]{:S(2)}) collective-permute-start(bf16[1,2,512,128]{3,2,1,0:T(8,128)(2,1)S(1)} %turn.1), channel_id=1, source_target_pairs={{0,64},{32,96},{64,128},{96,160},{128,192},{160,224},{1,65},{33,97... | collective-permute-start | bytes 786440 | tf_op jit(solution)/shard_map/ppermute | solution.py:28
  9.9 12.1 %collective-permute-start.10 = (bf16[1,2,512,128]{3,2,1,0:T(8,128)(2,1)S(1)}, bf16[1,2,512,128]{3,2,1,0:T(8,128)(2,1)S(1)}, u32[]{:S(2)}, u32[]{:S(2)}) collective-permute-start(bf16[1,2,512,128]{3,2,1,0:T(8,128)(2,1)S(1)} %turn.1), channel_id=1, source_target_pairs={{0,16},{16,0},{1,17},{17,1},{2,18},{18,2},{3,19},{19,3},{4,20},{20... | collective-permute-start | bytes 786440 | tf_op jit(solution)/shard_map/ppermute | solution.py:28
  11.5 18.2 %collective-permute-start.8 = (bf16[1,2,512,128]{3,2,1,0:T(8,128)(2,1)S(1)}, bf16[1,2,512,128]{3,2,1,0:T(8,128)(2,1)S(1)}, u32[]{:S(2)}, u32[]{:S(2)}) collective-permute-start(bf16[1,2,512,128]{3,2,1,0:T(8,128)(2,1)S(1)} %turn.1), channel_id=1, source_target_pairs={{0,32},{32,64},{64,96},{96,128},{128,160},{160,192},{192,224},{1,3... | collective-permute-start | bytes 786440 | tf_op jit(solution)/shard_map/ppermute | solution.py:28
  20.6 9.3 %collective-permute-start.9 = (bf16[1,2,512,128]{3,2,1,0:T(8,128)(2,1)S(1)}, bf16[1,2,512,128]{3,2,1,0:T(8,128)(2,1)S(1)}, u32[]{:S(2)}, u32[]{:S(2)}) collective-permute-start(bf16[1,2,512,128]{3,2,1,0:T(8,128)(2,1)S(1)} %collective-permute-done.7), channel_id=1, source_target_pairs={{0,16},{16,0},{1,17},{17,1},{2,18},{18,2},{3,19},{19,3},{4,20},{20... | collective-permute-start | bytes 786440 | tf_op jit(solution)/shard_map/ppermute | solution.py:28
  22.1 11.7 %collective-permute-start.11 = (bf16[1,2,512,128]{3,2,1,0:T(8,128)(2,1)S(1)}, bf16[1,2,512,128]{3,2,1,0:T(8,128)(2,1)S(1)}, u32[]{:S(2)}, u32[]{:S(2)}) collective-permute-start(bf16[1,2,512,128]{3,2,1,0:T(8,128)(2,1)S(1)} %collective-permute-done.10), channel_id=1, source_target_pairs={{0,32},{32,64},{64,96},{96,128},{128,160},{160,192},{192,224},{1,3... | collective-permute-start | bytes 786440 | tf_op jit(solution)/shard_map/ppermute | solution.py:28
  29.8 77.0 %copy-start = (bf16[3,2,512,128]{3,2,1,0:T(8,128)(2,1)}, bf16[3,2,512,128]{3,2,1,0:T(8,128)(2,1)S(1)}, u32[]{:S(2)}) copy-start(bf16[3,2,512,128]{3,2,1,0:T(8,128)(2,1)S(1)} %pad_maximum_fusion.r0.refs_11_.refs_5_.refs_6_.refs_9_) | copy-start | bytes 2359300
  29.8 39.8 %collective-permute-start.12 = (bf16[3,2,512,128]{3,2,1,0:T(8,128)(2,1)S(1)}, bf16[3,2,512,128]{3,2,1,0:T(8,128)(2,1)S(1)}, u32[]{:S(2)}, u32[]{:S(2)}) collective-permute-start(bf16[3,2,512,128]{3,2,1,0:T(8,128)(2,1)S(1)} %pad_maximum_fusion.r0.refs_11_.refs_5_.refs_6_.refs_9_), channel_id=1, source_target_pairs={{0,8},{8,0},{1,9},{9,1},{2,10},{10,2},{3,11},{11,3},{4,12},{12,4},... | collective-permute-start | bytes 2359304 | tf_op jit(solution)/shard_map/ppermute | solution.py:28
  33.8 72.9 %copy-start.1 = (bf16[3,2,512,128]{3,2,1,0:T(8,128)(2,1)}, bf16[3,2,512,128]{3,2,1,0:T(8,128)(2,1)S(1)}, u32[]{:S(2)}) copy-start(bf16[3,2,512,128]{3,2,1,0:T(8,128)(2,1)S(1)} %constant_dynamic-update-slice_fusion.r2.refs_12_.refs_6_.refs_7_.refs_10_) | copy-start | bytes 2359300
  33.8 35.8 %collective-permute-start.13 = (bf16[3,2,512,128]{3,2,1,0:T(8,128)(2,1)S(1)}, bf16[3,2,512,128]{3,2,1,0:T(8,128)(2,1)S(1)}, u32[]{:S(2)}, u32[]{:S(2)}) collective-permute-start(bf16[3,2,512,128]{3,2,1,0:T(8,128)(2,1)S(1)} %constant_dynamic-update-slice_fusion.r2.refs_12_.refs_6_.refs_7_.refs_10_), channel_id=1, source_target_pairs={{0,8},{8,0},{1,9},{9,1},{2,10},{10,2},{3,11},{11,3},{4,12},{12,4},... | collective-permute-start | bytes 2359304 | tf_op jit(solution)/shard_map/ppermute | solution.py:28
  33.9 17.6 %collective-permute-start.3 = (bf16[64,4608]{1,0:T(8,128)(2,1)}, bf16[64,4608]{1,0:T(8,128)(2,1)}, u32[]{:S(2)}, u32[]{:S(2)}) collective-permute-start(bf16[64,4608]{1,0:T(8,128)(2,1)} %refs_1_.1), channel_id=1, source_target_pairs={{0,4},{4,0},{1,5},{5,1},{2,6},{6,2},{3,7},{7,3},{8,12},{12,8},{9,1... | collective-permute-start | bytes 1769480 | tf_op jit(solution)/shard_map/ppermute | solution.py:28
  37.0 28.9 %collective-permute-start = (bf16[64,4608]{1,0:T(8,128)(2,1)}, bf16[64,4608]{1,0:T(8,128)(2,1)}, u32[]{:S(2)}, u32[]{:S(2)}) collective-permute-start(bf16[64,4608]{1,0:T(8,128)(2,1)} %refs_1_.1), channel_id=1, source_target_pairs={{1,0},{2,1},{3,2},{0,3},{5,4},{6,5},{7,6},{4,7},{9,8},{10,9},{11,1... | collective-permute-start | bytes 1769480 | tf_op jit(solution)/shard_map/ppermute | solution.py:28
  40.1 45.6 %collective-permute-start.1 = (bf16[64,4608]{1,0:T(8,128)(2,1)}, bf16[64,4608]{1,0:T(8,128)(2,1)}, u32[]{:S(2)}, u32[]{:S(2)}) collective-permute-start(bf16[64,4608]{1,0:T(8,128)(2,1)} %refs_1_.1), channel_id=1, source_target_pairs={{2,0},{3,1},{0,2},{1,3},{6,4},{7,5},{4,6},{5,7},{10,8},{11,9},{8,1... | collective-permute-start | bytes 1769480 | tf_op jit(solution)/shard_map/ppermute | solution.py:28
  42.7 27.9 %copy-start.12 = (bf16[512,256]{1,0:T(8,128)(2,1)S(1)}, bf16[512,256]{1,0:T(8,128)(2,1)}, u32[]{:S(2)}) copy-start(bf16[512,256]{1,0:T(8,128)(2,1)} %spin.1.qr_ref.refs_10_.refs_6_) | copy-start | bytes 786436
  46.1 37.4 %copy-start.21 = (s32[5]{0:T(128)}, s32[5]{0:T(128)S(1)}, u32[]{:S(2)}) copy-start(s32[5]{0:T(128)S(1)} %stack.23.info.refs_0_) | copy-start | bytes 64
  51.5 34.2 %collective-permute-start.2 = (bf16[64,4608]{1,0:T(8,128)(2,1)}, bf16[64,4608]{1,0:T(8,128)(2,1)S(1)}, u32[]{:S(2)}, u32[]{:S(2)}) collective-permute-start(bf16[64,4608]{1,0:T(8,128)(2,1)} %refs_1_.1), channel_id=1, source_target_pairs={{3,0},{0,1},{1,2},{2,3},{7,4},{4,5},{5,6},{6,7},{11,8},{8,9},{9,10... | collective-permute-start | bytes 1769480 | tf_op jit(solution)/shard_map/ppermute | solution.py:28
  65.9 28.7 %collective-permute-start.4 = (bf16[64,4608]{1,0:T(8,128)(2,1)}, bf16[64,4608]{1,0:T(8,128)(2,1)S(1)}, u32[]{:S(2)}, u32[]{:S(2)}) collective-permute-start(bf16[64,4608]{1,0:T(8,128)(2,1)} %collective-permute-done.3.refs_4_), channel_id=1, source_target_pairs={{1,0},{2,1},{3,2},{0,3},{5,4},{6,5},{7,6},{4,7},{9,8},{10,9},{11,1... | collective-permute-start | bytes 1769480 | tf_op jit(solution)/shard_map/ppermute | solution.py:28
  69.6 37.2 %copy-start.2 = (bf16[3,2,512,128]{3,2,1,0:T(8,128)(2,1)}, bf16[3,2,512,128]{3,2,1,0:T(8,128)(2,1)S(1)}, u32[]{:S(2)}) copy-start(bf16[3,2,512,128]{3,2,1,0:T(8,128)(2,1)S(1)} %collective-permute-done.12.r1.refs_13_.refs_7_.refs_8_.refs_11_) | copy-start | bytes 2359300
  69.6 25.0 %collective-permute-start.5 = (bf16[64,4608]{1,0:T(8,128)(2,1)}, bf16[64,4608]{1,0:T(8,128)(2,1)S(1)}, u32[]{:S(2)}, u32[]{:S(2)}) collective-permute-start(bf16[64,4608]{1,0:T(8,128)(2,1)} %collective-permute-done.3.refs_4_), channel_id=1, source_target_pairs={{2,0},{3,1},{0,2},{1,3},{6,4},{7,5},{4,6},{5,7},{10,8},{11,9},{8,1... | collective-permute-start | bytes 1769480 | tf_op jit(solution)/shard_map/ppermute | solution.py:28
  69.6 37.2 %copy-start.3 = (bf16[3,2,512,128]{3,2,1,0:T(8,128)(2,1)}, bf16[3,2,512,128]{3,2,1,0:T(8,128)(2,1)S(1)}, u32[]{:S(2)}) copy-start(bf16[3,2,512,128]{3,2,1,0:T(8,128)(2,1)S(1)} %collective-permute-done.13.r3.refs_14_.refs_8_.refs_9_.refs_12_) | copy-start | bytes 2359300
  69.6 28.5 %collective-permute-start.6 = (bf16[64,4608]{1,0:T(8,128)(2,1)}, bf16[64,4608]{1,0:T(8,128)(2,1)S(1)}, u32[]{:S(2)}, u32[]{:S(2)}) collective-permute-start(bf16[64,4608]{1,0:T(8,128)(2,1)} %collective-permute-done.3.refs_4_), channel_id=1, source_target_pairs={{3,0},{0,1},{1,2},{2,3},{7,4},{4,5},{5,6},{6,7},{11,8},{8,9},{9,10... | collective-permute-start | bytes 1769480 | tf_op jit(solution)/shard_map/ppermute | solution.py:28
  106.7 39.8 %collective-permute-start.22 = (bf16[128,4608]{1,0:T(8,128)(2,1)}, bf16[128,4608]{1,0:T(8,128)(2,1)}, u32[]{:S(2)}, u32[]{:S(2)}) collective-permute-start(bf16[128,4608]{1,0:T(8,128)(2,1)} %get-tuple-element.49), channel_id=1, source_target_pairs={{0,8},{8,0},{1,9},{9,1},{2,10},{10,2},{3,11},{11,3},{4,12},{12,4},... | collective-permute-start | bytes 3538952 | tf_op jit(solution)/shard_map/ppermute | solution.py:28
  131.1 14.3 %collective-permute-start.18 = (bf16[2,2,128,512]{3,2,1,0:T(8,128)(2,1)}, bf16[2,2,128,512]{3,2,1,0:T(8,128)(2,1)S(1)}, u32[]{:S(2)}, u32[]{:S(2)}) collective-permute-start(bf16[2,2,128,512]{3,2,1,0:T(8,128)(2,1)} %get-tuple-element.45), channel_id=1, source_target_pairs={{0,8},{8,0},{1,9},{9,1},{2,10},{10,2},{3,11},{11,3},{4,12},{12,4},... | collective-permute-start | bytes 1572872 | tf_op jit(solution)/shard_map/ppermute | solution.py:28
  138.5 10.9 %collective-permute-start.16 = (bf16[2,2,128,512]{3,2,1,0:T(8,128)(2,1)}, bf16[2,2,128,512]{3,2,1,0:T(8,128)(2,1)S(1)}, u32[]{:S(2)}, u32[]{:S(2)}) collective-permute-start(bf16[2,2,128,512]{3,2,1,0:T(8,128)(2,1)} %get-tuple-element.43), channel_id=1, source_target_pairs={{0,8},{8,0},{1,9},{9,1},{2,10},{10,2},{3,11},{11,3},{4,12},{12,4},... | collective-permute-start | bytes 1572872 | tf_op jit(solution)/shard_map/ppermute | solution.py:28
  144.5 32.9 %collective-permute-start.14 = (bf16[2,2,128,512]{3,2,1,0:T(8,128)(2,1)}, bf16[2,2,128,512]{3,2,1,0:T(8,128)(2,1)S(1)}, u32[]{:S(2)}, u32[]{:S(2)}) collective-permute-start(bf16[2,2,128,512]{3,2,1,0:T(8,128)(2,1)} %get-tuple-element.41), channel_id=1, source_target_pairs={{0,8},{8,0},{1,9},{9,1},{2,10},{10,2},{3,11},{11,3},{4,12},{12,4},... | collective-permute-start | bytes 1572872 | tf_op jit(solution)/shard_map/ppermute | solution.py:28
  145.6 9.3 %collective-permute-start.19 = (bf16[2,128,512]{2,1,0:T(8,128)(2,1)S(1)}, bf16[2,128,512]{2,1,0:T(8,128)(2,1)S(1)}, u32[]{:S(2)}, u32[]{:S(2)}) collective-permute-start(bf16[2,128,512]{2,1,0:T(8,128)(2,1)S(1)} %fusion.11), channel_id=1, source_target_pairs={{0,16},{16,0},{1,17},{17,1},{2,18},{18,2},{3,19},{19,3},{4,20},{20... | collective-permute-start | bytes 786440 | tf_op jit(solution)/shard_map/ppermute | solution.py:28
  148.3 19.2 %collective-permute-start.23 = (bf16[64,4608]{1,0:T(8,128)(2,1)S(1)}, bf16[64,4608]{1,0:T(8,128)(2,1)S(1)}, u32[]{:S(2)}, u32[]{:S(2)}) collective-permute-start(bf16[64,4608]{1,0:T(8,128)(2,1)S(1)} %fusion.1), channel_id=1, source_target_pairs={{0,16},{16,0},{1,17},{17,1},{2,18},{18,2},{3,19},{19,3},{4,20},{20... | collective-permute-start | bytes 1769480 | tf_op jit(solution)/shard_map/ppermute | solution.py:28
  149.6 28.6 %collective-permute-start.17 = (bf16[2,128,512]{2,1,0:T(8,128)(2,1)S(1)}, bf16[2,128,512]{2,1,0:T(8,128)(2,1)S(1)}, u32[]{:S(2)}, u32[]{:S(2)}) collective-permute-start(bf16[2,128,512]{2,1,0:T(8,128)(2,1)S(1)} %fusion.10), channel_id=1, source_target_pairs={{0,16},{16,0},{1,17},{17,1},{2,18},{18,2},{3,19},{19,3},{4,20},{20... | collective-permute-start | bytes 786440 | tf_op jit(solution)/shard_map/ppermute | solution.py:28
  155.6 22.6 %collective-permute-start.20 = (bf16[2,128,512]{2,1,0:T(8,128)(2,1)}, bf16[2,128,512]{2,1,0:T(8,128)(2,1)S(1)}, u32[]{:S(2)}, u32[]{:S(2)}) collective-permute-start(bf16[2,128,512]{2,1,0:T(8,128)(2,1)} %fusion.4), channel_id=1, source_target_pairs={{32,0},{64,32},{96,64},{128,96},{160,128},{192,160},{224,192},{33,... | collective-permute-start | bytes 786440 | tf_op jit(solution)/shard_map/ppermute | solution.py:28
  169.6 28.6 %all-to-all-start = ((bf16[8,8,4608]{2,1,0:T(8,128)(2,1)}), bf16[8,8,4608]{2,1,0:T(8,128)(2,1)S(1)}, u32[]{:S(2)}, u32[]{:S(2)}) async-start(bf16[8,8,4608]{2,1,0:T(8,128)(2,1)} %fusion.2), calls=%async_computation | async-start | bytes 1179648 | tf_op jit(solution)/shard_map/all_to_all | solution.py:521
  177.7 6.5 %collective-permute-start.15 = (bf16[2,128,512]{2,1,0:T(8,128)(2,1)S(1)}, bf16[2,128,512]{2,1,0:T(8,128)(2,1)S(1)}, u32[]{:S(2)}, u32[]{:S(2)}) collective-permute-start(bf16[2,128,512]{2,1,0:T(8,128)(2,1)S(1)} %fusion.9), channel_id=1, source_target_pairs={{0,16},{16,0},{1,17},{17,1},{2,18},{18,2},{3,19},{19,3},{4,20},{20... | collective-permute-start | bytes 786440 | tf_op jit(solution)/shard_map/ppermute | solution.py:28
  178.4 18.8 %collective-permute-start.21 = (bf16[2,128,512]{2,1,0:T(8,128)(2,1)S(1)}, bf16[2,128,512]{2,1,0:T(8,128)(2,1)S(1)}, u32[]{:S(2)}, u32[]{:S(2)}) collective-permute-start(bf16[2,128,512]{2,1,0:T(8,128)(2,1)S(1)} %fusion.7), channel_id=1, source_target_pairs={{32,0},{64,32},{96,64},{128,96},{160,128},{192,160},{224,192},{33,... | collective-permute-start | bytes 786440 | tf_op jit(solution)/shard_map/ppermute | solution.py:28
  (23 other events, 143.7 us)

commit v6 on v5

--- a/solution.py
+++ b/solution.py
@@ -453,26 +453,26 @@
     )(info, *cots, attn_t, w2, *rows[:3])
 
 
-def settle_kernel(own_ref, left_ref, down_ref, cos_ref, sin_ref, kg_ref, vg_ref):
-    both = own_ref[0] + left_ref[...].astype(F32) + down_ref[...].astype(F32)
+def settle_kernel(keep_ref, got_ref, left_ref, down_ref, cos_ref, sin_ref, kg_ref, vg_ref):
+    both = keep_ref[0].astype(F32) + got_ref[0].astype(F32) + left_ref[...].astype(F32) + down_ref[...].astype(F32)
     g = both[0].T
     kg_ref[...] = g * cos_ref[...] - pltpu.roll(g, HD // 2, 1) * sin_ref[...]
     vg_ref[...] = both[1].T
 
 
-def settle(both, left, down, cosf, sinf):
+def settle(keep, got, left, down, cosf, sinf):
     whole = lambda *shape: pl.BlockSpec(shape, lambda i, *_: (0,) * len(shape))
     sds = jax.ShapeDtypeStruct
     return pl.pallas_call(
         settle_kernel,
         out_shape=(sds((TOK, HD), F32), sds((TOK, HD), F32)),
         grid=(1,),
-        in_specs=[whole(1, 2, HD, TOK), whole(2, HD, TOK), whole(2, HD, TOK), whole(TOK, HD), whole(TOK, HD)],
+        in_specs=[whole(1, 2, HD, TOK)] * 2 + [whole(2, HD, TOK)] * 2 + [whole(TOK, HD)] * 2,
         out_specs=(whole(TOK, HD), whole(TOK, HD)),
         compiler_params=pltpu.CompilerParams(dimension_semantics=("arbitrary",), vmem_limit_bytes=46 << 20),
         cost_estimate=pl.CostEstimate(flops=500_000, bytes_accessed=2_000_000, transcendentals=0),
         name="settle",
-    )(both, left, down, cosf, sinf)
+    )(keep, got, left, down, cosf, sinf)
 
 
 def local(queries, keys, values, out_weight, cotangent):
@@ -496,11 +496,11 @@
     far = [far0]
     for d in (1, 2, 3):
         far.append(from_y(far0, d))
-    beside1 = along_z(across0, 1)
-    across = swap(behind2, "xl")
-    mine = jnp.concatenate([behind2, behind1, own])
+    back = jnp.concatenate([behind2, behind1])
+    across = swap(back, "xl")
+    mine = jnp.concatenate([back, own])
     partner1 = swap(mine, "c")
-    across = jnp.concatenate([across, beside1, across0])
+    across = jnp.concatenate([across, across0])
     partner2 = swap(across, "c")
     panels = (mine, across, partner1, partner2)
 
@@ -530,13 +530,13 @@
         keep, send, last = out
         carry = [*carry[:4], last]
         got = swap(send, "c")
-        both = keep.astype(F32) + got.astype(F32)
-        give = both[1].astype(BF16)
+        give = (keep[1].astype(F32) + got[1].astype(F32)).astype(BF16)
         turned = swap(give, "xl")
-        total.append((both, turned))
+        total.append((keep, got, turned))
+    wide = lambda keep, got, turned: keep[0].astype(F32) + got[0].astype(F32) + turned.astype(F32)
     query_grad = last
-    down1 = along_z((total[0][0][0] + total[0][1].astype(F32)).astype(BF16), -1)
-    down0 = along_z((total[1][0][0] + total[1][1].astype(F32) + down1.astype(F32)).astype(BF16), -1)
+    down1 = along_z(wide(*total[0]).astype(BF16), -1)
+    down0 = along_z((wide(*total[1]) + down1.astype(F32)).astype(BF16), -1)
     key_grad, value_grad = settle(*total[2], down0, cosf, sinf)
     return query_grad, key_grad, value_grad, weight_grad
 

time: 200 us -> 213 us (1.065)
  waiting for transfers between devices: 70.9 us -> 89.2 us
  starting transfers between devices: 49.8 us -> 40.4 us
  other arithmetic: 6.5 us -> 11.2 us
    ppermute x24 -> x23, waiting for transfers between devices: 70.9 us -> 89.2 us  [permute(): return lax.ppermute(x, axis, pairs)]
    ppermute x24 -> x23, starting transfers between devices: 41.9 us -> 32.9 us  [permute(): return lax.ppermute(x, axis, pairs)]
    convert_element_type x2 -> x5, other arithmetic: 0.87 us -> 5.87 us  [the longest x3 3.58 us: local(): give = (keep[1].astype(F32) + got[1].astype(F32)).astype(BF16)]
    unnamed x62 -> x63, local copies, waits for them, and re-layouts: 8.73 us -> 8.14 us
  transfers between devices with their start and end apart: 25 -> 24, of which waited for: 10 -> 12; matrix products, arithmetic and copies ran while one was open for 4% -> 6% of each run, Pallas kernels for 25% -> 24%
where the time goes in v6:
time: 213 us; the launch traced here: 212 us
  waiting for transfers between devices  89.2 us (42%)
  Pallas kernels  57.9 us (27%)
  starting transfers between devices  40.4 us (19%)
  local copies, waits for them, and re-layouts  12.4 us (6%)
  other arithmetic  11.2 us (5%)
    ppermute x23, waiting for transfers between devices, permute(): return lax.ppermute(x, axis, pairs)  89.2 us
    pallas_call x4, Pallas kernels, backward(): pl.pallas_call(kernel, out_shape=shapes, grid_spec=pltpu.PrefetchScalarGr...  34.2 us
    ppermute x23, starting transfers between devices, permute(): return lax.ppermute(x, axis, pairs)  32.9 us
    pallas_call x1, Pallas kernels, forward(): pl.pallas_call(forward_kernel, out_shape=(sds((SLOTS, 2, 2, TOK, TOK), BF...  12.9 us
    unnamed x63, local copies, waits for them, and re-layouts  8.14 us
    pallas_call x1, Pallas kernels, weight(): pl.pallas_call(weight_kernel, out_shape=(sds((HD, 4608), F32), sds((HD, 4...  7.65 us
    all_to_all x1, starting transfers between devices, local(): wz = lax.all_to_all(wz, 'z', 0, 0, tiled=True)  7.51 us
  transfers between devices with their start and end apart: 24, of which 12 were waited for; matrix products, arithmetic and copies ran while one was open for 6% of the time, Pallas kernels for 24%

profile of v6, /device:TPU:96, one launch (start us, length us, event | category | flops | bytes accessed | tf_op | source)
XLA Modules:
  0.0 212.1 jit_solution(11857963855649749084)
XLA Ops:
  0.7 1.7 fusion.6
  4.4 5.5 %collective-permute-start.7 = (bf16[1,2,512,128]{3,2,1,0:T(8,128)(2,1)S(1)}, bf16[1,2,512,128]{3,2,1,0:T(8,128)(2,1)S(1)}, u32[]{:S(2)}, u32[]{:S(2)}) collective-permute-start(bf16[1,2,512,128]{3,2,1,0:T(8,128)(2,1)S(1)} %turn.1), channel_id=1, source_target_pairs={{0,64},{32,96},{64,128},{96,160},{128,192},{160,224},{1,65},{33,97... | collective-permute-start | bytes 786440 | tf_op jit(solution)/shard_map/ppermute | solution.py:28
  9.9 2.9 %collective-permute-start.8 = (bf16[1,2,512,128]{3,2,1,0:T(8,128)(2,1)S(1)}, bf16[1,2,512,128]{3,2,1,0:T(8,128)(2,1)S(1)}, u32[]{:S(2)}, u32[]{:S(2)}) collective-permute-start(bf16[1,2,512,128]{3,2,1,0:T(8,128)(2,1)S(1)} %turn.1), channel_id=1, source_target_pairs={{0,32},{32,64},{64,96},{96,128},{128,160},{160,192},{192,224},{1,3... | collective-permute-start | bytes 786440 | tf_op jit(solution)/shard_map/ppermute | solution.py:28
  12.9 7.7 %collective-permute-done.7 = bf16[1,2,512,128]{3,2,1,0:T(8,128)(2,1)S(1)} collective-permute-done((bf16[1,2,512,128]{3,2,1,0:T(8,128)(2,1)S(1)}, bf16[1,2,512,128]{3,2,1,0:T(8,128)(2,1)S(1)}, u32[]{:S(2)}, u32[]{:S(2)}) %collective-permute-start.7) | collective-permute-done | bytes 262176 | tf_op jit(solution)/shard_map/ppermute | solution.py:28
  20.6 7.5 %collective-permute-done.8 = bf16[1,2,512,128]{3,2,1,0:T(8,128)(2,1)S(1)} collective-permute-done((bf16[1,2,512,128]{3,2,1,0:T(8,128)(2,1)S(1)}, bf16[1,2,512,128]{3,2,1,0:T(8,128)(2,1)S(1)}, u32[]{:S(2)}, u32[]{:S(2)}) %collective-permute-start.8) | collective-permute-done | bytes 262176 | tf_op jit(solution)/shard_map/ppermute | solution.py:28
  30.5 12.5 %collective-permute-done.9 = bf16[2,2,512,128]{3,2,1,0:T(8,128)(2,1)S(1)} collective-permute-done((bf16[2,2,512,128]{3,2,1,0:T(8,128)(2,1)S(1)}, bf16[2,2,512,128]{3,2,1,0:T(8,128)(2,1)S(1)}, u32[]{:S(2)}, u32[]{:S(2)}) %collective-permute-start.9) | collective-permute-done | bytes 524320 | tf_op jit(solution)/shard_map/ppermute | solution.py:28
  43.1 3.6 %collective-permute-done.10 = bf16[1,2,512,128]{3,2,1,0:T(8,128)(2,1)S(1)} collective-permute-done((bf16[1,2,512,128]{3,2,1,0:T(8,128)(2,1)S(1)}, bf16[1,2,512,128]{3,2,1,0:T(8,128)(2,1)S(1)}, u32[]{:S(2)}, u32[]{:S(2)}) %collective-permute-start.10) | collective-permute-done | bytes 262176 | tf_op jit(solution)/shard_map/ppermute | solution.py:28
  46.9 3.1 %collective-permute-start.3 = (bf16[64,4608]{1,0:T(8,128)(2,1)}, bf16[64,4608]{1,0:T(8,128)(2,1)}, u32[]{:S(2)}, u32[]{:S(2)}) collective-permute-start(bf16[64,4608]{1,0:T(8,128)(2,1)} %refs_1_.1), channel_id=1, source_target_pairs={{0,4},{4,0},{1,5},{5,1},{2,6},{6,2},{3,7},{7,3},{8,12},{12,8},{9,1... | collective-permute-start | bytes 1769480 | tf_op jit(solution)/shard_map/ppermute | solution.py:28
  50.0 3.0 %collective-permute-start = (bf16[64,4608]{1,0:T(8,128)(2,1)}, bf16[64,4608]{1,0:T(8,128)(2,1)}, u32[]{:S(2)}, u32[]{:S(2)}) collective-permute-start(bf16[64,4608]{1,0:T(8,128)(2,1)} %refs_1_.1), channel_id=1, source_target_pairs={{1,0},{2,1},{3,2},{0,3},{5,4},{6,5},{7,6},{4,7},{9,8},{10,9},{11,1... | collective-permute-start | bytes 1769480 | tf_op jit(solution)/shard_map/ppermute | solution.py:28
  53.6 2.0 spin.1.qr_ref.refs_10_.refs_6_
  55.6 3.4 %copy.12 = bf16[2,128,4608]{2,1,0:T(8,128)(2,1)} copy(bf16[2,128,4608]{2,0,1:T(2,128)(2,1)} %bitcast.39) | data formatting | bytes 4718592 | tf_op jit(solution)/shard_map/transpose | solution.py:507
  59.1 5.4 %collective-permute-done.3.refs_4_ = bf16[64,4608]{1,0:T(8,128)(2,1)} collective-permute-done((bf16[64,4608]{1,0:T(8,128)(2,1)}, bf16[64,4608]{1,0:T(8,128)(2,1)}, u32[]{:S(2)}, u32[]{:S(2)}) %collective-permute-start.3) | collective-permute-done | bytes 589856 | tf_op jit(solution)/shard_map/ppermute | solution.py:28
  66.0 12.8 %collective-permute-done.refs_1_.refs_2_ = bf16[64,4608]{1,0:T(8,128)(2,1)} collective-permute-done((bf16[64,4608]{1,0:T(8,128)(2,1)}, bf16[64,4608]{1,0:T(8,128)(2,1)}, u32[]{:S(2)}, u32[]{:S(2)}) %collective-permute-start) | collective-permute-done | bytes 589856 | tf_op jit(solution)/shard_map/ppermute | solution.py:28
  78.8 3.7 %collective-permute-start.4 = (bf16[64,4608]{1,0:T(8,128)(2,1)}, bf16[64,4608]{1,0:T(8,128)(2,1)S(1)}, u32[]{:S(2)}, u32[]{:S(2)}) collective-permute-start(bf16[64,4608]{1,0:T(8,128)(2,1)} %collective-permute-done.3.refs_4_), channel_id=1, source_target_pairs={{1,0},{2,1},{3,2},{0,3},{5,4},{6,5},{7,6},{4,7},{9,8},{10,9},{11,1... | collective-permute-start | bytes 1769480 | tf_op jit(solution)/shard_map/ppermute | solution.py:28
  83.5 12.9 %attend.1 = (bf16[12,2,2,512,512]{4,3,2,1,0:T(8,128)(2,1)}, bf16[512,256]{1,0:T(8,128)(2,1)S(1)}, f32[512,256]{1,0:T(8,128)S(1)}, bf16[256,512]{1,0:T(8,128)(2,1)S(1)}) custom-call(s32[5]{0:T(128)S(1)} %stack.23.info.refs_0_, bf16[512,256]{1,0:T(8,128)(2,1)S(1)} %copy-done.12, ...), custom_call_target="tpu_custom_call" | custom-call | flops 10000000000 | bytes 24000000 | tf_op jit(solution)/shard_map/attend/pallas_call | solution.py:189
  98.6 8.9 %collective-permute-done.4.refs_5_ = bf16[64,4608]{1,0:T(8,128)(2,1)S(1)} collective-permute-done((bf16[64,4608]{1,0:T(8,128)(2,1)}, bf16[64,4608]{1,0:T(8,128)(2,1)S(1)}, u32[]{:S(2)}, u32[]{:S(2)}) %collective-permute-start.4) | collective-permute-done | bytes 589856 | tf_op jit(solution)/shard_map/ppermute | solution.py:28
  107.5 3.6 %collective-permute-done.6.refs_7_ = bf16[64,4608]{1,0:T(8,128)(2,1)S(1)} collective-permute-done((bf16[64,4608]{1,0:T(8,128)(2,1)}, bf16[64,4608]{1,0:T(8,128)(2,1)S(1)}, u32[]{:S(2)}, u32[]{:S(2)}) %collective-permute-start.6) | collective-permute-done | bytes 589856 | tf_op jit(solution)/shard_map/ppermute | solution.py:28
  112.0 7.6 %weigh.1 = (f32[128,4608]{1,0:T(8,128)}, bf16[128,4608]{1,0:T(8,128)(2,1)}, bf16[256,256]{1,0:T(8,128)(2,1)}, f32[2,256,128]{2,1,0:T(8,128)}, bf16[2,128,256]{2,...) custom-call(s32[5]{0:T(128)} %copy-done.22, bf16[64,4608]{1,0:T(8,128)(2,1)} %refs_1_.1, ...), custom_call_target="tpu_custom_call" | custom-call | flops 1900000000 | bytes 11000000 | tf_op jit(solution)/shard_map/weigh/pallas_call | solution.py:440
  122.8 13.9 %shard_map.102 = (bf16[12,2,128,512]{3,2,1,0:T(8,128)(2,1)}, f32[512,256]{1,0:T(8,128)}) custom-call(s32[5]{0:T(128)S(1)} %copy-done.23, bf16[64,4608]{1,0:T(8,128)(2,1)} %refs_1_.1, bf16[64,4608]{1,0:T(8,128)(2,1)} %collective-permute-done.refs_1_.refs_2_, bf16[64,4608]{1,0:T(8,128)(2,1)} %collective-permute-done.1.refs_2_.refs_3_, ...), custom_call_target="tpu_custom_call" | custom-call | flops 8400000000 | bytes 24000000 | tf_op jit(solution)/shard_map/pallas_call | solution.py:385
  136.8 7.3 %shard_map.103 = (bf16[2,2,128,512]{3,2,1,0:T(8,128)(2,1)}, bf16[2,2,128,512]{3,2,1,0:T(8,128)(2,1)}, f32[2,256,128]{2,1,0:T(8,128)}) custom-call(s32[5]{0:T(128)} %copy-done.22, bf16[256,256]{1,0:T(8,128)(2,1)} %get-tuple-element.30.refs_1_, f32[2,256,128]{2,1,0:T(8,128)} %get-tuple-element.31.refs_2_, bf16[2,128,256]{2,1,0:T(8,128)(2,1)} %get-tuple-element.32.refs_3_, ...), custom_call_target="tpu_custom_call" | custom-call | flops 2800000000 | bytes 8000000 | tf_op jit(solution)/shard_map/pallas_call | solution.py:385
  144.1 7.5 %shard_map.104 = (bf16[2,2,128,512]{3,2,1,0:T(8,128)(2,1)}, bf16[2,2,128,512]{3,2,1,0:T(8,128)(2,1)}, f32[2,256,128]{2,1,0:T(8,128)}) custom-call(s32[5]{0:T(128)} %copy-done.22, bf16[256,256]{1,0:T(8,128)(2,1)} %get-tuple-element.30.refs_1_, f32[2,256,128]{2,1,0:T(8,128)} %get-tuple-element.31.refs_2_, bf16[2,128,256]{2,1,0:T(8,128)(2,1)} %get-tuple-element.32.refs_3_, ...), custom_call_target="tpu_custom_call" | custom-call | flops 2800000000 | bytes 8000000 | tf_op jit(solution)/shard_map/pallas_call | solution.py:385
  153.4 5.5 %shard_map.105 = (bf16[2,2,128,512]{3,2,1,0:T(8,128)(2,1)}, bf16[2,2,128,512]{3,2,1,0:T(8,128)(2,1)}, f32[512,256]{1,0:T(8,128)}) custom-call(s32[5]{0:T(128)} %copy-done.22, bf16[256,256]{1,0:T(8,128)(2,1)} %get-tuple-element.30.refs_1_, f32[2,256,128]{2,1,0:T(8,128)} %get-tuple-element.31.refs_2_, ...), custom_call_target="tpu_custom_call", output_to_operand_aliasing={{2}: (15, {})} | custom-call | flops 2800000000 | bytes 8000000 | tf_op jit(solution)/shard_map/pallas_call | solution.py:385
  159.8 1.7 fusion.8
  161.5 3.2 %collective-permute-start.16 = (bf16[2,128,512]{2,1,0:T(8,128)(2,1)}, bf16[2,128,512]{2,1,0:T(8,128)(2,1)}, u32[]{:S(2)}, u32[]{:S(2)}) collective-permute-start(bf16[2,128,512]{2,1,0:T(8,128)(2,1)} %fusion.8), channel_id=1, source_target_pairs={{0,16},{16,0},{1,17},{17,1},{2,18},{18,2},{3,19},{19,3},{4,20},{20... | collective-permute-start | bytes 786440 | tf_op jit(solution)/shard_map/ppermute | solution.py:28
  164.8 1.8 fusion.9
  166.5 3.1 %collective-permute-done.22 = bf16[64,4608]{1,0:T(8,128)(2,1)} collective-permute-done((bf16[64,4608]{1,0:T(8,128)(2,1)S(1)}, bf16[64,4608]{1,0:T(8,128)(2,1)}, u32[]{:S(2)}, u32[]{:S(2)}) %collective-permute-start.22) | collective-permute-done | bytes 589856 | tf_op jit(solution)/shard_map/ppermute | solution.py:28
  169.6 2.2 %fusion.2 = bf16[8,8,4608]{2,1,0:T(8,128)(2,1)} fusion(bf16[64,4608]{1,0:T(8,128)(2,1)} %collective-permute-done.22, f32[2,64,4608]{2,1,0:T(8,128)S(1)} %bitcast.38, s32[]{:T(128)S(6)} %select_n.10, bf16[2,64,4608]{2,1,0:T(8,128)(2,1)} %bitcast.13), kind=kLoop, calls=%fused_computation.6 | loop fusion | flops 1474560 | bytes 2949124 | tf_op jit(solution)/shard_map/reshape | solution.py:520
  171.9 7.5 %all-to-all-start = ((bf16[8,8,4608]{2,1,0:T(8,128)(2,1)}), bf16[8,8,4608]{2,1,0:T(8,128)(2,1)S(1)}, u32[]{:S(2)}, u32[]{:S(2)}) async-start(bf16[8,8,4608]{2,1,0:T(8,128)(2,1)} %fusion.2), calls=%async_computation | async-start | bytes 1179648 | tf_op jit(solution)/shard_map/all_to_all | solution.py:521
  181.2 2.1 collective-permute-start.19
  183.7 15.5 %collective-permute-done.19 = bf16[2,128,512]{2,1,0:T(8,128)(2,1)S(1)} collective-permute-done((bf16[2,128,512]{2,1,0:T(8,128)(2,1)S(1)}, bf16[2,128,512]{2,1,0:T(8,128)(2,1)S(1)}, u32[]{:S(2)}, u32[]{:S(2)}) %collective-permute-start.19) | collective-permute-done | bytes 262176 | tf_op jit(solution)/shard_map/ppermute | solution.py:28
  200.4 1.9 collective-permute-start.20
  202.3 7.9 %collective-permute-done.20.down_ref = bf16[2,128,512]{2,1,0:T(8,128)(2,1)S(1)} collective-permute-done((bf16[2,128,512]{2,1,0:T(8,128)(2,1)S(1)}, bf16[2,128,512]{2,1,0:T(8,128)(2,1)S(1)}, u32[]{:S(2)}, u32[]{:S(2)}) %collective-permute-start.20) | collective-permute-done | bytes 262176 | tf_op jit(solution)/shard_map/ppermute | solution.py:28
  (104 shorter events, 22.0 us)
Async XLA Ops:
  2.3 28.1 %copy-start.4 = (f32[512,128]{1,0:T(8,128)}, f32[512,128]{1,0:T(8,128)S(1)}, u32[]{:S(2)}) copy-start(f32[512,128]{1,0:T(8,128)S(1)} %get-tuple-element.50.sin_ref.refs_10_.refs_8_) | copy-start | bytes 786436
  4.4 16.1 %collective-permute-start.7 = (bf16[1,2,512,128]{3,2,1,0:T(8,128)(2,1)S(1)}, bf16[1,2,512,128]{3,2,1,0:T(8,128)(2,1)S(1)}, u32[]{:S(2)}, u32[]{:S(2)}) collective-permute-start(bf16[1,2,512,128]{3,2,1,0:T(8,128)(2,1)S(1)} %turn.1), channel_id=1, source_target_pairs={{0,64},{32,96},{64,128},{96,160},{128,192},{160,224},{1,65},{33,97... | collective-permute-start | bytes 786440 | tf_op jit(solution)/shard_map/ppermute | solution.py:28
  9.9 18.2 %collective-permute-start.8 = (bf16[1,2,512,128]{3,2,1,0:T(8,128)(2,1)S(1)}, bf16[1,2,512,128]{3,2,1,0:T(8,128)(2,1)S(1)}, u32[]{:S(2)}, u32[]{:S(2)}) collective-permute-start(bf16[1,2,512,128]{3,2,1,0:T(8,128)(2,1)S(1)} %turn.1), channel_id=1, source_target_pairs={{0,32},{32,64},{64,96},{96,128},{128,160},{160,192},{192,224},{1,3... | collective-permute-start | bytes 786440 | tf_op jit(solution)/shard_map/ppermute | solution.py:28
  28.2 14.9 %collective-permute-start.9 = (bf16[2,2,512,128]{3,2,1,0:T(8,128)(2,1)S(1)}, bf16[2,2,512,128]{3,2,1,0:T(8,128)(2,1)S(1)}, u32[]{:S(2)}, u32[]{:S(2)}) collective-permute-start(bf16[2,2,512,128]{3,2,1,0:T(8,128)(2,1)S(1)} %pad_maximum_fusion.1), channel_id=1, source_target_pairs={{0,16},{16,0},{1,17},{17,1},{2,18},{18,2},{3,19},{19,3},{4,20},{20... | collective-permute-start | bytes 1572872 | tf_op jit(solution)/shard_map/ppermute | solution.py:28
  29.8 17.0 %collective-permute-start.10 = (bf16[1,2,512,128]{3,2,1,0:T(8,128)(2,1)S(1)}, bf16[1,2,512,128]{3,2,1,0:T(8,128)(2,1)S(1)}, u32[]{:S(2)}, u32[]{:S(2)}) collective-permute-start(bf16[1,2,512,128]{3,2,1,0:T(8,128)(2,1)S(1)} %turn.1), channel_id=1, source_target_pairs={{0,16},{16,0},{1,17},{17,1},{2,18},{18,2},{3,19},{19,3},{4,20},{20... | collective-permute-start | bytes 786440 | tf_op jit(solution)/shard_map/ppermute | solution.py:28
  30.4 89.3 %copy-start = (bf16[3,2,512,128]{3,2,1,0:T(8,128)(2,1)}, bf16[3,2,512,128]{3,2,1,0:T(8,128)(2,1)S(1)}, u32[]{:S(2)}) copy-start(bf16[3,2,512,128]{3,2,1,0:T(8,128)(2,1)S(1)} %pad_maximum_fusion.r0.refs_11_.refs_5_.refs_6_.refs_9_) | copy-start | bytes 2359300
  30.4 52.1 %collective-permute-start.11 = (bf16[3,2,512,128]{3,2,1,0:T(8,128)(2,1)S(1)}, bf16[3,2,512,128]{3,2,1,0:T(8,128)(2,1)S(1)}, u32[]{:S(2)}, u32[]{:S(2)}) collective-permute-start(bf16[3,2,512,128]{3,2,1,0:T(8,128)(2,1)S(1)} %pad_maximum_fusion.r0.refs_11_.refs_5_.refs_6_.refs_9_), channel_id=1, source_target_pairs={{0,8},{8,0},{1,9},{9,1},{2,10},{10,2},{3,11},{11,3},{4,12},{12,4},... | collective-permute-start | bytes 2359304 | tf_op jit(solution)/shard_map/ppermute | solution.py:28
  46.8 73.0 %copy-start.1 = (bf16[3,2,512,128]{3,2,1,0:T(8,128)(2,1)}, bf16[3,2,512,128]{3,2,1,0:T(8,128)(2,1)S(1)}, u32[]{:S(2)}) copy-start(bf16[3,2,512,128]{3,2,1,0:T(8,128)(2,1)S(1)} %constant_dynamic-update-slice_fusion.r2.refs_12_.refs_6_.refs_7_.refs_10_) | copy-start | bytes 2359300
  46.8 35.8 %collective-permute-start.12 = (bf16[3,2,512,128]{3,2,1,0:T(8,128)(2,1)S(1)}, bf16[3,2,512,128]{3,2,1,0:T(8,128)(2,1)S(1)}, u32[]{:S(2)}, u32[]{:S(2)}) collective-permute-start(bf16[3,2,512,128]{3,2,1,0:T(8,128)(2,1)S(1)} %constant_dynamic-update-slice_fusion.r2.refs_12_.refs_6_.refs_7_.refs_10_), channel_id=1, source_target_pairs={{0,8},{8,0},{1,9},{9,1},{2,10},{10,2},{3,11},{11,3},{4,12},{12,4},... | collective-permute-start | bytes 2359304 | tf_op jit(solution)/shard_map/ppermute | solution.py:28
  46.9 17.6 %collective-permute-start.3 = (bf16[64,4608]{1,0:T(8,128)(2,1)}, bf16[64,4608]{1,0:T(8,128)(2,1)}, u32[]{:S(2)}, u32[]{:S(2)}) collective-permute-start(bf16[64,4608]{1,0:T(8,128)(2,1)} %refs_1_.1), channel_id=1, source_target_pairs={{0,4},{4,0},{1,5},{5,1},{2,6},{6,2},{3,7},{7,3},{8,12},{12,8},{9,1... | collective-permute-start | bytes 1769480 | tf_op jit(solution)/shard_map/ppermute | solution.py:28
  50.0 28.9 %collective-permute-start = (bf16[64,4608]{1,0:T(8,128)(2,1)}, bf16[64,4608]{1,0:T(8,128)(2,1)}, u32[]{:S(2)}, u32[]{:S(2)}) collective-permute-start(bf16[64,4608]{1,0:T(8,128)(2,1)} %refs_1_.1), channel_id=1, source_target_pairs={{1,0},{2,1},{3,2},{0,3},{5,4},{6,5},{7,6},{4,7},{9,8},{10,9},{11,1... | collective-permute-start | bytes 1769480 | tf_op jit(solution)/shard_map/ppermute | solution.py:28
  53.0 45.6 %collective-permute-start.1 = (bf16[64,4608]{1,0:T(8,128)(2,1)}, bf16[64,4608]{1,0:T(8,128)(2,1)}, u32[]{:S(2)}, u32[]{:S(2)}) collective-permute-start(bf16[64,4608]{1,0:T(8,128)(2,1)} %refs_1_.1), channel_id=1, source_target_pairs={{2,0},{3,1},{0,2},{1,3},{6,4},{7,5},{4,6},{5,7},{10,8},{11,9},{8,1... | collective-permute-start | bytes 1769480 | tf_op jit(solution)/shard_map/ppermute | solution.py:28
  59.1 37.4 %copy-start.22 = (s32[5]{0:T(128)}, s32[5]{0:T(128)S(1)}, u32[]{:S(2)}) copy-start(s32[5]{0:T(128)S(1)} %stack.23.info.refs_0_) | copy-start | bytes 64
  64.4 34.2 %collective-permute-start.2 = (bf16[64,4608]{1,0:T(8,128)(2,1)}, bf16[64,4608]{1,0:T(8,128)(2,1)S(1)}, u32[]{:S(2)}, u32[]{:S(2)}) collective-permute-start(bf16[64,4608]{1,0:T(8,128)(2,1)} %refs_1_.1), channel_id=1, source_target_pairs={{3,0},{0,1},{1,2},{2,3},{7,4},{4,5},{5,6},{6,7},{11,8},{8,9},{9,10... | collective-permute-start | bytes 1769480 | tf_op jit(solution)/shard_map/ppermute | solution.py:28
  78.8 28.7 %collective-permute-start.4 = (bf16[64,4608]{1,0:T(8,128)(2,1)}, bf16[64,4608]{1,0:T(8,128)(2,1)S(1)}, u32[]{:S(2)}, u32[]{:S(2)}) collective-permute-start(bf16[64,4608]{1,0:T(8,128)(2,1)} %collective-permute-done.3.refs_4_), channel_id=1, source_target_pairs={{1,0},{2,1},{3,2},{0,3},{5,4},{6,5},{7,6},{4,7},{9,8},{10,9},{11,1... | collective-permute-start | bytes 1769480 | tf_op jit(solution)/shard_map/ppermute | solution.py:28
  82.5 37.2 %copy-start.2 = (bf16[3,2,512,128]{3,2,1,0:T(8,128)(2,1)}, bf16[3,2,512,128]{3,2,1,0:T(8,128)(2,1)S(1)}, u32[]{:S(2)}) copy-start(bf16[3,2,512,128]{3,2,1,0:T(8,128)(2,1)S(1)} %collective-permute-done.11.r1.refs_13_.refs_7_.refs_8_.refs_11_) | copy-start | bytes 2359300
  82.5 25.0 %collective-permute-start.5 = (bf16[64,4608]{1,0:T(8,128)(2,1)}, bf16[64,4608]{1,0:T(8,128)(2,1)S(1)}, u32[]{:S(2)}, u32[]{:S(2)}) collective-permute-start(bf16[64,4608]{1,0:T(8,128)(2,1)} %collective-permute-done.3.refs_4_), channel_id=1, source_target_pairs={{2,0},{3,1},{0,2},{1,3},{6,4},{7,5},{4,6},{5,7},{10,8},{11,9},{8,1... | collective-permute-start | bytes 1769480 | tf_op jit(solution)/shard_map/ppermute | solution.py:28
  82.6 37.2 %copy-start.3 = (bf16[3,2,512,128]{3,2,1,0:T(8,128)(2,1)}, bf16[3,2,512,128]{3,2,1,0:T(8,128)(2,1)S(1)}, u32[]{:S(2)}) copy-start(bf16[3,2,512,128]{3,2,1,0:T(8,128)(2,1)S(1)} %collective-permute-done.12.r3.refs_14_.refs_8_.refs_9_.refs_12_) | copy-start | bytes 2359300
  82.6 28.5 %collective-permute-start.6 = (bf16[64,4608]{1,0:T(8,128)(2,1)}, bf16[64,4608]{1,0:T(8,128)(2,1)S(1)}, u32[]{:S(2)}, u32[]{:S(2)}) collective-permute-start(bf16[64,4608]{1,0:T(8,128)(2,1)} %collective-permute-done.3.refs_4_), channel_id=1, source_target_pairs={{3,0},{0,1},{1,2},{2,3},{7,4},{4,5},{5,6},{6,7},{11,8},{8,9},{9,10... | collective-permute-start | bytes 1769480 | tf_op jit(solution)/shard_map/ppermute | solution.py:28
  119.6 32.5 %collective-permute-start.21 = (bf16[128,4608]{1,0:T(8,128)(2,1)}, bf16[128,4608]{1,0:T(8,128)(2,1)}, u32[]{:S(2)}, u32[]{:S(2)}) collective-permute-start(bf16[128,4608]{1,0:T(8,128)(2,1)} %get-tuple-element.49), channel_id=1, source_target_pairs={{0,8},{8,0},{1,9},{9,1},{2,10},{10,2},{3,11},{11,3},{4,12},{12,4},... | collective-permute-start | bytes 3538952 | tf_op jit(solution)/shard_map/ppermute | solution.py:28
  151.5 8.3 %collective-permute-start.15 = (bf16[2,2,128,512]{3,2,1,0:T(8,128)(2,1)}, bf16[2,2,128,512]{3,2,1,0:T(8,128)(2,1)}, u32[]{:S(2)}, u32[]{:S(2)}) collective-permute-start(bf16[2,2,128,512]{3,2,1,0:T(8,128)(2,1)} %get-tuple-element.43), channel_id=1, source_target_pairs={{0,8},{8,0},{1,9},{9,1},{2,10},{10,2},{3,11},{11,3},{4,12},{12,4},... | collective-permute-start | bytes 1572872 | tf_op jit(solution)/shard_map/ppermute | solution.py:28
  151.6 13.2 %collective-permute-start.17 = (bf16[2,2,128,512]{3,2,1,0:T(8,128)(2,1)}, bf16[2,2,128,512]{3,2,1,0:T(8,128)(2,1)}, u32[]{:S(2)}, u32[]{:S(2)}) collective-permute-start(bf16[2,2,128,512]{3,2,1,0:T(8,128)(2,1)} %get-tuple-element.45), channel_id=1, source_target_pairs={{0,8},{8,0},{1,9},{9,1},{2,10},{10,2},{3,11},{11,3},{4,12},{12,4},... | collective-permute-start | bytes 1572872 | tf_op jit(solution)/shard_map/ppermute | solution.py:28
  153.2 16.4 %collective-permute-start.22 = (bf16[64,4608]{1,0:T(8,128)(2,1)S(1)}, bf16[64,4608]{1,0:T(8,128)(2,1)}, u32[]{:S(2)}, u32[]{:S(2)}) collective-permute-start(bf16[64,4608]{1,0:T(8,128)(2,1)S(1)} %fusion.1), channel_id=1, source_target_pairs={{0,16},{16,0},{1,17},{17,1},{2,18},{18,2},{3,19},{19,3},{4,20},{20... | collective-permute-start | bytes 1769480 | tf_op jit(solution)/shard_map/ppermute | solution.py:28
  158.9 24.3 %collective-permute-start.13 = (bf16[2,2,128,512]{3,2,1,0:T(8,128)(2,1)}, bf16[2,2,128,512]{3,2,1,0:T(8,128)(2,1)S(1)}, u32[]{:S(2)}, u32[]{:S(2)}) collective-permute-start(bf16[2,2,128,512]{3,2,1,0:T(8,128)(2,1)} %get-tuple-element.41), channel_id=1, source_target_pairs={{0,8},{8,0},{1,9},{9,1},{2,10},{10,2},{3,11},{11,3},{4,12},{12,4},... | collective-permute-start | bytes 1572872 | tf_op jit(solution)/shard_map/ppermute | solution.py:28
  161.5 22.2 %collective-permute-start.16 = (bf16[2,128,512]{2,1,0:T(8,128)(2,1)}, bf16[2,128,512]{2,1,0:T(8,128)(2,1)}, u32[]{:S(2)}, u32[]{:S(2)}) collective-permute-start(bf16[2,128,512]{2,1,0:T(8,128)(2,1)} %fusion.8), channel_id=1, source_target_pairs={{0,16},{16,0},{1,17},{17,1},{2,18},{18,2},{3,19},{19,3},{4,20},{20... | collective-permute-start | bytes 786440 | tf_op jit(solution)/shard_map/ppermute | solution.py:28
  166.5 13.5 %collective-permute-start.18 = (bf16[2,128,512]{2,1,0:T(8,128)(2,1)}, bf16[2,128,512]{2,1,0:T(8,128)(2,1)}, u32[]{:S(2)}, u32[]{:S(2)}) collective-permute-start(bf16[2,128,512]{2,1,0:T(8,128)(2,1)} %fusion.9), channel_id=1, source_target_pairs={{0,16},{16,0},{1,17},{17,1},{2,18},{18,2},{3,19},{19,3},{4,20},{20... | collective-permute-start | bytes 786440 | tf_op jit(solution)/shard_map/ppermute | solution.py:28
  171.9 39.3 %all-to-all-start = ((bf16[8,8,4608]{2,1,0:T(8,128)(2,1)}), bf16[8,8,4608]{2,1,0:T(8,128)(2,1)S(1)}, u32[]{:S(2)}, u32[]{:S(2)}) async-start(bf16[8,8,4608]{2,1,0:T(8,128)(2,1)} %fusion.2), calls=%async_computation | async-start | bytes 1179648 | tf_op jit(solution)/shard_map/all_to_all | solution.py:521
  181.1 29.1 %copy-start.6 = (f32[512,128]{1,0:T(8,128)S(1)}, f32[512,128]{1,0:T(8,128)}, u32[]{:S(2)}) copy-start(f32[512,128]{1,0:T(8,128)} %copy-done.4) | copy-start | bytes 786436
  181.2 29.1 %copy-start.9 = (f32[512,128]{1,0:T(8,128)S(1)}, f32[512,128]{1,0:T(8,128)}, u32[]{:S(2)}) copy-start(f32[512,128]{1,0:T(8,128)} %copy-done.7) | copy-start | bytes 786436
  181.2 18.0 %collective-permute-start.19 = (bf16[2,128,512]{2,1,0:T(8,128)(2,1)S(1)}, bf16[2,128,512]{2,1,0:T(8,128)(2,1)S(1)}, u32[]{:S(2)}, u32[]{:S(2)}) collective-permute-start(bf16[2,128,512]{2,1,0:T(8,128)(2,1)S(1)} %fusion.3), channel_id=1, source_target_pairs={{32,0},{64,32},{96,64},{128,96},{160,128},{192,160},{224,192},{33,... | collective-permute-start | bytes 786440 | tf_op jit(solution)/shard_map/ppermute | solution.py:28
  183.3 19.0 %collective-permute-start.14 = (bf16[2,128,512]{2,1,0:T(8,128)(2,1)S(1)}, bf16[2,128,512]{2,1,0:T(8,128)(2,1)S(1)}, u32[]{:S(2)}, u32[]{:S(2)}) collective-permute-start(bf16[2,128,512]{2,1,0:T(8,128)(2,1)S(1)} %fusion.7), channel_id=1, source_target_pairs={{0,16},{16,0},{1,17},{17,1},{2,18},{18,2},{3,19},{19,3},{4,20},{20... | collective-permute-start | bytes 786440 | tf_op jit(solution)/shard_map/ppermute | solution.py:28
  200.4 9.8 %collective-permute-start.20 = (bf16[2,128,512]{2,1,0:T(8,128)(2,1)S(1)}, bf16[2,128,512]{2,1,0:T(8,128)(2,1)S(1)}, u32[]{:S(2)}, u32[]{:S(2)}) collective-permute-start(bf16[2,128,512]{2,1,0:T(8,128)(2,1)S(1)} %fusion.5), channel_id=1, source_target_pairs={{32,0},{64,32},{96,64},{128,96},{160,128},{192,160},{224,192},{33,... | collective-permute-start | bytes 786440 | tf_op jit(solution)/shard_map/ppermute | solution.py:28
  (23 other events, 168.7 us)
